TPU v7x, 32 devices: a whole 2x2x4 slice. The times are simulated.
32 devices in a mesh: enc: 4 (over x, core), row: 4 (over z), col: 2 (over y).
Axes of the slice: x: 2, y: 2, z: 4, core: 2. Of those that a mesh axis runs over, the one named last changes fastest.
Arguments:
- out_grad: bfloat16 [48, 8192], P(None, ('enc', 'col')), may hold values from -6 to 6
- gate_pre: bfloat16 [48, 29568], P('enc', 'row'), may hold values from -6 to 6
- up_pre: bfloat16 [48, 29568], P('enc', 'row'), may hold values from -6 to 6
- w_gate: bfloat16 [8192, 29568], P(('enc', 'col'), 'row'), may hold values from -0.0625 to 0.0625
- w_up: bfloat16 [8192, 29568], P(('enc', 'col'), 'row'), may hold values from -0.0625 to 0.0625
- w_down: bfloat16 [29568, 8192], P('row', ('enc', 'col')), may hold values from -0.03125 to 0.03125
- w_proj: bfloat16 [12800, 8192], P(None, ('enc', 'col')), may hold values from -0.0546875 to 0.0546875
- enc_hidden: bfloat16 [192, 6400], P('row', ('enc', 'col')), may hold values from -6 to 6
- route: int32 [48], replicated, may hold values from 0 to 47, each once
- img_count: int32 [4], replicated, may hold values from 1 to 12
Outputs:
- enc_grad: bfloat16 [3200, 6400], P(None, ('enc', 'col'))
Inputs may be any that keep to these rules, and one draw needn't show every extreme that they name: route[12 * r + k] is the language row that holds slot k of row group r; every language row appears once. Slots k of row group r with k >= img_count[r] are empty.
All inputs are finite; a program needn't handle non-finite values.
Results may differ from a plain program's by a relative error of at most 0.02.
Values may be sent and summed in bfloat16 or wider, within the bound.
No kernel may reach another device: no remote copies, remote signals or barrier semaphores. Data moves between devices by JAX's collectives and lax.ppermute only.
A program may use at most 128 MiB of HBM per device.

v0:
```python
import math

import jax
import jax.numpy as jnp
from jax import lax
from jax.sharding import PartitionSpec as P

SHUF = 4
IMG = 12


def contract_last(left, right):
    return lax.dot_general(
        left, right, (((1,), (1,)), ((), ())), preferred_element_type=jnp.float32
    )


def contract_first(left, right):
    return lax.dot_general(
        left, right, (((0,), (0,)), ((), ())), preferred_element_type=jnp.float32
    )


def gate_grads(hidden_grad, gate_pre, up_pre):
    share_rows = hidden_grad.shape[0]
    offset = lax.axis_index("col") * share_rows
    gate_vals = lax.dynamic_slice_in_dim(gate_pre, offset, share_rows, 0).astype(jnp.float32)
    up_vals = lax.dynamic_slice_in_dim(up_pre, offset, share_rows, 0).astype(jnp.float32)
    squash = jax.nn.sigmoid(gate_vals)
    grad_gate = (hidden_grad * up_vals * squash * (1.0 + gate_vals * (1.0 - squash))).astype(
        jnp.bfloat16
    )
    grad_up = (hidden_grad * gate_vals * squash).astype(jnp.bfloat16)
    return (grad_gate, grad_up)


def shards(out_grad, gate_pre, up_pre, w_gate, w_up, w_down, w_proj, enc_hidden, route, img_count):
    hidden_part = contract_last(out_grad, w_down)
    enc_share = lax.psum_scatter(hidden_part, "enc", scatter_dimension=0, tiled=True)
    hidden_grad = lax.psum_scatter(enc_share, "col", scatter_dimension=0, tiled=True)
    grad_gate, grad_up = gate_grads(hidden_grad, gate_pre, up_pre)
    grad_gate, grad_up = (
        lax.all_gather(grad_gate, "col", axis=0, tiled=True),
        lax.all_gather(grad_up, "col", axis=0, tiled=True),
    )
    grad_gate, grad_up = (
        lax.all_gather(grad_gate, "enc", axis=0, tiled=True),
        lax.all_gather(grad_up, "enc", axis=0, tiled=True),
    )
    routed_gate = jnp.take(grad_gate, route, axis=0)
    routed_up = jnp.take(grad_up, route, axis=0)
    input_part = contract_last(routed_gate, w_gate) + contract_last(routed_up, w_up)
    positions = jnp.arange(route.shape[0], dtype=jnp.int32)
    alive_mask = positions % IMG < jnp.repeat(img_count, IMG)
    input_part = jnp.where(alive_mask[:, None], input_part, jnp.zeros_like(input_part))
    image_grad = lax.psum_scatter(input_part, "row", scatter_dimension=0, tiled=True).astype(
        jnp.bfloat16
    )
    shuffled_grad = lax.psum_scatter(
        contract_last(image_grad, w_proj), ("enc", "col"), scatter_dimension=1, tiled=True
    )
    feature_share = shuffled_grad.shape[1] // SHUF
    patch_grad = (
        shuffled_grad.reshape(IMG, feature_share, SHUF)
        .transpose(0, 2, 1)
        .reshape(IMG * SHUF, feature_share)
        .astype(jnp.bfloat16)
    )
    patch_total = enc_hidden.shape[0] * lax.axis_size("row")
    scale = 1.0 / math.sqrt(patch_total)
    group_term = (
        contract_first(lax.all_gather(patch_grad, ("enc", "col"), axis=1, tiled=True), enc_hidden)
        * scale
    )
    total = lax.psum(group_term.astype(jnp.bfloat16), "row")
    return total


def solution(mesh):
    placed = (
        P(None, ("enc", "col")),
        P("enc", "row"),
        P("enc", "row"),
        P(("enc", "col"), "row"),
        P(("enc", "col"), "row"),
        P("row", ("enc", "col")),
        P(None, ("enc", "col")),
        P("row", ("enc", "col")),
        P(),
        P(),
    )
    return jax.shard_map(
        shards, mesh=mesh, in_specs=placed, out_specs=P(None, ("enc", "col")), check_vma=False
    )
```

profile of v0, /device:TPU:0, one launch (start us, length us, event | category | flops | bytes accessed | tf_op | source)
XLA Modules:
  0.0 432.6 jit_solution(12022463329798389478)
XLA Ops:
  6.6 0.8 copy-done
  7.4 9.9 %fusion.25 = f32[48,7392]{1,0:T(8,128)S(1)} fusion(bf16[48,1024]{1,0:T(8,128)(2,1)S(1)} %copy-done, bf16[7392,1024]{1,0:T(8,128)(2,1)} %param.17), kind=kOutput, calls=%fused_computation.36 | convolution fusion | flops 726663168 | bytes 16656384 | tf_op jit(solution)/shard_map/dot_general | solution.py:13
  17.3 22.6 %fusion = f32[16,7392]{1,0:T(8,128)S(1)} fusion(f32[48,7392]{1,0:T(8,128)S(1)} %fusion.25), kind=kCustom, calls=%all-reduce-scatter | all-reduce-scatter fusion | flops 473089 | bytes 1892864
  40.0 1.3 collective-permute-start
  44.8 9.3 %fusion.1 = f32[8,7392]{1,0:T(8,128)S(1)} fusion(f32[12,7392]{1,0:T(8,128)S(1)} %constant_dynamic-slice_fusion), kind=kCustom, calls=%all-reduce-scatter.1 | all-reduce-scatter fusion | flops 118273 | bytes 591872
  54.1 2.4 collective-permute-start.1
  56.5 1.8 collective-permute-done.1
  58.9 6.2 %all-gather.2 = bf16[2,6,7392]{2,1,0:T(8,128)(2,1)S(1)} all-gather(bf16[1,6,7392]{2,1,0:T(8,128)(2,1)S(1)} %get-tuple-element.6), channel_id=1, replica_groups=mesh['enc'=4,'row'=4,'col'=2] {'col'}, dimensions={0}, use_global_device_ids=true | all-gather | bytes 266112 | tf_op jit(solution)/shard_map/all_gather | solution.py:44
  65.2 6.8 %all-gather = bf16[2,6,7392]{2,1,0:T(8,128)(2,1)S(1)} all-gather(bf16[1,6,7392]{2,1,0:T(8,128)(2,1)S(1)} %get-tuple-element.7), channel_id=1, replica_groups=mesh['enc'=4,'row'=4,'col'=2] {'col'}, dimensions={0}, use_global_device_ids=true | all-gather | bytes 266112 | tf_op jit(solution)/shard_map/all_gather | solution.py:43
  72.2 13.2 %all-gather.1 = bf16[4,12,7392]{2,1,0:T(8,128)(2,1)S(1)} all-gather(bf16[1,12,7392]{2,1,0:T(8,128)(2,1)S(1)} %reshape.47), channel_id=1, replica_groups=mesh['enc'=4,'row'=4,'col'=2] {'enc'}, dimensions={0}, use_global_device_ids=true | all-gather | bytes 887040 | tf_op jit(solution)/shard_map/all_gather | solution.py:47
  85.7 9.6 %all-gather.3 = bf16[4,12,7392]{2,1,0:T(8,128)(2,1)S(1)} all-gather(bf16[1,12,7392]{2,1,0:T(8,128)(2,1)S(1)} %reshape.51), channel_id=1, replica_groups=mesh['enc'=4,'row'=4,'col'=2] {'enc'}, dimensions={0}, use_global_device_ids=true | all-gather | bytes 887040 | tf_op jit(solution)/shard_map/all_gather | solution.py:48
  95.7 1.0 gather_fusion
  96.7 1.0 gather_fusion.1
  97.7 8.1 %fusion.5 = f32[48,1024]{1,0:T(8,128)S(1)} fusion(bf16[1024,7392]{0,1:T(8,128)(2,1)} %param.15, bf16[48,7392]{1,0:T(8,128)(2,1)S(1)} %gather_fusion, pred[48]{0:T(512)(128)(4,1)S(1)} %compare_and_fusion), kind=kOutput, calls=%fused_computation.7 | convolution fusion | flops 727017984 | bytes 16045104 | tf_op jit(solution)/shard_map/dot_general | solution.py:13
  105.8 8.1 %fusion.3 = f32[48,1024]{1,0:T(8,128)S(1)} fusion(f32[48,1024]{1,0:T(8,128)S(1)} %fusion.5, bf16[1024,7392]{0,1:T(8,128)(2,1)} %param.16, bf16[48,7392]{1,0:T(8,128)(2,1)S(1)} %gather_fusion.1, pred[48]{0:T(512)(128)(4,1)S(1)} %compare_and_fusion, pred[48]{0:T(512)(128)(4,1)S(1)} %fusion.22), kind=kOutput, calls=%fused_computation.5 | convolution fusion | flops 727116288 | bytes 16241760 | tf_op jit(solution)/shard_map/dot_general | solution.py:13
  114.0 15.4 %fusion.2 = f32[16,1024]{1,0:T(8,128)S(1)} fusion(f32[48,1024]{1,0:T(8,128)S(1)} %fusion.3), kind=kCustom, calls=%all-reduce-scatter.2 | all-reduce-scatter fusion | flops 65537 | bytes 262656
  129.4 2.0 collective-permute-start.2
  133.2 14.8 %convolution_bitcast_fusion = f32[12800,12]{1,0:T(8,128)} fusion(bf16[12800,1024]{1,0:T(8,128)(2,1)} %param.18, bf16[28,1024]{1,0:T(8,128)(2,1)S(1)} %concatenate.2, u32[]{:S(6)} %subtract.2), kind=kOutput, calls=%fused_computation.2 | convolution fusion | flops 314572800 | bytes 26861572
  148.1 63.4 %reduce-scatter.10.cloned.1.call-done = f32[1600,12]{1,0:T(8,128)} async-done(((f32[12800,12]{1,0:T(8,128)}), f32[1600,12]{1,0:T(8,128)}) %reduce-scatter.10.cloned.1.call-update) | async-done | bytes 76816
  211.5 1.4 copy.18
  213.5 17.1 %all-gather.4 = bf16[8,400,48]{1,2,0:T(8,128)(2,1)S(1)} all-gather(bf16[1,400,48]{1,2,0:T(8,128)(2,1)S(1)} %bitcast.33), channel_id=1, replica_groups=mesh['enc'=4,'row'=4,'col'=2] {'enc','col'}, dimensions={0}, use_global_device_ids=true | all-gather | bytes 345600 | tf_op jit(solution)/shard_map/all_gather | solution.py:72
  231.3 3.9 multiply_convert_fusion
  235.2 185.4 %all-reduce.8.cloned.1.call-done = bf16[3200,800]{0,1:T(8,128)(2,1)} async-done(((bf16[3200,800]{0,1:T(8,128)(2,1)}), bf16[3200,800]{0,1:T(8,128)(2,1)}) %all-reduce.8.cloned.1.call-update) | async-done | bytes 5120016 | tf_op jit(solution)/shard_map/psum | solution.py:75
  420.6 5.1 %copy.20 = bf16[3200,800]{0,1:T(8,128)(2,1)} copy(bf16[3200,800]{0,1:T(8,128)(2,1)} %all-reduce.8.cloned.1.call-done) | data formatting | bytes 10240000
  (51 shorter events, 6.2 us)
Async XLA Ops:
  6.5 0.9 copy-start
  6.5 34.8 %copy-start.8 = (u32[32]{0:T(128)S(1)}, u32[32]{0:T(128)}, u32[]{:S(2)}) copy-start(u32[32]{0:T(128)} %constant.41) | copy-start | bytes 388
  6.5 36.0 %copy-start.7 = (u32[32]{0:T(128)S(1)}, u32[32]{0:T(128)}, u32[]{:S(2)}) copy-start(u32[32]{0:T(128)} %constant.37) | copy-start | bytes 388
  6.5 36.6 %copy-start.9 = (s32[48]{0:T(128)S(1)}, s32[48]{0:T(128)}, u32[]{:S(2)}) copy-start(s32[48]{0:T(128)} %param.20) | copy-start | bytes 580
  6.5 36.6 %copy-start.5 = (s32[4]{0:T(128)S(1)}, s32[4]{0:T(128)}, u32[]{:S(2)}) copy-start(s32[4]{0:T(128)} %param.21) | copy-start | bytes 52
  6.5 52.1 %copy-start.4 = (bf16[12,7392]{1,0:T(8,128)(2,1)S(1)}, bf16[12,7392]{1,0:T(8,128)(2,1)}, u32[]{:S(2)}) copy-start(bf16[12,7392]{1,0:T(8,128)(2,1)} %param.14) | copy-start | bytes 532228
  6.6 52.1 %copy-start.3 = (bf16[12,7392]{1,0:T(8,128)(2,1)S(1)}, bf16[12,7392]{1,0:T(8,128)(2,1)}, u32[]{:S(2)}) copy-start(bf16[12,7392]{1,0:T(8,128)(2,1)} %param.13) | copy-start | bytes 532228
  6.6 204.9 %reduce-scatter.10.cloned.1.call-start = ((), (), s32[]{:S(2)}) async-start(), calls=%async_computation.2 | async-start | bytes 7372800
  40.0 4.0 collective-permute-start
  54.1 4.2 collective-permute-start.1
  105.8 25.7 %copy-start.6 = (u32[32]{0:T(128)S(1)}, u32[32]{0:T(128)}, u32[]{:S(2)}) copy-start(u32[32]{0:T(128)} %constant.45) | copy-start | bytes 388
  129.4 3.6 collective-permute-start.2
  133.2 98.1 %copy-start.2 = (bf16[48,800]{1,0:T(8,128)(2,1)S(1)}, bf16[48,800]{1,0:T(8,128)(2,1)}, u32[]{:S(2)}) copy-start(bf16[48,800]{1,0:T(8,128)(2,1)} %param.19) | copy-start | bytes 230404
  148.0 277.7 %copy-start.1 = (bf16[48,1024]{1,0:T(8,128)(2,1)S(1)}, bf16[48,1024]{1,0:T(8,128)(2,1)}, u32[]{:S(2)}) copy-start(bf16[48,1024]{1,0:T(8,128)(2,1)} %param.12) | copy-start | bytes 294916
  148.1 272.5 %all-reduce.8.cloned.1.call-start = ((), (), s32[]{:S(2)}) async-start(), calls=%async_computation.1 | async-start | bytes 10240000 | tf_op jit(solution)/shard_map/psum | solution.py:75
Sparse Core Ops, SparseCore 0:
  148.2 63.2 reduce-scatter.9
  235.3 185.2 all-reduce.7
where the time goes:
time: 433 us
  waiting for transfers between devices  251 us (58%)
  blocking collectives  100 us (23%)
  matrix products  44.8 us (10%)
  between operations  15.7 us (4%)
  local copies, waits for them, and re-layouts  15 us (3%)
  starting transfers between devices  5.85 us (1%)
    psum x1, waiting for transfers between devices, shards(): total = lax.psum(group_term.astype(jnp.bfloat16), 'row')  185 us
    unnamed x6, waiting for transfers between devices  65.5 us
    unnamed x3, blocking collectives  47.2 us
    dot_general x3, matrix products, contract_last(): lax.dot_general(left, right, (((1,), (1,)), ((), ())), preferred_element_...  26.1 us
    all_gather x1, blocking collectives, shards(): lax.all_gather(patch_grad, ('enc', 'col'), axis=1, tiled=True)  17.1 us
    unnamed x1, matrix products  14.8 us
    all_gather x1, blocking collectives, shards(): lax.all_gather(grad_gate, 'enc', axis=0, tiled=True)  13.2 us
    unnamed x37, local copies, waits for them, and re-layouts  11.9 us
  transfers between devices with their start and end apart: 5, of which 4 were waited for; matrix products, arithmetic and copies ran while one was open for 0% of the time, Pallas kernels for 0%

commit v1 on v0

v1 whole, which is shorter than its diff:
```python
import functools
import math

import jax
import jax.numpy as jnp
from jax import lax
from jax.experimental import pallas as pl
from jax.experimental.pallas import tpu as pltpu
from jax.sharding import PartitionSpec as P

SHUF = 4
CORES = 2
LANES = 128
AXES = ("enc", "row", "col")
BF = jnp.bfloat16
F32 = jnp.float32


def cdiv(a, b):
    return -(-a // b)


def dot_nt(left, right):
    return lax.dot_general(left, right, (((1,), (1,)), ((), ())), preferred_element_type=F32)


def dot_nn(left, right):
    return lax.dot_general(left, right, (((1,), (0,)), ((), ())), preferred_element_type=F32)


def dot_tn(left, right):
    return lax.dot_general(left, right, (((0,), (0,)), ((), ())), preferred_element_type=F32)


class Grid:
    def __init__(self):
        self.enc, self.rows, self.cols = (lax.axis_size(a) for a in AXES)
        self.xs = self.enc // CORES
        self.chips = self.xs * self.cols
        enc = lax.axis_index("enc")
        self.core = enc % CORES
        self.x = enc // CORES
        self.y = lax.axis_index("col")
        self.z = lax.axis_index("row")
        self.shifts = [(dx, dy) for dx in range(self.xs) for dy in range(self.cols)]

    def send(self, value, dx=0, dy=0, core=0, row=None):
        pairs = []
        for e in range(self.enc):
            for r in range(self.rows):
                for c in range(self.cols):
                    x, k = divmod(e, CORES)
                    target = (((x + dx) % self.xs) * CORES + (k ^ core), r if row is None else row(r), (c + dy) % self.cols)
                    flat = [(a * self.rows + b) * self.cols + d for a, b, d in ((e, r, c), target)]
                    pairs.append(tuple(flat))
        return lax.ppermute(value, AXES, pairs)

    def swap(self, value):
        return self.send(value, core=1)


def shuffle_matmul(image_grad, w_proj, first, steps):
    slots, width = image_grad.shape
    half = slots // CORES
    block = SHUF * LANES
    last = cdiv(w_proj.shape[0], block) - 1

    def kernel(first_ref, grad_ref, w_ref, out_ref, order):
        @pl.when(pl.program_id(0) == 0)
        def _():
            source = lax.broadcasted_iota(jnp.int32, (block, block), 0)
            target = lax.broadcasted_iota(jnp.int32, (block, block), 1)
            order[...] = jnp.where(source == SHUF * (target % LANES) + target // LANES, 1.0, 0.0).astype(BF)

        part = dot_nt(grad_ref[...], w_ref[...]).astype(BF)
        part = dot_nn(part, order[...]).astype(BF)
        for core in range(CORES):
            for q in range(SHUF):
                out_ref[core, q] = part[core * half : (core + 1) * half, q * LANES : (q + 1) * LANES]

    return pl.pallas_call(
        kernel,
        out_shape=jax.ShapeDtypeStruct((CORES, SHUF, half, steps * LANES), BF),
        grid_spec=pltpu.PrefetchScalarGridSpec(
            num_scalar_prefetch=1,
            grid=(steps,),
            in_specs=[
                pl.BlockSpec((slots, width), lambda i, first: (0, 0)),
                pl.BlockSpec((block, width), lambda i, first: (jnp.minimum(first[0] + i, last), 0)),
            ],
            out_specs=pl.BlockSpec((CORES, SHUF, half, LANES), lambda i, first: (0, 0, 0, i)),
            scratch_shapes=[pltpu.VMEM((block, block), BF)],
        ),
        cost_estimate=pl.CostEstimate(
            flops=2 * slots * width * block * steps, bytes_accessed=2 * width * block * steps, transcendentals=0
        ),
        name="shuffle_matmul",
    )(first, image_grad, w_proj)


def weight_grad(patches, hidden, where, features, scale):
    count, patch, block = patches.shape
    units = hidden.shape[1]

    def kernel(where_ref, patch_ref, hidden_ref, out_ref):
        out_ref[...] = (dot_tn(hidden_ref[...], patch_ref[0]) * scale).astype(BF)

    return pl.pallas_call(
        kernel,
        out_shape=jax.ShapeDtypeStruct((units, features), BF),
        grid_spec=pltpu.PrefetchScalarGridSpec(
            num_scalar_prefetch=1,
            grid=(count,),
            in_specs=[
                pl.BlockSpec((1, patch, block), lambda i, where: (i, 0, 0)),
                pl.BlockSpec((patch, units), lambda i, where: (0, 0)),
            ],
            out_specs=pl.BlockSpec((units, block), lambda i, where: (0, where[i])),
        ),
        cost_estimate=pl.CostEstimate(
            flops=2 * count * patch * block * units, bytes_accessed=2 * units * features, transcendentals=0
        ),
        name="weight_grad",
    )(where, patches, hidden)


def gather_rows(g, value):
    stack = value[None]
    if g.rows & (g.rows - 1):
        return lax.all_gather(value, "row", axis=0, tiled=False)
    for mask in row_masks(g):
        stack = jnp.concatenate([stack, g.send(stack, row=lambda r: r ^ mask)])
    return stack


def row_masks(g):
    return [2 ** (s + 1) - 1 for s in range(g.rows.bit_length() - 1)]


def row_order(g):
    if g.rows & (g.rows - 1):
        return jnp.arange(g.rows, dtype=jnp.int32)
    order = [0]
    for mask in row_masks(g):
        order = order + [o ^ mask for o in order]
    return jnp.array(order, jnp.int32) ^ g.z


def sum_rows(g, value):
    if g.rows & (g.rows - 1):
        return lax.psum(value.astype(F32), "row").astype(BF)
    for mask in row_masks(g):
        value = (value.astype(F32) + g.send(value, row=lambda r: r ^ mask).astype(F32)).astype(BF)
    return value


def shards(out_grad, gate_pre, up_pre, w_gate, w_up, w_down, w_proj, enc_hidden, route, img_count):
    g = Grid()
    slots = route.shape[0]
    own = gate_pre.shape[0]
    half = slots // CORES
    units = w_down.shape[0]
    share = cdiv(cdiv(units, g.cols), LANES) * LANES
    padded = share * g.cols

    hidden = dot_nt(out_grad, w_down)
    hidden = jnp.pad(hidden, ((0, 0), (0, padded - units)))
    hidden = hidden.reshape(g.xs, CORES, own, g.cols, share).transpose(3, 1, 0, 2, 4)

    def core_part(a, core):
        return lax.dynamic_index_in_dim(a, core, 1, keepdims=False)

    other = g.swap(core_part(hidden.astype(BF), 1 - g.core))
    mine = core_part(hidden, g.core) + other.astype(F32)
    def for_chip(a, dx, dy):
        a = lax.dynamic_index_in_dim(a, (g.y + dy) % g.cols, 0, keepdims=False)
        return lax.dynamic_index_in_dim(a, (g.x + dx) % g.xs, 0, keepdims=False)

    narrow = mine.astype(BF)
    total = for_chip(mine, 0, 0)
    for dx, dy in g.shifts[1:]:
        total = total + g.send(for_chip(narrow, dx, dy), dx=dx, dy=dy).astype(F32)

    def my_share(a):
        a = jnp.pad(a, ((0, 0), (0, padded - units)))
        return lax.dynamic_slice_in_dim(a, g.y * share, share, 1).astype(F32)

    gate, up = my_share(gate_pre), my_share(up_pre)
    squash = jax.nn.sigmoid(gate)
    grads = jnp.stack([total * up * squash * (1.0 + gate * (1.0 - squash)), total * gate * squash]).astype(BF)
    pieces = jnp.stack([grads] + [g.send(grads, dx=dx, dy=dy) for dx, dy in g.shifts[1:]])
    pieces = jnp.stack([pieces, g.swap(pieces)])
    pieces = pieces.reshape(CORES, g.xs, g.cols, 2, own, share)
    flipped = jnp.flip(pieces, 2)
    pieces = jnp.where(g.y == 0, pieces, flipped) if g.cols == 2 else jnp.roll(flipped, g.y + 1, axis=2)
    pieces = pieces.transpose(3, 0, 1, 4, 2, 5).reshape(2, slots, padded)[:, :, :units]
    input_part = dot_nt(pieces[0], w_gate) + dot_nt(pieces[1], w_up)

    image = slots // g.rows
    chip, local = route // own, route % own
    x, core = chip // CORES, chip % CORES
    place = ((core ^ g.core) * g.xs + (g.x - x) % g.xs) * own + local
    positions = jnp.arange(slots, dtype=jnp.int32)
    alive = positions % image < jnp.repeat(img_count, image)
    place = jnp.where(alive, place, -1)
    pick = (place[:, None] == positions[None, :]).astype(BF)
    image_grad = dot_nn(pick, input_part.astype(BF)).astype(BF)
    image_grad = sum_rows(g, image_grad)

    features = w_proj.shape[0] // SHUF
    steps = cdiv(cdiv(features, g.rows), LANES)
    shuffled = shuffle_matmul(image_grad, w_proj, (g.z * steps).reshape(1), steps)
    wide = steps * LANES
    keep = lax.dynamic_index_in_dim(shuffled, g.core, 0, keepdims=False)
    give = lax.dynamic_index_in_dim(shuffled, 1 - g.core, 0, keepdims=False)
    mine = (keep.astype(F32) + g.swap(give).astype(F32)).reshape(g.chips, SHUF * half // g.chips, wide)
    narrow = mine.astype(BF)

    def chip_part(a, dx, dy):
        index = ((g.x + dx) % g.xs) * g.cols + (g.y + dy) % g.cols
        return lax.dynamic_index_in_dim(a, index, 0, keepdims=False)

    total = chip_part(mine, 0, 0)
    for dx, dy in g.shifts[1:]:
        total = total + g.send(chip_part(narrow, dx, dy), dx=dx, dy=dy).astype(F32)
    patch_grad = total.astype(BF)
    patch_grad = jnp.concatenate([patch_grad] + [g.send(patch_grad, dx=dx, dy=dy) for dx, dy in g.shifts[1:]])
    patch_grad = gather_rows(g, patch_grad)
    patch_grad = jnp.concatenate([patch_grad, g.swap(patch_grad)], axis=1)

    all_hidden = gather_rows(g, enc_hidden)
    group = enc_hidden.shape[0]
    patches = group * g.rows
    piece = SHUF * half // g.chips
    spot = jnp.arange(patches, dtype=jnp.int32)
    core = (spot // (g.chips * piece)) ^ g.core
    shift = (spot // piece) % g.chips
    chip = ((g.x - shift // g.cols) % g.xs) * g.cols + (g.y - shift % g.cols) % g.cols
    inner = chip * piece + spot % piece
    patch = (core * half + inner % half) * SHUF + inner // half
    order = row_order(g)
    source = order[:, None] * group + jnp.arange(group, dtype=jnp.int32)[None, :]
    pick = (patch[:, None] == source.reshape(1, patches)).astype(BF)
    all_hidden = dot_nn(pick, all_hidden.reshape(patches, -1)).astype(BF)

    result = weight_grad(patch_grad, all_hidden, order, features, 1.0 / math.sqrt(patches))
    return result.T


def solution(mesh):
    placed = (
        P(None, ("enc", "col")),
        P("enc", "row"),
        P("enc", "row"),
        P(("enc", "col"), "row"),
        P(("enc", "col"), "row"),
        P("row", ("enc", "col")),
        P(None, ("enc", "col")),
        P("row", ("enc", "col")),
        P(),
        P(),
    )
    return jax.shard_map(
        shards, mesh=mesh, in_specs=placed, out_specs=P(None, ("enc", "col")), check_vma=False
    )
```

time: 433 us -> 148 us (0.34)
  waiting for transfers between devices: 251 us -> 52.4 us
  blocking collectives: 100 us -> 0 us
  starting transfers between devices: 5.85 us -> 27.8 us
  matrix products: 44.8 us -> 27.2 us
  between operations: 15.7 us -> 0.29 us
  Pallas kernels: 0 us -> 14.5 us
  other arithmetic: 0.23 us -> 6.22 us
  local copies, waits for them, and re-layouts: 15 us -> 19.5 us
    psum x1 -> x0, waiting for transfers between devices: 185 us -> none  [shards(): total = lax.psum(group_term.astype(jnp.bfloat16), 'row')]
    unnamed x6 -> x0, waiting for transfers between devices: 65.5 us -> none
    all_gather x5 -> x0, blocking collectives: 52.8 us -> none  [the longest x1 17.1 us: shards(): lax.all_gather(patch_grad, ('enc', 'col'), axis=1, tiled=True)]
    ppermute x0 -> x22, waiting for transfers between devices: none -> 52.4 us  [send(): return lax.ppermute(value, AXES, pairs)]
    unnamed x3 -> x0, blocking collectives: 47.2 us -> none
    ppermute x0 -> x22, starting transfers between devices: none -> 27.8 us  [send(): return lax.ppermute(value, AXES, pairs)]
    unnamed x1 -> x0, matrix products: 14.8 us -> none
    pallas_call x0 -> x2, Pallas kernels: none -> 14.5 us  [the longest x1 8.11 us: shuffle_matmul(): pl.pallas_call(kernel, out_shape=jax.ShapeDtypeStruct((CORES, SHUF, half,...]
  transfers between devices with their start and end apart: 5 -> 22, of which waited for: 4 -> 19; matrix products, arithmetic and copies ran while one was open for 0% -> 2% of each run, Pallas kernels for 0% -> 0%
where the time goes in v1:
time: 148 us
  waiting for transfers between devices  52.4 us (35%)
  starting transfers between devices  27.8 us (19%)
  matrix products  27.2 us (18%)
  local copies, waits for them, and re-layouts  19.5 us (13%)
  Pallas kernels  14.5 us (10%)
  other arithmetic  6.22 us (4%)
    ppermute x22, waiting for transfers between devices, send(): return lax.ppermute(value, AXES, pairs)  52.4 us
    ppermute x22, starting transfers between devices, send(): return lax.ppermute(value, AXES, pairs)  27.8 us
    dot_general x2, matrix products, dot_nt(): lax.dot_general(left, right, (((1,), (1,)), ((), ())), preferred_element_...  18 us
    rev x1, local copies, waits for them, and re-layouts, shards(): flipped = jnp.flip(pieces, 2)  12.6 us
    dot_general x2, matrix products, dot_nn(): lax.dot_general(left, right, (((1,), (0,)), ((), ())), preferred_element_...  9.24 us
    pallas_call x1, Pallas kernels, shuffle_matmul(): pl.pallas_call(kernel, out_shape=jax.ShapeDtypeStruct((CORES, SHUF, half,...  8.11 us
    pallas_call x1, Pallas kernels, weight_grad(): pl.pallas_call(kernel, out_shape=jax.ShapeDtypeStruct((units, features),...  6.41 us
  transfers between devices with their start and end apart: 22, of which 19 were waited for; matrix products, arithmetic and copies ran while one was open for 2% of the time, Pallas kernels for 0%

profile of v1, /device:TPU:0, one launch (start us, length us, event | category | flops | bytes accessed | tf_op | source)
XLA Modules:
  0.0 147.9 jit_solution(15179754836210675642)
XLA Ops:
  0.9 9.9 %fusion.41 = f32[48,7392]{1,0:T(8,128)S(1)} fusion(bf16[48,1024]{1,0:T(8,128)(2,1)S(1)} %copy-done, bf16[7392,1024]{1,0:T(8,128)(2,1)} %param.16), kind=kOutput, calls=%fused_computation.120 | convolution fusion | flops 726663168 | bytes 16656384 | tf_op jit(solution)/shard_map/dot_general | solution.py:24
  15.1 2.9 %collective-permute-start.2 = (bf16[12,3712]{1,0:T(8,128)(2,1)S(1)}, bf16[12,3712]{1,0:T(8,128)(2,1)S(1)}, u32[]{:S(2)}, u32[]{:S(2)}) collective-permute-start(bf16[12,3712]{1,0:T(8,128)(2,1)S(1)} %bitcast.94), channel_id=1, source_target_pairs={{0,16},{1,17},{2,18},{3,19},{4,20},{5,21},{6,22},{7,23},{8,24},{9,... | collective-permute-start | bytes 267272 | tf_op jit(solution)/shard_map/ppermute | solution.py:56
  19.7 2.0 %collective-permute-done.2 = bf16[12,3712]{1,0:T(8,128)(2,1)S(1)} collective-permute-done((bf16[12,3712]{1,0:T(8,128)(2,1)S(1)}, bf16[12,3712]{1,0:T(8,128)(2,1)S(1)}, u32[]{:S(2)}, u32[]{:S(2)}) %collective-permute-start.2) | collective-permute-done | bytes 89120 | tf_op jit(solution)/shard_map/ppermute | solution.py:56
  21.7 3.7 %collective-permute-done.3 = bf16[12,3712]{1,0:T(8,128)(2,1)S(1)} collective-permute-done((bf16[12,3712]{1,0:T(8,128)(2,1)S(1)}, bf16[12,3712]{1,0:T(8,128)(2,1)S(1)}, u32[]{:S(2)}, u32[]{:S(2)}) %collective-permute-start.3) | collective-permute-done | bytes 89120 | tf_op jit(solution)/shard_map/ppermute | solution.py:56
  28.9 1.7 %collective-permute-start.4 = (bf16[2,12,3712]{2,1,0:T(8,128)(2,1)S(1)}, bf16[2,12,3712]{2,1,0:T(8,128)(2,1)S(1)}, u32[]{:S(2)}, u32[]{:S(2)}) collective-permute-start(bf16[2,12,3712]{2,1,0:T(8,128)(2,1)S(1)} %pad_maximum_fusion.5), channel_id=1, source_target_pairs={{0,1},{1,0},{2,3},{3,2},{4,5},{5,4},{6,7},{7,6},{8,9},{9,8},{10,11... | collective-permute-start | bytes 534536 | tf_op jit(solution)/shard_map/ppermute | solution.py:56
  30.6 6.1 %collective-permute-done.6 = bf16[2,12,3712]{2,1,0:T(8,128)(2,1)S(1)} collective-permute-done((bf16[2,12,3712]{2,1,0:T(8,128)(2,1)S(1)}, bf16[2,12,3712]{2,1,0:T(8,128)(2,1)S(1)}, u32[]{:S(2)}, u32[]{:S(2)}) %collective-permute-start.6) | collective-permute-done | bytes 178208 | tf_op jit(solution)/shard_map/ppermute | solution.py:56
  36.7 2.2 %collective-permute-done.5 = bf16[2,12,3712]{2,1,0:T(8,128)(2,1)S(1)} collective-permute-done((bf16[2,12,3712]{2,1,0:T(8,128)(2,1)S(1)}, bf16[2,12,3712]{2,1,0:T(8,128)(2,1)S(1)}, u32[]{:S(2)}, u32[]{:S(2)}) %collective-permute-start.5) | collective-permute-done | bytes 178208 | tf_op jit(solution)/shard_map/ppermute | solution.py:56
  41.3 1.6 %collective-permute-done.7 = bf16[4,2,12,3712]{3,0,2,1:T(4,128)(2,1)S(1)} collective-permute-done((bf16[4,2,12,3712]{3,0,2,1:T(4,128)(2,1)S(1)}, bf16[4,2,12,3712]{3,0,2,1:T(4,128)(2,1)S(1)}, u32[]{:S(2)}, u32[]{:S(2)}) %collective-permute-start.7) | collective-permute-done | bytes 712736 | tf_op jit(solution)/shard_map/ppermute | solution.py:56
  43.8 12.6 %rev.4 = bf16[2,2,2,2,12,3712]{5,2,4,1,0,3:T(2,128)(2,1)} reverse(bf16[2,2,2,2,12,3712]{5,2,4,1,0,3:T(2,128)(2,1)S(1)} %copy_dynamic-update-slice_fusion), dimensions={2} | reverse | bytes 2850816 | tf_op jit(solution)/shard_map/jit(_flip)/rev | solution.py:194
  58.8 8.0 %fusion.2 = f32[48,1024]{1,0:T(8,128)S(1)} fusion(bf16[1024,7392]{0,1:T(8,128)(2,1)} %param.14, bf16[2,48,7424]{2,1,0:T(8,128)(2,1)S(1)} %reshape.191), kind=kOutput, calls=%fused_computation.10 | convolution fusion | flops 726663168 | bytes 16048128 | tf_op jit(solution)/shard_map/dot_general | solution.py:24
  66.9 8.2 %convolution_convert_fusion.1 = bf16[48,1024]{1,0:T(8,128)(2,1)S(1)} fusion(f32[48,1024]{1,0:T(8,128)S(1)} %fusion.2, bf16[1024,7392]{0,1:T(8,128)(2,1)} %param.15, bf16[2,48,7424]{2,1,0:T(8,128)(2,1)S(1)} %reshape.191, s32[48]{0:T(128)S(1)} %compare_select_fusion.8), kind=kOutput, calls=%fused_computation.6 | convolution fusion | flops 731531520 | bytes 16146944 | tf_op jit(solution)/shard_map/dot_general | solution.py:28
  75.1 1.6 %collective-permute-start.8 = (bf16[48,1024]{1,0:T(8,128)(2,1)S(1)}, bf16[48,1024]{1,0:T(8,128)(2,1)S(1)}, u32[]{:S(2)}, u32[]{:S(2)}) collective-permute-start(bf16[48,1024]{1,0:T(8,128)(2,1)S(1)} %convolution_convert_fusion.1), channel_id=1, source_target_pairs={{0,2},{1,3},{2,0},{3,1},{4,6},{5,7},{6,4},{7,5},{8,10},{9,11},{10,... | collective-permute-start | bytes 294920 | tf_op jit(solution)/shard_map/ppermute | solution.py:56
  76.7 3.3 %collective-permute-done.8 = bf16[48,1024]{1,0:T(8,128)(2,1)S(1)} collective-permute-done((bf16[48,1024]{1,0:T(8,128)(2,1)S(1)}, bf16[48,1024]{1,0:T(8,128)(2,1)S(1)}, u32[]{:S(2)}, u32[]{:S(2)}) %collective-permute-start.8) | collective-permute-done | bytes 98336 | tf_op jit(solution)/shard_map/ppermute | solution.py:56
  80.0 3.7 %collective-permute-start.9 = (bf16[48,1024]{1,0:T(8,128)(2,1)S(1)}, bf16[48,1024]{1,0:T(8,128)(2,1)S(1)}, u32[]{:S(2)}, u32[]{:S(2)}) collective-permute-start(bf16[48,1024]{1,0:T(8,128)(2,1)S(1)} %add_convert_fusion.1), channel_id=1, source_target_pairs={{0,6},{1,7},{2,4},{3,5},{4,2},{5,3},{6,0},{7,1},{8,14},{9,15},{10,... | collective-permute-start | bytes 294920 | tf_op jit(solution)/shard_map/ppermute | solution.py:56
  83.7 2.9 %collective-permute-done.9 = bf16[48,1024]{1,0:T(8,128)(2,1)S(1)} collective-permute-done((bf16[48,1024]{1,0:T(8,128)(2,1)S(1)}, bf16[48,1024]{1,0:T(8,128)(2,1)S(1)}, u32[]{:S(2)}, u32[]{:S(2)}) %collective-permute-start.9) | collective-permute-done | bytes 98336 | tf_op jit(solution)/shard_map/ppermute | solution.py:56
  87.3 8.1 %shuffle_matmul.1 = bf16[2,4,24,896]{3,2,1,0:T(8,128)(2,1)} custom-call(s32[1]{0:T(128)} %bitcast.first_ref, bf16[48,1024]{1,0:T(8,128)(2,1)} %add_convert_fusion.grad_ref, bf16[12800,1024]{1,0:T(8,128)(2,1)} %w_ref.1), custom_call_target="tpu_custom_call" | custom-call | flops 352321536 | bytes 7340032 | tf_op jit(solution)/shard_map/shuffle_matmul/pallas_call | solution.py:81
  98.8 2.0 %collective-permute-start.11 = (bf16[24,896]{1,0:T(8,128)(2,1)S(1)}, bf16[24,896]{1,0:T(8,128)(2,1)S(1)}, u32[]{:S(2)}, u32[]{:S(2)}) collective-permute-start(bf16[24,896]{1,0:T(8,128)(2,1)S(1)} %get-tuple-element.14), channel_id=1, source_target_pairs={{0,1},{1,0},{2,3},{3,2},{4,5},{5,4},{6,7},{7,6},{8,9},{9,8},{10,11... | collective-permute-start | bytes 129032 | tf_op jit(solution)/shard_map/ppermute | solution.py:56
  102.9 3.2 %collective-permute-done.13 = bf16[24,896]{1,0:T(8,128)(2,1)S(1)} collective-permute-done((bf16[24,896]{1,0:T(8,128)(2,1)S(1)}, bf16[24,896]{1,0:T(8,128)(2,1)S(1)}, u32[]{:S(2)}, u32[]{:S(2)}) %collective-permute-start.13) | collective-permute-done | bytes 43040 | tf_op jit(solution)/shard_map/ppermute | solution.py:56
  106.1 1.7 %collective-permute-start.16 = (bf16[24,896]{1,0:T(8,128)(2,1)S(1)}, bf16[24,896]{1,0:T(8,128)(2,1)S(1)}, u32[]{:S(2)}, u32[]{:S(2)}) collective-permute-start(bf16[24,896]{1,0:T(8,128)(2,1)S(1)} %fusion.19), channel_id=1, source_target_pairs={{0,17},{1,16},{2,19},{3,18},{4,21},{5,20},{6,23},{7,22},{8,25},{9,... | collective-permute-start | bytes 129032 | tf_op jit(solution)/shard_map/ppermute | solution.py:56
  114.6 4.3 %collective-permute-done.17 = bf16[1,96,896]{2,1,0:T(8,128)(2,1)S(1)} collective-permute-done((bf16[1,96,896]{2,1,0:T(8,128)(2,1)S(1)}, bf16[1,96,896]{2,1,0:T(8,128)(2,1)S(1)}, u32[]{:S(2)}, u32[]{:S(2)}) %collective-permute-start.17) | collective-permute-done | bytes 172064 | tf_op jit(solution)/shard_map/ppermute | solution.py:56
  118.9 3.6 %collective-permute-start.18 = (bf16[2,96,896]{2,1,0:T(8,128)(2,1)S(1)}, bf16[2,96,896]{2,1,0:T(8,128)(2,1)S(1)}, u32[]{:S(2)}, u32[]{:S(2)}) collective-permute-start(bf16[2,96,896]{2,1,0:T(8,128)(2,1)S(1)} %pad_maximum_fusion.3), channel_id=1, source_target_pairs={{0,6},{1,7},{2,4},{3,5},{4,2},{5,3},{6,0},{7,1},{8,14},{9,15},{10,... | collective-permute-start | bytes 1032200 | tf_op jit(solution)/shard_map/ppermute | solution.py:56
  124.6 7.1 %collective-permute-done.20 = bf16[1,48,800]{2,1,0:T(8,128)(2,1)S(1)} collective-permute-done((bf16[1,48,800]{2,1,0:T(8,128)(2,1)S(1)}, bf16[1,48,800]{2,1,0:T(8,128)(2,1)S(1)}, u32[]{:S(2)}, u32[]{:S(2)}) %collective-permute-start.20) | collective-permute-done | bytes 76832 | tf_op jit(solution)/shard_map/ppermute | solution.py:56
  132.2 6.8 %collective-permute-done.21 = bf16[2,48,800]{2,1,0:T(8,128)(2,1)S(1)} collective-permute-done((bf16[2,48,800]{2,1,0:T(8,128)(2,1)S(1)}, bf16[2,48,800]{2,1,0:T(8,128)(2,1)S(1)}, u32[]{:S(2)}, u32[]{:S(2)}) %collective-permute-start.21) | collective-permute-done | bytes 153632 | tf_op jit(solution)/shard_map/ppermute | solution.py:56
  141.4 6.4 %weight_grad.1 = bf16[800,3200]{1,0:T(8,128)(2,1)} custom-call(s32[4]{0:T(128)} %get-tuple-element.18.where_ref, bf16[4,192,896]{2,1,0:T(8,128)(2,1)} %pad_maximum_fusion.patch_ref, bf16[192,800]{1,0:T(8,128)(2,1)} %convolution_convert_fusion.hidden_ref), custom_call_target="tpu_custom_call" | custom-call | flops 1101004800 | bytes 5120000 | tf_op jit(solution)/shard_map/weight_grad/pallas_call | solution.py:108
  (80 shorter events, 33.8 us)
Async XLA Ops:
  12.1 1.9 %collective-permute-start = (bf16[2,2,12,3712]{3,0,2,1:T(2,128)(2,1)S(1)}, bf16[2,2,12,3712]{3,0,2,1:T(2,128)(2,1)S(1)}, u32[]{:S(2)}, u32[]{:S(2)}) collective-permute-start(bf16[2,2,12,3712]{3,0,2,1:T(2,128)(2,1)S(1)} %fusion.3), channel_id=1, source_target_pairs={{0,8},{1,9},{2,10},{3,11},{4,12},{5,13},{6,14},{7,15},{8,0},{9,1},... | collective-permute-start | bytes 1069064 | tf_op jit(solution)/shard_map/ppermute | solution.py:56
  15.1 6.6 %collective-permute-start.2 = (bf16[12,3712]{1,0:T(8,128)(2,1)S(1)}, bf16[12,3712]{1,0:T(8,128)(2,1)S(1)}, u32[]{:S(2)}, u32[]{:S(2)}) collective-permute-start(bf16[12,3712]{1,0:T(8,128)(2,1)S(1)} %bitcast.94), channel_id=1, source_target_pairs={{0,16},{1,17},{2,18},{3,19},{4,20},{5,21},{6,22},{7,23},{8,24},{9,... | collective-permute-start | bytes 267272 | tf_op jit(solution)/shard_map/ppermute | solution.py:56
  18.0 7.4 %collective-permute-start.3 = (bf16[12,3712]{1,0:T(8,128)(2,1)S(1)}, bf16[12,3712]{1,0:T(8,128)(2,1)S(1)}, u32[]{:S(2)}, u32[]{:S(2)}) collective-permute-start(bf16[12,3712]{1,0:T(8,128)(2,1)S(1)} %bitcast.93), channel_id=1, source_target_pairs={{0,17},{1,16},{2,19},{3,18},{4,21},{5,20},{6,23},{7,22},{8,25},{9,... | collective-permute-start | bytes 267272 | tf_op jit(solution)/shard_map/ppermute | solution.py:56
  19.5 7.3 %collective-permute-start.1 = (bf16[12,3712]{1,0:T(8,128)(2,1)S(1)}, bf16[12,3712]{1,0:T(8,128)(2,1)S(1)}, u32[]{:S(2)}, u32[]{:S(2)}) collective-permute-start(bf16[12,3712]{1,0:T(8,128)(2,1)S(1)} %bitcast.92), channel_id=1, source_target_pairs={{0,1},{1,0},{2,3},{3,2},{4,5},{5,4},{6,7},{7,6},{8,9},{9,8},{10,11... | collective-permute-start | bytes 267272 | tf_op jit(solution)/shard_map/ppermute | solution.py:56
  27.0 9.7 %collective-permute-start.6 = (bf16[2,12,3712]{2,1,0:T(8,128)(2,1)S(1)}, bf16[2,12,3712]{2,1,0:T(8,128)(2,1)S(1)}, u32[]{:S(2)}, u32[]{:S(2)}) collective-permute-start(bf16[2,12,3712]{2,1,0:T(8,128)(2,1)S(1)} %pad_maximum_fusion.5), channel_id=1, source_target_pairs={{0,17},{1,16},{2,19},{3,18},{4,21},{5,20},{6,23},{7,22},{8,25},{9,... | collective-permute-start | bytes 534536 | tf_op jit(solution)/shard_map/ppermute | solution.py:56
  28.5 10.4 %collective-permute-start.5 = (bf16[2,12,3712]{2,1,0:T(8,128)(2,1)S(1)}, bf16[2,12,3712]{2,1,0:T(8,128)(2,1)S(1)}, u32[]{:S(2)}, u32[]{:S(2)}) collective-permute-start(bf16[2,12,3712]{2,1,0:T(8,128)(2,1)S(1)} %pad_maximum_fusion.5), channel_id=1, source_target_pairs={{0,16},{1,17},{2,18},{3,19},{4,20},{5,21},{6,22},{7,23},{8,24},{9,... | collective-permute-start | bytes 534536 | tf_op jit(solution)/shard_map/ppermute | solution.py:56
  28.9 11.2 %collective-permute-start.4 = (bf16[2,12,3712]{2,1,0:T(8,128)(2,1)S(1)}, bf16[2,12,3712]{2,1,0:T(8,128)(2,1)S(1)}, u32[]{:S(2)}, u32[]{:S(2)}) collective-permute-start(bf16[2,12,3712]{2,1,0:T(8,128)(2,1)S(1)} %pad_maximum_fusion.5), channel_id=1, source_target_pairs={{0,1},{1,0},{2,3},{3,2},{4,5},{5,4},{6,7},{7,6},{8,9},{9,8},{10,11... | collective-permute-start | bytes 534536 | tf_op jit(solution)/shard_map/ppermute | solution.py:56
  40.7 2.2 %collective-permute-start.7 = (bf16[4,2,12,3712]{3,0,2,1:T(4,128)(2,1)S(1)}, bf16[4,2,12,3712]{3,0,2,1:T(4,128)(2,1)S(1)}, u32[]{:S(2)}, u32[]{:S(2)}) collective-permute-start(bf16[4,2,12,3712]{3,0,2,1:T(4,128)(2,1)S(1)} %copy.27), channel_id=1, source_target_pairs={{0,8},{1,9},{2,10},{3,11},{4,12},{5,13},{6,14},{7,15},{8,0},{9,1},... | collective-permute-start | bytes 2138120 | tf_op jit(solution)/shard_map/ppermute | solution.py:56
  75.1 4.9 %collective-permute-start.8 = (bf16[48,1024]{1,0:T(8,128)(2,1)S(1)}, bf16[48,1024]{1,0:T(8,128)(2,1)S(1)}, u32[]{:S(2)}, u32[]{:S(2)}) collective-permute-start(bf16[48,1024]{1,0:T(8,128)(2,1)S(1)} %convolution_convert_fusion.1), channel_id=1, source_target_pairs={{0,2},{1,3},{2,0},{3,1},{4,6},{5,7},{6,4},{7,5},{8,10},{9,11},{10,... | collective-permute-start | bytes 294920 | tf_op jit(solution)/shard_map/ppermute | solution.py:56
  80.0 6.6 %collective-permute-start.9 = (bf16[48,1024]{1,0:T(8,128)(2,1)S(1)}, bf16[48,1024]{1,0:T(8,128)(2,1)S(1)}, u32[]{:S(2)}, u32[]{:S(2)}) collective-permute-start(bf16[48,1024]{1,0:T(8,128)(2,1)S(1)} %add_convert_fusion.1), channel_id=1, source_target_pairs={{0,6},{1,7},{2,4},{3,5},{4,2},{5,3},{6,0},{7,1},{8,14},{9,15},{10,... | collective-permute-start | bytes 294920 | tf_op jit(solution)/shard_map/ppermute | solution.py:56
  95.4 27.2 %copy-start.2 = (bf16[48,800]{1,0:T(8,128)(2,1)S(1)}, bf16[48,800]{1,0:T(8,128)(2,1)}, u32[]{:S(2)}) copy-start(bf16[48,800]{1,0:T(8,128)(2,1)} %param.18) | copy-start | bytes 230404
  95.4 28.8 %copy-start.7 = (s32[4]{0:T(128)S(1)}, s32[4]{0:T(128)}, u32[]{:S(2)}) copy-start(s32[4]{0:T(128)} %constant.329.clone) | copy-start | bytes 52
  96.3 1.5 collective-permute-start.10
  98.8 4.1 %collective-permute-start.11 = (bf16[24,896]{1,0:T(8,128)(2,1)S(1)}, bf16[24,896]{1,0:T(8,128)(2,1)S(1)}, u32[]{:S(2)}, u32[]{:S(2)}) collective-permute-start(bf16[24,896]{1,0:T(8,128)(2,1)S(1)} %get-tuple-element.14), channel_id=1, source_target_pairs={{0,1},{1,0},{2,3},{3,2},{4,5},{5,4},{6,7},{7,6},{8,9},{9,8},{10,11... | collective-permute-start | bytes 129032 | tf_op jit(solution)/shard_map/ppermute | solution.py:56
  100.8 5.3 %collective-permute-start.13 = (bf16[24,896]{1,0:T(8,128)(2,1)S(1)}, bf16[24,896]{1,0:T(8,128)(2,1)S(1)}, u32[]{:S(2)}, u32[]{:S(2)}) collective-permute-start(bf16[24,896]{1,0:T(8,128)(2,1)S(1)} %get-tuple-element.15), channel_id=1, source_target_pairs={{0,17},{1,16},{2,19},{3,18},{4,21},{5,20},{6,23},{7,22},{8,25},{9,... | collective-permute-start | bytes 129032 | tf_op jit(solution)/shard_map/ppermute | solution.py:56
  101.8 4.3 %collective-permute-start.12 = (bf16[24,896]{1,0:T(8,128)(2,1)S(1)}, bf16[24,896]{1,0:T(8,128)(2,1)S(1)}, u32[]{:S(2)}, u32[]{:S(2)}) collective-permute-start(bf16[24,896]{1,0:T(8,128)(2,1)S(1)} %get-tuple-element.16), channel_id=1, source_target_pairs={{0,16},{1,17},{2,18},{3,19},{4,20},{5,21},{6,22},{7,23},{8,24},{9,... | collective-permute-start | bytes 129032 | tf_op jit(solution)/shard_map/ppermute | solution.py:56
  106.1 5.0 %collective-permute-start.16 = (bf16[24,896]{1,0:T(8,128)(2,1)S(1)}, bf16[24,896]{1,0:T(8,128)(2,1)S(1)}, u32[]{:S(2)}, u32[]{:S(2)}) collective-permute-start(bf16[24,896]{1,0:T(8,128)(2,1)S(1)} %fusion.19), channel_id=1, source_target_pairs={{0,17},{1,16},{2,19},{3,18},{4,21},{5,20},{6,23},{7,22},{8,25},{9,... | collective-permute-start | bytes 129032 | tf_op jit(solution)/shard_map/ppermute | solution.py:56
  107.9 4.0 %collective-permute-start.15 = (bf16[24,896]{1,0:T(8,128)(2,1)S(1)}, bf16[24,896]{1,0:T(8,128)(2,1)S(1)}, u32[]{:S(2)}, u32[]{:S(2)}) collective-permute-start(bf16[24,896]{1,0:T(8,128)(2,1)S(1)} %fusion.19), channel_id=1, source_target_pairs={{0,16},{1,17},{2,18},{3,19},{4,20},{5,21},{6,22},{7,23},{8,24},{9,... | collective-permute-start | bytes 129032 | tf_op jit(solution)/shard_map/ppermute | solution.py:56
  109.4 4.0 %collective-permute-start.14 = (bf16[24,896]{1,0:T(8,128)(2,1)S(1)}, bf16[24,896]{1,0:T(8,128)(2,1)S(1)}, u32[]{:S(2)}, u32[]{:S(2)}) collective-permute-start(bf16[24,896]{1,0:T(8,128)(2,1)S(1)} %fusion.19), channel_id=1, source_target_pairs={{0,1},{1,0},{2,3},{3,2},{4,5},{5,4},{6,7},{7,6},{8,9},{9,8},{10,11... | collective-permute-start | bytes 129032 | tf_op jit(solution)/shard_map/ppermute | solution.py:56
  113.4 5.5 %collective-permute-start.17 = (bf16[1,96,896]{2,1,0:T(8,128)(2,1)S(1)}, bf16[1,96,896]{2,1,0:T(8,128)(2,1)S(1)}, u32[]{:S(2)}, u32[]{:S(2)}) collective-permute-start(bf16[1,96,896]{2,1,0:T(8,128)(2,1)S(1)} %maximum_bitcast_fusion), channel_id=1, source_target_pairs={{0,2},{1,3},{2,0},{3,1},{4,6},{5,7},{6,4},{7,5},{8,10},{9,11},{10,... | collective-permute-start | bytes 516104 | tf_op jit(solution)/shard_map/ppermute | solution.py:56
  118.9 12.9 %collective-permute-start.18 = (bf16[2,96,896]{2,1,0:T(8,128)(2,1)S(1)}, bf16[2,96,896]{2,1,0:T(8,128)(2,1)S(1)}, u32[]{:S(2)}, u32[]{:S(2)}) collective-permute-start(bf16[2,96,896]{2,1,0:T(8,128)(2,1)S(1)} %pad_maximum_fusion.3), channel_id=1, source_target_pairs={{0,6},{1,7},{2,4},{3,5},{4,2},{5,3},{6,0},{7,1},{8,14},{9,15},{10,... | collective-permute-start | bytes 1032200 | tf_op jit(solution)/shard_map/ppermute | solution.py:56
  122.6 9.1 %collective-permute-start.20 = (bf16[1,48,800]{2,1,0:T(8,128)(2,1)S(1)}, bf16[1,48,800]{2,1,0:T(8,128)(2,1)S(1)}, u32[]{:S(2)}, u32[]{:S(2)}) collective-permute-start(bf16[1,48,800]{2,1,0:T(8,128)(2,1)S(1)} %bitcast.86), channel_id=1, source_target_pairs={{0,2},{1,3},{2,0},{3,1},{4,6},{5,7},{6,4},{7,5},{8,10},{9,11},{10,... | collective-permute-start | bytes 230408 | tf_op jit(solution)/shard_map/ppermute | solution.py:56
  131.7 7.4 %collective-permute-start.21 = (bf16[2,48,800]{2,1,0:T(8,128)(2,1)S(1)}, bf16[2,48,800]{2,1,0:T(8,128)(2,1)S(1)}, u32[]{:S(2)}, u32[]{:S(2)}) collective-permute-start(bf16[2,48,800]{2,1,0:T(8,128)(2,1)S(1)} %pad_maximum_fusion.6), channel_id=1, source_target_pairs={{0,6},{1,7},{2,4},{3,5},{4,2},{5,3},{6,0},{7,1},{8,14},{9,15},{10,... | collective-permute-start | bytes 460808 | tf_op jit(solution)/shard_map/ppermute | solution.py:56
  132.0 8.3 %collective-permute-start.19 = (bf16[4,96,896]{2,1,0:T(8,128)(2,1)S(1)}, bf16[4,96,896]{2,1,0:T(8,128)(2,1)S(1)}, u32[]{:S(2)}, u32[]{:S(2)}) collective-permute-start(bf16[4,96,896]{2,1,0:T(8,128)(2,1)S(1)} %pad_maximum_fusion.2), channel_id=1, source_target_pairs={{0,8},{1,9},{2,10},{3,11},{4,12},{5,13},{6,14},{7,15},{8,0},{9,1},... | collective-permute-start | bytes 2064392 | tf_op jit(solution)/shard_map/ppermute | solution.py:56
  (6 other events, 49.3 us)

commit v2 on v0

v2 whole, which is shorter than its diff:
```python
import functools
import math

import jax
import jax.numpy as jnp
from jax import lax
from jax.experimental import pallas as pl
from jax.experimental.pallas import tpu as pltpu
from jax.sharding import PartitionSpec as P

SHUF = 4
CORES = 2
LANES = 128
AXES = ("enc", "row", "col")
BF = jnp.bfloat16
F32 = jnp.float32


def cdiv(a, b):
    return -(-a // b)


def dot_nt(left, right):
    return lax.dot_general(left, right, (((1,), (1,)), ((), ())), preferred_element_type=F32)


def dot_nn(left, right):
    return lax.dot_general(left, right, (((1,), (0,)), ((), ())), preferred_element_type=F32)


def dot_tn(left, right):
    return lax.dot_general(left, right, (((0,), (0,)), ((), ())), preferred_element_type=F32)


class Grid:
    def __init__(self):
        self.enc, self.rows, self.cols = (lax.axis_size(a) for a in AXES)
        self.xs = self.enc // CORES
        self.chips = self.xs * self.cols
        enc = lax.axis_index("enc")
        self.core = enc % CORES
        self.x = enc // CORES
        self.y = lax.axis_index("col")
        self.z = lax.axis_index("row")
        self.shifts = [(dx, dy) for dx in range(self.xs) for dy in range(self.cols)]

    def send(self, value, dx=0, dy=0, core=0, row=None):
        pairs = []
        for e in range(self.enc):
            for r in range(self.rows):
                for c in range(self.cols):
                    x, k = divmod(e, CORES)
                    target = (((x + dx) % self.xs) * CORES + (k ^ core), r if row is None else row(r), (c + dy) % self.cols)
                    flat = [(a * self.rows + b) * self.cols + d for a, b, d in ((e, r, c), target)]
                    pairs.append(tuple(flat))
        return lax.ppermute(value, AXES, pairs)

    def swap(self, value):
        return self.send(value, core=1)

    def place(self):
        return jnp.stack([self.core, self.x, self.y, self.z]).astype(jnp.int32)


MIB = 2**20
HINT = (4 * 10**10, 10**8)
VM = pl.BlockSpec(memory_space=pltpu.VMEM)
SM = pl.BlockSpec(memory_space=pltpu.SMEM)
HBM = pl.BlockSpec(memory_space=pltpu.HBM)


def local_call(kernel, name, out_shape, in_specs, args, limit, scratch=(), busy=(0, 0), out_specs=None):
    return pl.pallas_call(
        kernel,
        out_shape=out_shape,
        in_specs=in_specs,
        out_specs=jax.tree.map(lambda _: VM, out_shape) if out_specs is None else out_specs,
        scratch_shapes=list(scratch),
        compiler_params=pltpu.CompilerParams(vmem_limit_bytes=limit * MIB),
        cost_estimate=pl.CostEstimate(flops=busy[0], bytes_accessed=busy[1], transcendentals=0),
        name=name,
    )(*args)


def spans(total, step):
    return [(s, min(step, total - s)) for s in range(0, total, step)]


def down_matmul(g, at, out_grad, w_down, own, tall, share):
    slots, width = out_grad.shape
    units = w_down.shape[0]
    half = g.xs * tall
    parts = []
    for c in range(g.cols):
        valid = max(0, min(share, units - c * share))
        parts += [(c, off, n) for off, n in spans(valid, 2048)]

    def kernel(pos, grad_hbm, w_ref, keep_ref, give_ref, grad_ref, buf, sem):
        first = pltpu.make_async_copy(grad_hbm, grad_ref, sem.at[len(parts)])
        first.start()
        copies = []
        for i, (c, off, n) in enumerate(parts):
            span = pl.ds(c * share + off, n)
            copies.append(pltpu.make_async_copy(w_ref.at[span], buf.at[span], sem.at[i]))
            copies[-1].start()
        row = lax.broadcasted_iota(jnp.int32, (CORES * half, slots), 0)
        col = lax.broadcasted_iota(jnp.int32, (CORES * half, slots), 1)
        core, x, inner = row // half, row // tall % g.xs, row % tall
        device = (x + pos[1]) % g.xs * CORES + (core + pos[0]) % CORES
        pick = jnp.where((inner < own) & (col == device * own + inner), 1.0, 0.0).astype(BF)
        first.wait()
        left = dot_nn(pick, grad_ref[...]).astype(BF)
        for copy, (c, off, n) in zip(copies, parts):
            copy.wait()
            out = dot_nt(left, buf[c * share + off : c * share + off + n]).astype(BF)
            keep_ref[c, :, off : off + n] = out[:half]
            give_ref[c, :, off : off + n] = out[half:]
        for c in range(g.cols):
            valid = max(0, min(share, units - c * share))
            if valid < share:
                for ref in (keep_ref, give_ref):
                    ref[c, :, valid:] = jnp.zeros((half, share - valid), BF)

    shape = jax.ShapeDtypeStruct((g.cols, half, share), BF)
    return local_call(
        kernel, "down_matmul", [shape, shape], [SM, HBM, HBM], (at, out_grad, w_down), 52,
        [pltpu.VMEM((slots, width), BF), pltpu.VMEM((units, width), BF), pltpu.SemaphoreType.DMA((len(parts) + 1,))],
        busy=(2 * slots * units * width, 2 * units * width),
    )


def core_sum(g, at, keep, other, tall):
    share = keep.shape[2]

    def kernel(pos, keep_ref, other_ref, own_ref, *piece_refs):
        for (dx, dy), ref in zip(g.shifts, (own_ref,) + piece_refs):
            col = (pos[2] + dy) % g.cols
            rows = pl.ds(dx * tall, tall)
            ref[...] = (keep_ref[col, rows].astype(F32) + other_ref[col, rows].astype(F32)).astype(ref.dtype)

    shapes = [jax.ShapeDtypeStruct((tall, share), F32 if s == (0, 0) else BF) for s in g.shifts]
    return local_call(kernel, "core_sum", shapes, [SM, VM, VM], (at, keep, other), 4, busy=HINT)


def gate_grads(g, at, total, others, gate_pre, up_pre):
    share = total.shape[1]
    own, units = gate_pre.shape

    def kernel(pos, total_ref, *refs):
        other_refs, (gate_ref, up_ref, out_ref) = refs[:-3], refs[-3:]
        hidden = total_ref[...]
        for ref in other_refs:
            hidden = hidden + ref[...].astype(F32)
        hidden = hidden[:own]
        for c in range(g.cols):
            valid = max(0, min(share, units - c * share))

            @pl.when(pos[2] == c)
            def _():
                gate = gate_ref[:, c * share : c * share + valid].astype(F32)
                up = up_ref[:, c * share : c * share + valid].astype(F32)
                grad = hidden[:, :valid]
                squash = 1.0 / (1.0 + jnp.exp(-gate))
                base = grad * squash
                out_ref[:own, :valid] = (base * up * (1.0 + gate * (1.0 - squash))).astype(BF)
                out_ref[own:, :valid] = (base * gate).astype(BF)
                if valid < share:
                    out_ref[:, valid:] = jnp.zeros((2 * own, share - valid), BF)

    shape = jax.ShapeDtypeStruct((2 * own, share), BF)
    return local_call(
        kernel, "gate_grads", shape, [SM] + [VM] * (len(others) + 3),
        (at, total, *others, gate_pre, up_pre), 4, busy=HINT,
    )


def input_matmul(g, at, pieces, route, img_count, w_gate, w_up, own):
    share = pieces[0].shape[1]
    units, width = w_gate.shape
    slots = route.shape[1]
    image = slots // g.rows
    half = slots // CORES
    rows = len(pieces) // g.cols
    order = [(core, dx, dy) for core in range(CORES) for dx, dy in g.shifts]

    def kernel(pos, count_ref, *refs):
        piece_refs, (route_ref, gate_ref, up_ref, out_ref, left) = refs[: len(pieces)], refs[len(pieces) :]
        for (core, dx, dy), ref in zip(order, piece_refs):
            at_row = (core * g.xs + dx) * 2 * own
            left[(pos[2] - dy + g.cols) % g.cols, at_row : at_row + 2 * own] = ref[...]
        gate, up = 0.0, 0.0
        for c in range(g.cols):
            valid = max(0, min(share, units - c * share))
            for off, n in spans(valid, 1920):
                row = c * share + off
                part = left[c, :, off : off + n]
                gate = gate + dot_nn(part, gate_ref[row : row + n])
                up = up + dot_nn(part, up_ref[row : row + n])
        both = [gate[2 * r * own : 2 * r * own + own] + up[2 * r * own + own : 2 * (r + 1) * own] for r in range(rows)]
        line = route_ref[...]
        device, local = lax.div(line, own), lax.rem(line, own)
        x, core = lax.div(device, CORES), lax.rem(device, CORES)
        away = lax.rem(pos[1] - x + g.xs, g.xs)
        place = (lax.rem(core + pos[0], CORES) * g.xs + away) * own + local
        slot = lax.broadcasted_iota(jnp.int32, (1, slots), 1)
        live = jnp.zeros((1, slots), jnp.int32)
        for r in range(g.rows):
            live = jnp.where(lax.div(slot, image) == r, count_ref[r], live)
        place = jnp.where(lax.rem(slot, image) < live, place, -1)
        pick = jnp.where(lax.broadcasted_iota(jnp.int32, (slots, slots), 0) == place, 1.0, 0.0).astype(BF)
        done = dot_tn(pick, jnp.concatenate(both).astype(BF)).astype(BF)
        for k in range(CORES):

            @pl.when(pos[0] == k)
            def _():
                out_ref[:half] = done[k * half : (k + 1) * half]
                out_ref[half:] = done[(1 - k) * half : (2 - k) * half]

    return local_call(
        kernel, "input_matmul", jax.ShapeDtypeStruct((slots, width), BF), [SM, SM] + [VM] * (len(pieces) + 3),
        (at, img_count, *pieces, route, w_gate, w_up), 8,
        [pltpu.VMEM((g.cols, 2 * own * rows, share), BF)],
        busy=(8 * slots * units * width, 4 * units * width),
    )


def fetch_rows(g, at, w_proj, steps):
    block = SHUF * LANES
    last = cdiv(w_proj.shape[0], block) - 1

    def kernel(pos, w_ref, out_ref, sem):
        copies = []
        for i in range(steps):
            first = jnp.minimum(pos[3] * steps + i, last) * block
            copies.append(pltpu.make_async_copy(w_ref.at[pl.ds(first, block)], out_ref.at[i], sem.at[i]))
            copies[-1].start()
        for copy in copies:
            copy.wait()

    shape = jax.ShapeDtypeStruct((steps, block, w_proj.shape[1]), BF)
    return local_call(
        kernel, "fetch_rows", shape, [SM, HBM], (at, w_proj), 22, [pltpu.SemaphoreType.DMA((steps,))],
        busy=(0, 2 * steps * block * w_proj.shape[1]),
    )


def shuffle_matmul(g, image_grad, w_rows):
    slots, width = image_grad.shape
    half = slots // CORES
    steps, block, width = w_rows.shape
    sub = g.chips // SHUF
    piece = half // sub

    def kernel(grad_ref, w_ref, keep_ref, give_ref, parts):
        source = lax.broadcasted_iota(jnp.int32, (block, block), 0)
        target = lax.broadcasted_iota(jnp.int32, (block, block), 1)
        order = jnp.where(source == SHUF * (target % LANES) + target // LANES, 1.0, 0.0).astype(BF)
        for i in range(steps):
            parts[i * slots : (i + 1) * slots] = dot_nt(grad_ref[...], w_ref[i]).astype(BF)
        done = dot_nn(parts[...], order).astype(BF)
        for i in range(steps):
            for ref, top in ((keep_ref, i * slots), (give_ref, i * slots + half)):
                for q in range(SHUF):
                    for s in range(sub):
                        rows = done[top + s * piece : top + (s + 1) * piece, q * LANES : (q + 1) * LANES]
                        ref[q * sub + s, :, i * LANES : (i + 1) * LANES] = rows

    shape = jax.ShapeDtypeStruct((g.chips, piece, steps * LANES), BF)
    return local_call(
        kernel, "shuffle_matmul", [shape, shape], [VM, VM], (image_grad, w_rows), 8,
        [pltpu.VMEM((steps * slots, block), BF)],
        busy=(2 * slots * width * block * steps, 2 * width * block * steps),
    )


def chip_sum(g, at, keep, other):
    def kernel(pos, keep_ref, other_ref, own_ref, *piece_refs):
        for (dx, dy), ref in zip(g.shifts, (own_ref,) + piece_refs):
            chip = (pos[1] + dx) % g.xs * g.cols + (pos[2] + dy) % g.cols
            ref[...] = (keep_ref[chip].astype(F32) + other_ref[chip].astype(F32)).astype(ref.dtype)

    shapes = [jax.ShapeDtypeStruct(keep.shape[1:], F32 if s == (0, 0) else BF) for s in g.shifts]
    return local_call(kernel, "chip_sum", shapes, [SM, VM, VM], (at, keep, other), 4)


def order_hidden(g, at, parts, piece):
    group, units = parts[0].shape[1:]
    patches = group * g.rows
    half = patches // (CORES * SHUF)
    masks = row_masks(g)

    def kernel(pos, *refs):
        spot = lax.broadcasted_iota(jnp.int32, (patches, group), 0)
        inner = lax.rem(spot, piece)
        shift = lax.rem(lax.div(spot, piece), g.chips)
        core = lax.rem(lax.div(spot, g.chips * piece) + pos[0], CORES)
        x = lax.rem(pos[1] - lax.div(shift, g.cols) + g.xs, g.xs)
        y = lax.rem(pos[2] - lax.rem(shift, g.cols) + g.cols, g.cols)
        inner = (x * g.cols + y) * piece + inner
        patch = (core * half + lax.rem(inner, half)) * SHUF + lax.div(inner, half)
        source = lax.broadcasted_iota(jnp.int32, (patches, group), 1)
        total, i = 0.0, 0
        for ref in refs[:-1]:
            for part in range(ref.shape[0]):
                row = i if masks is None else masks[i] ^ pos[3]
                pick = jnp.where(patch == source + row * group, 1.0, 0.0).astype(BF)
                total = total + lax.dot_general(
                    ref[part], pick, (((0,), (1,)), ((), ())), preferred_element_type=F32
                )
                i += 1
        refs[-1][...] = total.astype(BF)

    shape = jax.ShapeDtypeStruct((units, patches), BF)
    return local_call(
        kernel, "order_hidden", shape, [SM] + [VM] * len(parts), (at, *parts), 8, busy=(2 * units * patches * patches, 0)
    )


def weight_grad(g, at, result, features, first, pieces, hidden):
    units, patches = hidden.shape
    count, piece, wide = pieces[0].shape
    scale = 1.0 / math.sqrt(patches)
    masks = row_masks(g)
    full, tail = divmod(features, wide)
    fresh = result is None

    def kernel(pos, *refs):
        refs = refs if fresh else refs[1:]
        piece_refs, (hidden_ref, out_ref, patch, buf, sem) = refs[:-5], refs[-5:]
        sends = []
        for i in range(count):
            row = first + i if masks is None else masks[first + i] ^ pos[3]
            for n, ref in enumerate(piece_refs):
                patch[i, n * piece : (n + 1) * piece] = ref[i]
            buf[i] = (dot_nn(hidden_ref[...], patch[i]) * scale).astype(BF)
            begun = []
            if masks is not None or row < full:
                ends = out_ref.at[:, pl.ds(row * wide, wide)]
                begun.append((row < full, pltpu.make_async_copy(buf.at[i], ends, sem.at[i])))
            if tail:
                ends = out_ref.at[:, pl.ds(full * wide, tail)]
                begun.append((row == full, pltpu.make_async_copy(buf.at[i, :, pl.ds(0, tail)], ends, sem.at[i])))
            for now, copy in begun:
                pl.when(now)(copy.start)
            sends += begun
        for now, copy in sends:
            pl.when(now)(copy.wait)

    return pl.pallas_call(
        kernel,
        out_shape=jax.ShapeDtypeStruct((units, features), BF),
        in_specs=[SM] + ([] if fresh else [HBM]) + [VM] * (len(pieces) + 1),
        out_specs=HBM,
        scratch_shapes=[
            pltpu.VMEM((count, patches, wide), BF),
            pltpu.VMEM((count, units, wide), BF),
            pltpu.SemaphoreType.DMA((count,)),
        ],
        input_output_aliases={} if fresh else {1: 0},
        compiler_params=pltpu.CompilerParams(vmem_limit_bytes=16 * MIB),
        cost_estimate=pl.CostEstimate(
            flops=2 * count * patches * wide * units, bytes_accessed=2 * count * units * wide, transcendentals=0
        ),
        name="weight_grad",
    )(at, *([] if fresh else [result]), *pieces, hidden)


def row_masks(g):
    if g.rows & (g.rows - 1):
        return None
    masks = [0]
    while len(masks) < g.rows:
        masks = masks + [m ^ (2 * len(masks) - 1) for m in masks]
    return masks


def sum_rows(g, value, beside):
    if g.rows & (g.rows - 1):
        return lax.psum(value.astype(F32), "row").astype(BF), beside
    beside, step, n = list(beside), 1, 0
    while step < g.rows:
        mask = 2 * step - 1
        other = g.send(value, row=lambda r: r ^ mask)
        if n < len(beside):
            other, beside[n] = lax.optimization_barrier((other, beside[n]))
        value = (value.astype(F32) + other.astype(F32)).astype(BF)
        step, n = 2 * step, n + 1
    return value, beside


def ordered(first, *later):
    return lax.optimization_barrier((first, *later))[1:]


def shards(out_grad, gate_pre, up_pre, w_gate, w_up, w_down, w_proj, enc_hidden, route, img_count):
    g = Grid()
    at = g.place()
    slots = route.shape[0]
    own = gate_pre.shape[0]
    half = slots // CORES
    units = w_down.shape[0]
    tall = cdiv(own, 16) * 16
    share = cdiv(cdiv(units, g.cols), LANES) * LANES
    doubling = not g.rows & (g.rows - 1)

    def to_chips(pieces):
        return [g.send(p, dx=dx, dy=dy) for p, (dx, dy) in zip(pieces, g.shifts[1:])]

    saved = enc_hidden[None]
    keep, give = down_matmul(g, at, out_grad, w_down, own, tall, share)
    total, *pieces = core_sum(g, at, keep, g.swap(give), tall)
    saved_parts = [saved]
    if doubling and g.rows > 1:
        (mine,) = ordered(total, saved)
        saved_parts.append(g.send(mine, row=lambda r: r ^ 1))
        total, *pieces = lax.optimization_barrier((total, *pieces))
    arrived = to_chips(pieces)
    if doubling and g.rows > 1:
        saved_parts[1], *arrived = lax.optimization_barrier((saved_parts[1], *arrived))
    grads = gate_grads(g, at, total, arrived, gate_pre, up_pre)
    step = 2
    while doubling and step < g.rows:
        (mine,) = ordered(grads, jnp.concatenate(saved_parts))
        mask = 2 * step - 1
        saved_parts.append(g.send(mine, row=lambda r: r ^ mask))
        step *= 2
    pieces = [grads] + to_chips([grads] * (g.chips - 1))
    pieces = pieces + [g.swap(p) for p in pieces]
    if not doubling:
        saved_parts = [lax.all_gather(enc_hidden, "row", axis=0, tiled=False)]
    image_grad = input_matmul(g, at, pieces, route.reshape(1, slots), img_count, w_gate.T, w_up.T, own)

    features = w_proj.shape[0] // SHUF
    steps = cdiv(cdiv(features, g.rows), LANES)
    piece = SHUF * half // g.chips
    image_grad, late = lax.optimization_barrier((image_grad, at))
    w_rows = fetch_rows(g, late, w_proj, steps)
    hidden = order_hidden(g, late, saved_parts, piece)
    image_grad, (hidden, w_rows) = sum_rows(g, image_grad, (hidden, w_rows))

    keep, give = shuffle_matmul(g, image_grad, w_rows)
    total, *pieces = chip_sum(g, at, keep, g.swap(give))
    for part in to_chips(pieces):
        total = total + part.astype(F32)
    patch_grad = total.astype(BF)

    if not doubling:
        batches = [lax.all_gather(patch_grad, "row", axis=0, tiled=False)]
    else:
        stack, batches, step = patch_grad[None], [], 1
        while step < g.rows:
            mask = 2 * step - 1
            other = g.send(stack, row=lambda r: r ^ mask)
            stack = jnp.concatenate([stack, other])
            batches.append(stack if step == 1 else other)
            step *= 2
        batches = batches or [stack]
    result, first = None, 0
    for batch in batches:
        pieces = [batch] + to_chips([batch] * (g.chips - 1))
        pieces = pieces + [g.swap(p) for p in pieces]
        result = weight_grad(g, at, result, features, first, pieces, hidden)
        first += batch.shape[0]
    return result.T


def solution(mesh):
    placed = (
        P(None, ("enc", "col")),
        P("enc", "row"),
        P("enc", "row"),
        P(("enc", "col"), "row"),
        P(("enc", "col"), "row"),
        P("row", ("enc", "col")),
        P(None, ("enc", "col")),
        P("row", ("enc", "col")),
        P(),
        P(),
    )
    return jax.shard_map(
        shards, mesh=mesh, in_specs=placed, out_specs=P(None, ("enc", "col")), check_vma=False
    )
```

time: 433 us -> 90.7 us (0.21)
  waiting for transfers between devices: 251 us -> 29.3 us
  blocking collectives: 100 us -> 0 us
  matrix products: 44.8 us -> 0 us
  Pallas kernels: 0 us -> 29 us
  starting transfers between devices: 5.85 us -> 30.6 us
  between operations: 15.7 us -> 0.5 us
  local copies, waits for them, and re-layouts: 15 us -> 0.96 us
    psum x1 -> x0, waiting for transfers between devices: 185 us -> none  [shards(): total = lax.psum(group_term.astype(jnp.bfloat16), 'row')]
    unnamed x6 -> x0, waiting for transfers between devices: 65.5 us -> none
    all_gather x5 -> x0, blocking collectives: 52.8 us -> none  [the longest x1 17.1 us: shards(): lax.all_gather(patch_grad, ('enc', 'col'), axis=1, tiled=True)]
    unnamed x3 -> x0, blocking collectives: 47.2 us -> none
    ppermute x0 -> x35, starting transfers between devices: none -> 30.6 us  [send(): return lax.ppermute(value, AXES, pairs)]
    dot_general x4 -> x0, matrix products: 30 us -> none  [the longest x3 26.1 us: contract_last(): lax.dot_general(left, right, (((1,), (1,)), ((), ())), preferred_element_...]
    ppermute x0 -> x35, waiting for transfers between devices: none -> 29.3 us  [send(): return lax.ppermute(value, AXES, pairs)]
    pallas_call x0 -> x10, Pallas kernels: none -> 29 us  [the longest x8 23.6 us: local_call(): pl.pallas_call(kernel, out_shape=out_shape, in_specs=in_specs, out_specs=...]
  transfers between devices with their start and end apart: 5 -> 35, of which waited for: 4 -> 17; matrix products, arithmetic and copies ran while one was open for 0% -> 0% of each run, Pallas kernels for 0% -> 15%
where the time goes in v2:
time: 90.7 us; the launch traced here: 90.6 us
  starting transfers between devices  30.6 us (34%)
  waiting for transfers between devices  29.3 us (32%)
  Pallas kernels  29 us (32%)
  local copies, waits for them, and re-layouts  0.96 us (1%)
    ppermute x35, starting transfers between devices, send(): return lax.ppermute(value, AXES, pairs)  30.6 us
    ppermute x35, waiting for transfers between devices, send(): return lax.ppermute(value, AXES, pairs)  29.3 us
    pallas_call x8, Pallas kernels, local_call(): pl.pallas_call(kernel, out_shape=out_shape, in_specs=in_specs, out_specs=...  23.6 us
    pallas_call x2, Pallas kernels, weight_grad(): pl.pallas_call(kernel, out_shape=jax.ShapeDtypeStruct((units, features),...  5.41 us
  transfers between devices with their start and end apart: 35, of which 17 were waited for; matrix products, arithmetic and copies ran while one was open for 0% of the time, Pallas kernels for 15%

profile of v2, /device:TPU:0, one launch (start us, length us, event | category | flops | bytes accessed | tf_op | source)
XLA Modules:
  0.0 90.6 jit_solution(12570840935557295227)
XLA Ops:
  1.0 8.0 %down_matmul.1 = (bf16[2,32,3712]{2,1,0:T(8,128)(2,1)S(1)}, bf16[2,32,3712]{2,1,0:T(8,128)(2,1)S(1)}) custom-call(s32[4]{0:T(128)S(1)} %pad_add_fusion.pos, bf16[48,1024]{1,0:T(8,128)(2,1)S(1)} %copy-done.1, bf16[7392,1024]{1,0:T(8,128)(2,1)} %w_ref.2), custom_call_target="tpu_custom_call" | custom-call | flops 726663168 | bytes 15138816 | tf_op jit(solution)/shard_map/down_matmul/pallas_call | solution.py:73
  9.6 1.5 %collective-permute-done.other_ref = bf16[2,32,3712]{2,1,0:T(8,128)(2,1)S(1)} collective-permute-done((bf16[2,32,3712]{2,1,0:T(8,128)(2,1)S(1)}, bf16[2,32,3712]{2,1,0:T(8,128)(2,1)S(1)}, u32[]{:S(2)}, u32[]{:S(2)}) %collective-permute-start) | collective-permute-done | bytes 475168 | tf_op jit(solution)/shard_map/ppermute | solution.py:56
  11.7 2.9 %collective-permute-start.2 = (bf16[16,3712]{1,0:T(8,128)(2,1)S(1)}, bf16[16,3712]{1,0:T(8,128)(2,1)S(1)}, u32[]{:S(2)}, u32[]{:S(2)}) collective-permute-start(bf16[16,3712]{1,0:T(8,128)(2,1)S(1)} %get-tuple-element.31), channel_id=1, source_target_pairs={{0,1},{1,0},{2,3},{3,2},{4,5},{5,4},{6,7},{7,6},{8,9},{9,8},{10,11... | collective-permute-start | bytes 356360 | tf_op jit(solution)/shard_map/ppermute | solution.py:56
  14.7 1.5 %collective-permute-start.3 = (bf16[16,3712]{1,0:T(8,128)(2,1)S(1)}, bf16[16,3712]{1,0:T(8,128)(2,1)S(1)}, u32[]{:S(2)}, u32[]{:S(2)}) collective-permute-start(bf16[16,3712]{1,0:T(8,128)(2,1)S(1)} %get-tuple-element.32), channel_id=1, source_target_pairs={{0,16},{1,17},{2,18},{3,19},{4,20},{5,21},{6,22},{7,23},{8,24},{9,... | collective-permute-start | bytes 356360 | tf_op jit(solution)/shard_map/ppermute | solution.py:56
  16.2 2.0 %collective-permute-start.1 = (bf16[1,48,800]{2,1,0:T(8,128)(2,1)S(1)}, bf16[1,48,800]{2,1,0:T(8,128)(2,1)S(1)}, u32[]{:S(2)}, u32[]{:S(2)}) collective-permute-start(bf16[1,48,800]{2,1,0:T(8,128)(2,1)S(1)} %bitcast.17), channel_id=1, source_target_pairs={{0,2},{1,3},{2,0},{3,1},{4,6},{5,7},{6,4},{7,5},{8,10},{9,11},{10,... | collective-permute-start | bytes 230408 | tf_op jit(solution)/shard_map/ppermute | solution.py:56
  18.2 2.5 %collective-permute-done.1.refs_1_ = bf16[1,48,800]{2,1,0:T(8,128)(2,1)S(1)} collective-permute-done((bf16[1,48,800]{2,1,0:T(8,128)(2,1)S(1)}, bf16[1,48,800]{2,1,0:T(8,128)(2,1)S(1)}, u32[]{:S(2)}, u32[]{:S(2)}) %collective-permute-start.1) | collective-permute-done | bytes 76832 | tf_op jit(solution)/shard_map/ppermute | solution.py:56
  22.8 2.7 %collective-permute-start.7 = (bf16[24,3712]{1,0:T(8,128)(2,1)S(1)}, bf16[24,3712]{1,0:T(8,128)(2,1)S(1)}, u32[]{:S(2)}, u32[]{:S(2)}) collective-permute-start(bf16[24,3712]{1,0:T(8,128)(2,1)S(1)} %gate_grads.1.refs_0_), channel_id=1, source_target_pairs={{0,17},{1,16},{2,19},{3,18},{4,21},{5,20},{6,23},{7,22},{8,25},{9,... | collective-permute-start | bytes 534536 | tf_op jit(solution)/shard_map/ppermute | solution.py:56
  26.4 4.7 %collective-permute-done.7.refs_3_ = bf16[24,3712]{1,0:T(8,128)(2,1)S(1)} collective-permute-done((bf16[24,3712]{1,0:T(8,128)(2,1)S(1)}, bf16[24,3712]{1,0:T(8,128)(2,1)S(1)}, u32[]{:S(2)}, u32[]{:S(2)}) %collective-permute-start.7) | collective-permute-done | bytes 178208 | tf_op jit(solution)/shard_map/ppermute | solution.py:56
  31.1 2.2 %collective-permute-done.6.refs_2_ = bf16[24,3712]{1,0:T(8,128)(2,1)S(1)} collective-permute-done((bf16[24,3712]{1,0:T(8,128)(2,1)S(1)}, bf16[24,3712]{1,0:T(8,128)(2,1)S(1)}, u32[]{:S(2)}, u32[]{:S(2)}) %collective-permute-start.6) | collective-permute-done | bytes 178208 | tf_op jit(solution)/shard_map/ppermute | solution.py:56
  33.8 3.7 %collective-permute-start.13 = (bf16[2,48,800]{2,1,0:T(8,128)(2,1)S(1)}, bf16[2,48,800]{2,1,0:T(8,128)(2,1)S(1)}, u32[]{:S(2)}, u32[]{:S(2)}) collective-permute-start(bf16[2,48,800]{2,1,0:T(8,128)(2,1)S(1)} %pad_maximum_fusion), channel_id=1, source_target_pairs={{0,6},{1,7},{2,4},{3,5},{4,2},{5,3},{6,0},{7,1},{8,14},{9,15},{10,... | collective-permute-start | bytes 460808 | tf_op jit(solution)/shard_map/ppermute | solution.py:56
  37.6 6.0 %input_matmul.1 = bf16[48,1024]{1,0:T(8,128)(2,1)S(1)} custom-call(s32[4]{0:T(128)S(1)} %pad_add_fusion.pos, s32[4]{0:T(128)S(1)} %copy-done.2, bf16[24,3712]{1,0:T(8,128)(2,1)S(1)} %gate_grads.1.refs_0_, bf16[24,3712]{1,0:T(8,128)(2,1)S(1)} %collective-permute-done.5.refs_1_, bf16[24,3712]{1,0:T(8,128)(2,1)S(1)} %collective-permute-done.6.refs_2_, ...), custom_call_target="tpu_custom_call" | custom-call | flops 2906652672 | bytes 30277632 | tf_op jit(solution)/shard_map/input_matmul/pallas_call | solution.py:73
  45.0 3.2 %collective-permute-done.12 = bf16[48,1024]{1,0:T(8,128)(2,1)S(1)} collective-permute-done((bf16[48,1024]{1,0:T(8,128)(2,1)S(1)}, bf16[48,1024]{1,0:T(8,128)(2,1)S(1)}, u32[]{:S(2)}, u32[]{:S(2)}) %collective-permute-start.12) | collective-permute-done | bytes 98336 | tf_op jit(solution)/shard_map/ppermute | solution.py:56
  49.7 3.7 %fetch_rows.1.w_ref = bf16[7,512,1024]{2,1,0:T(8,128)(2,1)S(1)} custom-call(s32[4]{0:T(128)S(1)} %pad_add_fusion.pos, bf16[12800,1024]{1,0:T(8,128)(2,1)} %w_ref.3), custom_call_target="tpu_custom_call" | custom-call | bytes 7340032 | tf_op jit(solution)/shard_map/fetch_rows/pallas_call | solution.py:73
  54.8 2.5 %shuffle_matmul.1 = (bf16[4,24,896]{2,1,0:T(8,128)(2,1)S(1)}, bf16[4,24,896]{2,1,0:T(8,128)(2,1)S(1)}) custom-call(bf16[48,1024]{1,0:T(8,128)(2,1)S(1)} %add_convert_fusion.grad_ref, bf16[7,512,1024]{2,1,0:T(8,128)(2,1)S(1)} %fetch_rows.1.w_ref), custom_call_target="tpu_custom_call" | custom-call | flops 352321536 | bytes 7340032 | tf_op jit(solution)/shard_map/shuffle_matmul/pallas_call | solution.py:73
  60.7 1.5 %collective-permute-start.17 = (bf16[24,896]{1,0:T(8,128)(2,1)S(1)}, bf16[24,896]{1,0:T(8,128)(2,1)S(1)}, u32[]{:S(2)}, u32[]{:S(2)}) collective-permute-start(bf16[24,896]{1,0:T(8,128)(2,1)S(1)} %get-tuple-element.48), channel_id=1, source_target_pairs={{0,16},{1,17},{2,18},{3,19},{4,20},{5,21},{6,22},{7,23},{8,24},{9,... | collective-permute-start | bytes 129032 | tf_op jit(solution)/shard_map/ppermute | solution.py:56
  63.5 1.4 %collective-permute-done.17 = bf16[24,896]{1,0:T(8,128)(2,1)S(1)} collective-permute-done((bf16[24,896]{1,0:T(8,128)(2,1)S(1)}, bf16[24,896]{1,0:T(8,128)(2,1)S(1)}, u32[]{:S(2)}, u32[]{:S(2)}) %collective-permute-start.17) | collective-permute-done | bytes 43040 | tf_op jit(solution)/shard_map/ppermute | solution.py:56
  64.9 2.2 %collective-permute-done.18 = bf16[24,896]{1,0:T(8,128)(2,1)S(1)} collective-permute-done((bf16[24,896]{1,0:T(8,128)(2,1)S(1)}, bf16[24,896]{1,0:T(8,128)(2,1)S(1)}, u32[]{:S(2)}, u32[]{:S(2)}) %collective-permute-start.18) | collective-permute-done | bytes 43040 | tf_op jit(solution)/shard_map/ppermute | solution.py:56
  67.8 3.4 %collective-permute-done.19 = bf16[1,24,896]{2,1,0:T(8,128)(2,1)S(1)} collective-permute-done((bf16[1,24,896]{2,1,0:T(8,128)(2,1)S(1)}, bf16[1,24,896]{2,1,0:T(8,128)(2,1)S(1)}, u32[]{:S(2)}, u32[]{:S(2)}) %collective-permute-start.19) | collective-permute-done | bytes 43040 | tf_op jit(solution)/shard_map/ppermute | solution.py:56
  71.3 1.7 %collective-permute-start.27 = (bf16[2,24,896]{2,1,0:T(8,128)(2,1)S(1)}, bf16[2,24,896]{2,1,0:T(8,128)(2,1)S(1)}, u32[]{:S(2)}, u32[]{:S(2)}) collective-permute-start(bf16[2,24,896]{2,1,0:T(8,128)(2,1)S(1)} %pad_maximum_fusion.1.refs_0_), channel_id=1, source_target_pairs={{0,6},{1,7},{2,4},{3,5},{4,2},{5,3},{6,0},{7,1},{8,14},{9,15},{10,... | collective-permute-start | bytes 258056 | tf_op jit(solution)/shard_map/ppermute | solution.py:56
  73.7 1.5 %collective-permute-start.21 = (bf16[2,24,896]{2,1,0:T(8,128)(2,1)S(1)}, bf16[2,24,896]{2,1,0:T(8,128)(2,1)S(1)}, u32[]{:S(2)}, u32[]{:S(2)}) collective-permute-start(bf16[2,24,896]{2,1,0:T(8,128)(2,1)S(1)} %pad_maximum_fusion.1.refs_0_), channel_id=1, source_target_pairs={{0,16},{1,17},{2,18},{3,19},{4,20},{5,21},{6,22},{7,23},{8,24},{9,... | collective-permute-start | bytes 258056 | tf_op jit(solution)/shard_map/ppermute | solution.py:56
  78.4 1.5 %collective-permute-start.29 = (bf16[2,24,896]{2,1,0:T(8,128)(2,1)S(1)}, bf16[2,24,896]{2,1,0:T(8,128)(2,1)S(1)}, u32[]{:S(2)}, u32[]{:S(2)}) collective-permute-start(bf16[2,24,896]{2,1,0:T(8,128)(2,1)S(1)} %collective-permute-done.27.refs_1_), channel_id=1, source_target_pairs={{0,16},{1,17},{2,18},{3,19},{4,20},{5,21},{6,22},{7,23},{8,24},{9,... | collective-permute-start | bytes 258056 | tf_op jit(solution)/shard_map/ppermute | solution.py:56
  81.6 1.7 %collective-permute-done.30.refs_4_ = bf16[2,24,896]{2,1,0:T(8,128)(2,1)S(1)} collective-permute-done((bf16[2,24,896]{2,1,0:T(8,128)(2,1)S(1)}, bf16[2,24,896]{2,1,0:T(8,128)(2,1)S(1)}, u32[]{:S(2)}, u32[]{:S(2)}) %collective-permute-start.30) | collective-permute-done | bytes 86048 | tf_op jit(solution)/shard_map/ppermute | solution.py:56
  84.9 2.7 %weight_grad.2.refs_0_ = bf16[800,3200]{1,0:T(8,128)(2,1)} custom-call(s32[4]{0:T(128)S(1)} %pad_add_fusion.pos, bf16[2,24,896]{2,1,0:T(8,128)(2,1)S(1)} %pad_maximum_fusion.1.refs_0_, bf16[2,24,896]{2,1,0:T(8,128)(2,1)S(1)} %collective-permute-done.20.refs_1_, bf16[2,24,896]{2,1,0:T(8,128)(2,1)S(1)} %collective-permute-done.21.refs_2_, ...), custom_call_target="tpu_custom_call" | custom-call | flops 550502400 | bytes 2867200 | tf_op jit(solution)/shard_map/weight_grad/pallas_call | solution.py:349
  87.7 2.7 %weight_grad.3 = bf16[800,3200]{1,0:T(8,128)(2,1)} custom-call(s32[4]{0:T(128)S(1)} %pad_add_fusion.pos, bf16[800,3200]{1,0:T(8,128)(2,1)} %weight_grad.2.refs_0_, bf16[2,24,896]{2,1,0:T(8,128)(2,1)S(1)} %collective-permute-done.27.refs_1_, bf16[2,24,896]{2,1,0:T(8,128)(2,1)S(1)} %collective-permute-done.28.refs_2_, ...), custom_call_target="tpu_custom_call", output_to_operand_aliasing={{}: (1, {})} | custom-call | flops 550502400 | bytes 2867200 | tf_op jit(solution)/shard_map/weight_grad/pallas_call | solution.py:349
  (92 shorter events, 22.6 us)
Async XLA Ops:
  11.7 9.0 %collective-permute-start.2 = (bf16[16,3712]{1,0:T(8,128)(2,1)S(1)}, bf16[16,3712]{1,0:T(8,128)(2,1)S(1)}, u32[]{:S(2)}, u32[]{:S(2)}) collective-permute-start(bf16[16,3712]{1,0:T(8,128)(2,1)S(1)} %get-tuple-element.31), channel_id=1, source_target_pairs={{0,1},{1,0},{2,3},{3,2},{4,5},{5,4},{6,7},{7,6},{8,9},{9,8},{10,11... | collective-permute-start | bytes 356360 | tf_op jit(solution)/shard_map/ppermute | solution.py:56
  14.7 6.1 %collective-permute-start.3 = (bf16[16,3712]{1,0:T(8,128)(2,1)S(1)}, bf16[16,3712]{1,0:T(8,128)(2,1)S(1)}, u32[]{:S(2)}, u32[]{:S(2)}) collective-permute-start(bf16[16,3712]{1,0:T(8,128)(2,1)S(1)} %get-tuple-element.32), channel_id=1, source_target_pairs={{0,16},{1,17},{2,18},{3,19},{4,20},{5,21},{6,22},{7,23},{8,24},{9,... | collective-permute-start | bytes 356360 | tf_op jit(solution)/shard_map/ppermute | solution.py:56
  16.2 5.8 %collective-permute-start.4 = (bf16[16,3712]{1,0:T(8,128)(2,1)S(1)}, bf16[16,3712]{1,0:T(8,128)(2,1)S(1)}, u32[]{:S(2)}, u32[]{:S(2)}) collective-permute-start(bf16[16,3712]{1,0:T(8,128)(2,1)S(1)} %get-tuple-element.33), channel_id=1, source_target_pairs={{0,17},{1,16},{2,19},{3,18},{4,21},{5,20},{6,23},{7,22},{8,25},{9,... | collective-permute-start | bytes 356360 | tf_op jit(solution)/shard_map/ppermute | solution.py:56
  16.2 4.5 %collective-permute-start.1 = (bf16[1,48,800]{2,1,0:T(8,128)(2,1)S(1)}, bf16[1,48,800]{2,1,0:T(8,128)(2,1)S(1)}, u32[]{:S(2)}, u32[]{:S(2)}) collective-permute-start(bf16[1,48,800]{2,1,0:T(8,128)(2,1)S(1)} %bitcast.17), channel_id=1, source_target_pairs={{0,2},{1,3},{2,0},{3,1},{4,6},{5,7},{6,4},{7,5},{8,10},{9,11},{10,... | collective-permute-start | bytes 230408 | tf_op jit(solution)/shard_map/ppermute | solution.py:56
  22.8 8.2 %collective-permute-start.7 = (bf16[24,3712]{1,0:T(8,128)(2,1)S(1)}, bf16[24,3712]{1,0:T(8,128)(2,1)S(1)}, u32[]{:S(2)}, u32[]{:S(2)}) collective-permute-start(bf16[24,3712]{1,0:T(8,128)(2,1)S(1)} %gate_grads.1.refs_0_), channel_id=1, source_target_pairs={{0,17},{1,16},{2,19},{3,18},{4,21},{5,20},{6,23},{7,22},{8,25},{9,... | collective-permute-start | bytes 534536 | tf_op jit(solution)/shard_map/ppermute | solution.py:56
  25.5 7.7 %collective-permute-start.6 = (bf16[24,3712]{1,0:T(8,128)(2,1)S(1)}, bf16[24,3712]{1,0:T(8,128)(2,1)S(1)}, u32[]{:S(2)}, u32[]{:S(2)}) collective-permute-start(bf16[24,3712]{1,0:T(8,128)(2,1)S(1)} %gate_grads.1.refs_0_), channel_id=1, source_target_pairs={{0,16},{1,17},{2,18},{3,19},{4,20},{5,21},{6,22},{7,23},{8,24},{9,... | collective-permute-start | bytes 534536 | tf_op jit(solution)/shard_map/ppermute | solution.py:56
  26.0 7.2 %collective-permute-start.5 = (bf16[24,3712]{1,0:T(8,128)(2,1)S(1)}, bf16[24,3712]{1,0:T(8,128)(2,1)S(1)}, u32[]{:S(2)}, u32[]{:S(2)}) collective-permute-start(bf16[24,3712]{1,0:T(8,128)(2,1)S(1)} %gate_grads.1.refs_0_), channel_id=1, source_target_pairs={{0,1},{1,0},{2,3},{3,2},{4,5},{5,4},{6,7},{7,6},{8,9},{9,8},{10,11... | collective-permute-start | bytes 534536 | tf_op jit(solution)/shard_map/ppermute | solution.py:56
  26.4 11.1 %collective-permute-start.8 = (bf16[24,3712]{1,0:T(8,128)(2,1)S(1)}, bf16[24,3712]{1,0:T(8,128)(2,1)S(1)}, u32[]{:S(2)}, u32[]{:S(2)}) collective-permute-start(bf16[24,3712]{1,0:T(8,128)(2,1)S(1)} %gate_grads.1.refs_0_), channel_id=1, source_target_pairs={{0,8},{1,9},{2,10},{3,11},{4,12},{5,13},{6,14},{7,15},{8,0},{9,1},... | collective-permute-start | bytes 534536 | tf_op jit(solution)/shard_map/ppermute | solution.py:56
  31.1 6.4 %collective-permute-start.11 = (bf16[24,3712]{1,0:T(8,128)(2,1)S(1)}, bf16[24,3712]{1,0:T(8,128)(2,1)S(1)}, u32[]{:S(2)}, u32[]{:S(2)}) collective-permute-start(bf16[24,3712]{1,0:T(8,128)(2,1)S(1)} %collective-permute-done.7.refs_3_), channel_id=1, source_target_pairs={{0,8},{1,9},{2,10},{3,11},{4,12},{5,13},{6,14},{7,15},{8,0},{9,1},... | collective-permute-start | bytes 534536 | tf_op jit(solution)/shard_map/ppermute | solution.py:56
  33.2 4.2 %collective-permute-start.10 = (bf16[24,3712]{1,0:T(8,128)(2,1)S(1)}, bf16[24,3712]{1,0:T(8,128)(2,1)S(1)}, u32[]{:S(2)}, u32[]{:S(2)}) collective-permute-start(bf16[24,3712]{1,0:T(8,128)(2,1)S(1)} %collective-permute-done.6.refs_2_), channel_id=1, source_target_pairs={{0,8},{1,9},{2,10},{3,11},{4,12},{5,13},{6,14},{7,15},{8,0},{9,1},... | collective-permute-start | bytes 534536 | tf_op jit(solution)/shard_map/ppermute | solution.py:56
  33.2 4.2 %collective-permute-start.9 = (bf16[24,3712]{1,0:T(8,128)(2,1)S(1)}, bf16[24,3712]{1,0:T(8,128)(2,1)S(1)}, u32[]{:S(2)}, u32[]{:S(2)}) collective-permute-start(bf16[24,3712]{1,0:T(8,128)(2,1)S(1)} %collective-permute-done.5.refs_1_), channel_id=1, source_target_pairs={{0,8},{1,9},{2,10},{3,11},{4,12},{5,13},{6,14},{7,15},{8,0},{9,1},... | collective-permute-start | bytes 534536 | tf_op jit(solution)/shard_map/ppermute | solution.py:56
  33.8 9.9 %collective-permute-start.13 = (bf16[2,48,800]{2,1,0:T(8,128)(2,1)S(1)}, bf16[2,48,800]{2,1,0:T(8,128)(2,1)S(1)}, u32[]{:S(2)}, u32[]{:S(2)}) collective-permute-start(bf16[2,48,800]{2,1,0:T(8,128)(2,1)S(1)} %pad_maximum_fusion), channel_id=1, source_target_pairs={{0,6},{1,7},{2,4},{3,5},{4,2},{5,3},{6,0},{7,1},{8,14},{9,15},{10,... | collective-permute-start | bytes 460808 | tf_op jit(solution)/shard_map/ppermute | solution.py:56
  43.5 4.7 %collective-permute-start.12 = (bf16[48,1024]{1,0:T(8,128)(2,1)S(1)}, bf16[48,1024]{1,0:T(8,128)(2,1)S(1)}, u32[]{:S(2)}, u32[]{:S(2)}) collective-permute-start(bf16[48,1024]{1,0:T(8,128)(2,1)S(1)} %input_matmul.1), channel_id=1, source_target_pairs={{0,2},{1,3},{2,0},{3,1},{4,6},{5,7},{6,4},{7,5},{8,10},{9,11},{10,... | collective-permute-start | bytes 294920 | tf_op jit(solution)/shard_map/ppermute | solution.py:56
  48.3 6.5 %collective-permute-start.14 = (bf16[48,1024]{1,0:T(8,128)(2,1)S(1)}, bf16[48,1024]{1,0:T(8,128)(2,1)S(1)}, u32[]{:S(2)}, u32[]{:S(2)}) collective-permute-start(bf16[48,1024]{1,0:T(8,128)(2,1)S(1)} %add_convert_fusion.1), channel_id=1, source_target_pairs={{0,6},{1,7},{2,4},{3,5},{4,2},{5,3},{6,0},{7,1},{8,14},{9,15},{10,... | collective-permute-start | bytes 294920 | tf_op jit(solution)/shard_map/ppermute | solution.py:56
  60.7 4.2 %collective-permute-start.17 = (bf16[24,896]{1,0:T(8,128)(2,1)S(1)}, bf16[24,896]{1,0:T(8,128)(2,1)S(1)}, u32[]{:S(2)}, u32[]{:S(2)}) collective-permute-start(bf16[24,896]{1,0:T(8,128)(2,1)S(1)} %get-tuple-element.48), channel_id=1, source_target_pairs={{0,16},{1,17},{2,18},{3,19},{4,20},{5,21},{6,22},{7,23},{8,24},{9,... | collective-permute-start | bytes 129032 | tf_op jit(solution)/shard_map/ppermute | solution.py:56
  62.2 4.9 %collective-permute-start.18 = (bf16[24,896]{1,0:T(8,128)(2,1)S(1)}, bf16[24,896]{1,0:T(8,128)(2,1)S(1)}, u32[]{:S(2)}, u32[]{:S(2)}) collective-permute-start(bf16[24,896]{1,0:T(8,128)(2,1)S(1)} %get-tuple-element.49), channel_id=1, source_target_pairs={{0,17},{1,16},{2,19},{3,18},{4,21},{5,20},{6,23},{7,22},{8,25},{9,... | collective-permute-start | bytes 129032 | tf_op jit(solution)/shard_map/ppermute | solution.py:56
  71.3 6.3 %collective-permute-start.27 = (bf16[2,24,896]{2,1,0:T(8,128)(2,1)S(1)}, bf16[2,24,896]{2,1,0:T(8,128)(2,1)S(1)}, u32[]{:S(2)}, u32[]{:S(2)}) collective-permute-start(bf16[2,24,896]{2,1,0:T(8,128)(2,1)S(1)} %pad_maximum_fusion.1.refs_0_), channel_id=1, source_target_pairs={{0,6},{1,7},{2,4},{3,5},{4,2},{5,3},{6,0},{7,1},{8,14},{9,15},{10,... | collective-permute-start | bytes 258056 | tf_op jit(solution)/shard_map/ppermute | solution.py:56
  72.9 5.4 %collective-permute-start.23 = (bf16[2,24,896]{2,1,0:T(8,128)(2,1)S(1)}, bf16[2,24,896]{2,1,0:T(8,128)(2,1)S(1)}, u32[]{:S(2)}, u32[]{:S(2)}) collective-permute-start(bf16[2,24,896]{2,1,0:T(8,128)(2,1)S(1)} %pad_maximum_fusion.1.refs_0_), channel_id=1, source_target_pairs={{0,8},{1,9},{2,10},{3,11},{4,12},{5,13},{6,14},{7,15},{8,0},{9,1},... | collective-permute-start | bytes 258056 | tf_op jit(solution)/shard_map/ppermute | solution.py:56
  72.9 6.9 %collective-permute-start.22 = (bf16[2,24,896]{2,1,0:T(8,128)(2,1)S(1)}, bf16[2,24,896]{2,1,0:T(8,128)(2,1)S(1)}, u32[]{:S(2)}, u32[]{:S(2)}) collective-permute-start(bf16[2,24,896]{2,1,0:T(8,128)(2,1)S(1)} %pad_maximum_fusion.1.refs_0_), channel_id=1, source_target_pairs={{0,17},{1,16},{2,19},{3,18},{4,21},{5,20},{6,23},{7,22},{8,25},{9,... | collective-permute-start | bytes 258056 | tf_op jit(solution)/shard_map/ppermute | solution.py:56
  73.7 7.4 %collective-permute-start.21 = (bf16[2,24,896]{2,1,0:T(8,128)(2,1)S(1)}, bf16[2,24,896]{2,1,0:T(8,128)(2,1)S(1)}, u32[]{:S(2)}, u32[]{:S(2)}) collective-permute-start(bf16[2,24,896]{2,1,0:T(8,128)(2,1)S(1)} %pad_maximum_fusion.1.refs_0_), channel_id=1, source_target_pairs={{0,16},{1,17},{2,18},{3,19},{4,20},{5,21},{6,22},{7,23},{8,24},{9,... | collective-permute-start | bytes 258056 | tf_op jit(solution)/shard_map/ppermute | solution.py:56
  75.2 6.0 %collective-permute-start.20 = (bf16[2,24,896]{2,1,0:T(8,128)(2,1)S(1)}, bf16[2,24,896]{2,1,0:T(8,128)(2,1)S(1)}, u32[]{:S(2)}, u32[]{:S(2)}) collective-permute-start(bf16[2,24,896]{2,1,0:T(8,128)(2,1)S(1)} %pad_maximum_fusion.1.refs_0_), channel_id=1, source_target_pairs={{0,1},{1,0},{2,3},{3,2},{4,5},{5,4},{6,7},{7,6},{8,9},{9,8},{10,11... | collective-permute-start | bytes 258056 | tf_op jit(solution)/shard_map/ppermute | solution.py:56
  77.6 5.8 %collective-permute-start.30 = (bf16[2,24,896]{2,1,0:T(8,128)(2,1)S(1)}, bf16[2,24,896]{2,1,0:T(8,128)(2,1)S(1)}, u32[]{:S(2)}, u32[]{:S(2)}) collective-permute-start(bf16[2,24,896]{2,1,0:T(8,128)(2,1)S(1)} %collective-permute-done.27.refs_1_), channel_id=1, source_target_pairs={{0,17},{1,16},{2,19},{3,18},{4,21},{5,20},{6,23},{7,22},{8,25},{9,... | collective-permute-start | bytes 258056 | tf_op jit(solution)/shard_map/ppermute | solution.py:56
  78.4 5.3 %collective-permute-start.29 = (bf16[2,24,896]{2,1,0:T(8,128)(2,1)S(1)}, bf16[2,24,896]{2,1,0:T(8,128)(2,1)S(1)}, u32[]{:S(2)}, u32[]{:S(2)}) collective-permute-start(bf16[2,24,896]{2,1,0:T(8,128)(2,1)S(1)} %collective-permute-done.27.refs_1_), channel_id=1, source_target_pairs={{0,16},{1,17},{2,18},{3,19},{4,20},{5,21},{6,22},{7,23},{8,24},{9,... | collective-permute-start | bytes 258056 | tf_op jit(solution)/shard_map/ppermute | solution.py:56
  79.9 4.5 %collective-permute-start.28 = (bf16[2,24,896]{2,1,0:T(8,128)(2,1)S(1)}, bf16[2,24,896]{2,1,0:T(8,128)(2,1)S(1)}, u32[]{:S(2)}, u32[]{:S(2)}) collective-permute-start(bf16[2,24,896]{2,1,0:T(8,128)(2,1)S(1)} %collective-permute-done.27.refs_1_), channel_id=1, source_target_pairs={{0,1},{1,0},{2,3},{3,2},{4,5},{5,4},{6,7},{7,6},{8,9},{9,8},{10,11... | collective-permute-start | bytes 258056 | tf_op jit(solution)/shard_map/ppermute | solution.py:56
  (25 other events, 260.5 us)

commit v3 on v2

--- a/solution.py
+++ b/solution.py
@@ -1,4 +1,3 @@
-import functools
 import math
 
 import jax
@@ -69,7 +68,7 @@
 HBM = pl.BlockSpec(memory_space=pltpu.HBM)
 
 
-def local_call(kernel, name, out_shape, in_specs, args, limit, scratch=(), busy=(0, 0), out_specs=None):
+def local_call(kernel, out_shape, in_specs, args, limit, scratch=(), busy=(0, 0), out_specs=None):
     return pl.pallas_call(
         kernel,
         out_shape=out_shape,
@@ -78,8 +77,11 @@
         scratch_shapes=list(scratch),
         compiler_params=pltpu.CompilerParams(vmem_limit_bytes=limit * MIB),
         cost_estimate=pl.CostEstimate(flops=busy[0], bytes_accessed=busy[1], transcendentals=0),
-        name=name,
     )(*args)
+
+
+def in_hbm(value):
+    return pltpu.with_memory_space_constraint(value, pltpu.HBM)
 
 
 def spans(total, step):
@@ -123,7 +125,7 @@
 
     shape = jax.ShapeDtypeStruct((g.cols, half, share), BF)
     return local_call(
-        kernel, "down_matmul", [shape, shape], [SM, HBM, HBM], (at, out_grad, w_down), 52,
+        kernel, [shape, shape], [SM, HBM, HBM], (at, in_hbm(out_grad), in_hbm(w_down)), 52,
         [pltpu.VMEM((slots, width), BF), pltpu.VMEM((units, width), BF), pltpu.SemaphoreType.DMA((len(parts) + 1,))],
         busy=(2 * slots * units * width, 2 * units * width),
     )
@@ -131,46 +133,60 @@
 
 def core_sum(g, at, keep, other, tall):
     share = keep.shape[2]
+    fold = cdiv(share // LANES, 2) * LANES
 
     def kernel(pos, keep_ref, other_ref, own_ref, *piece_refs):
         for (dx, dy), ref in zip(g.shifts, (own_ref,) + piece_refs):
             col = (pos[2] + dy) % g.cols
-            rows = pl.ds(dx * tall, tall)
-            ref[...] = (keep_ref[col, rows].astype(F32) + other_ref[col, rows].astype(F32)).astype(ref.dtype)
-
-    shapes = [jax.ShapeDtypeStruct((tall, share), F32 if s == (0, 0) else BF) for s in g.shifts]
-    return local_call(kernel, "core_sum", shapes, [SM, VM, VM], (at, keep, other), 4, busy=HINT)
+            both = keep_ref[col].astype(F32) + other_ref[col].astype(F32)
+            part = both[dx * tall : (dx + 1) * tall]
+            if (dx, dy) == (0, 0):
+                ref[...] = part
+            else:
+                ref[:tall] = part[:, :fold].astype(BF)
+                ref[tall:, : share - fold] = part[:, fold:].astype(BF)
+                if share < 2 * fold:
+                    ref[tall:, share - fold :] = jnp.zeros((tall, 2 * fold - share), BF)
+
+    shapes = [
+        jax.ShapeDtypeStruct((tall, share), F32) if s == (0, 0) else jax.ShapeDtypeStruct((2 * tall, fold), BF)
+        for s in g.shifts
+    ]
+    return local_call(kernel, shapes, [SM, VM, VM], (at, keep, other), 4, busy=HINT)
 
 
 def gate_grads(g, at, total, others, gate_pre, up_pre):
+    own, units = gate_pre.shape
     share = total.shape[1]
-    own, units = gate_pre.shape
+    fold = cdiv(share // LANES, 2) * LANES
 
     def kernel(pos, total_ref, *refs):
         other_refs, (gate_ref, up_ref, out_ref) = refs[:-3], refs[-3:]
-        hidden = total_ref[...]
-        for ref in other_refs:
-            hidden = hidden + ref[...].astype(F32)
-        hidden = hidden[:own]
-        for c in range(g.cols):
-            valid = max(0, min(share, units - c * share))
-
-            @pl.when(pos[2] == c)
-            def _():
-                gate = gate_ref[:, c * share : c * share + valid].astype(F32)
-                up = up_ref[:, c * share : c * share + valid].astype(F32)
-                grad = hidden[:, :valid]
-                squash = 1.0 / (1.0 + jnp.exp(-gate))
-                base = grad * squash
-                out_ref[:own, :valid] = (base * up * (1.0 + gate * (1.0 - squash))).astype(BF)
-                out_ref[own:, :valid] = (base * gate).astype(BF)
-                if valid < share:
-                    out_ref[:, valid:] = jnp.zeros((2 * own, share - valid), BF)
+        for low, high in ((0, fold), (fold, share)):
+            grad = total_ref[:, low:high]
+            for ref in other_refs:
+                folded = ref[...].astype(F32)
+                grad = grad + (folded[:own] if low == 0 else folded[own:, : high - low])
+            for c in range(g.cols):
+                valid = max(0, min(high, units - c * share) - low)
+
+                @pl.when(pos[2] == c)
+                def _():
+                    if valid:
+                        start = c * share + low
+                        gate = gate_ref[:, start : start + valid].astype(F32)
+                        up = up_ref[:, start : start + valid].astype(F32)
+                        squash = 1.0 / (1.0 + jnp.exp(-gate))
+                        base = grad[:, :valid] * squash
+                        out_ref[:own, low : low + valid] = (base * up * (1.0 + gate * (1.0 - squash))).astype(BF)
+                        out_ref[own:, low : low + valid] = (base * gate).astype(BF)
+                    if valid < high - low:
+                        out_ref[:, low + valid : high] = jnp.zeros((2 * own, high - low - valid), BF)
 
     shape = jax.ShapeDtypeStruct((2 * own, share), BF)
     return local_call(
-        kernel, "gate_grads", shape, [SM] + [VM] * (len(others) + 3),
-        (at, total, *others, gate_pre, up_pre), 4, busy=HINT,
+        kernel, shape, [SM] + [VM] * (len(others) + 3),
+        (at, total, *others, gate_pre, up_pre), 6, busy=HINT,
     )
 
 
@@ -217,46 +233,49 @@
                 out_ref[half:] = done[(1 - k) * half : (2 - k) * half]
 
     return local_call(
-        kernel, "input_matmul", jax.ShapeDtypeStruct((slots, width), BF), [SM, SM] + [VM] * (len(pieces) + 3),
+        kernel, jax.ShapeDtypeStruct((slots, width), BF), [SM, SM] + [VM] * (len(pieces) + 3),
         (at, img_count, *pieces, route, w_gate, w_up), 8,
         [pltpu.VMEM((g.cols, 2 * own * rows, share), BF)],
         busy=(8 * slots * units * width, 4 * units * width),
     )
 
 
-def fetch_rows(g, at, w_proj, steps):
+def fetch_rows(at, w_proj, steps, start, count):
     block = SHUF * LANES
     last = cdiv(w_proj.shape[0], block) - 1
 
     def kernel(pos, w_ref, out_ref, sem):
         copies = []
-        for i in range(steps):
-            first = jnp.minimum(pos[3] * steps + i, last) * block
+        for i in range(count):
+            first = jnp.minimum(pos[3] * steps + start + i, last) * block
             copies.append(pltpu.make_async_copy(w_ref.at[pl.ds(first, block)], out_ref.at[i], sem.at[i]))
             copies[-1].start()
         for copy in copies:
             copy.wait()
 
-    shape = jax.ShapeDtypeStruct((steps, block, w_proj.shape[1]), BF)
+    shape = jax.ShapeDtypeStruct((count, block, w_proj.shape[1]), BF)
     return local_call(
-        kernel, "fetch_rows", shape, [SM, HBM], (at, w_proj), 22, [pltpu.SemaphoreType.DMA((steps,))],
-        busy=(0, 2 * steps * block * w_proj.shape[1]),
+        kernel, shape, [SM, HBM], (at, in_hbm(w_proj)), 22, [pltpu.SemaphoreType.DMA((count,))],
+        busy=(0, 2 * count * block * w_proj.shape[1]),
     )
 
 
-def shuffle_matmul(g, image_grad, w_rows):
+def shuffle_matmul(g, image_grad, w_parts):
     slots, width = image_grad.shape
     half = slots // CORES
-    steps, block, width = w_rows.shape
+    block, width = w_parts[0].shape[1:]
+    steps = sum(w.shape[0] for w in w_parts)
     sub = g.chips // SHUF
     piece = half // sub
 
-    def kernel(grad_ref, w_ref, keep_ref, give_ref, parts):
+    def kernel(grad_ref, *refs):
+        w_refs, (keep_ref, give_ref, parts) = refs[: len(w_parts)], refs[len(w_parts) :]
+        blocks = [(ref, n) for ref in w_refs for n in range(ref.shape[0])]
         source = lax.broadcasted_iota(jnp.int32, (block, block), 0)
         target = lax.broadcasted_iota(jnp.int32, (block, block), 1)
         order = jnp.where(source == SHUF * (target % LANES) + target // LANES, 1.0, 0.0).astype(BF)
-        for i in range(steps):
-            parts[i * slots : (i + 1) * slots] = dot_nt(grad_ref[...], w_ref[i]).astype(BF)
+        for i, (ref, n) in enumerate(blocks):
+            parts[i * slots : (i + 1) * slots] = dot_nt(grad_ref[...], ref[n]).astype(BF)
         done = dot_nn(parts[...], order).astype(BF)
         for i in range(steps):
             for ref, top in ((keep_ref, i * slots), (give_ref, i * slots + half)):
@@ -267,7 +286,7 @@
 
     shape = jax.ShapeDtypeStruct((g.chips, piece, steps * LANES), BF)
     return local_call(
-        kernel, "shuffle_matmul", [shape, shape], [VM, VM], (image_grad, w_rows), 8,
+        kernel, [shape, shape], [VM] * (1 + len(w_parts)), (image_grad, *w_parts), 8,
         [pltpu.VMEM((steps * slots, block), BF)],
         busy=(2 * slots * width * block * steps, 2 * width * block * steps),
     )
@@ -280,7 +299,7 @@
             ref[...] = (keep_ref[chip].astype(F32) + other_ref[chip].astype(F32)).astype(ref.dtype)
 
     shapes = [jax.ShapeDtypeStruct(keep.shape[1:], F32 if s == (0, 0) else BF) for s in g.shifts]
-    return local_call(kernel, "chip_sum", shapes, [SM, VM, VM], (at, keep, other), 4)
+    return local_call(kernel, shapes, [SM, VM, VM], (at, keep, other), 4)
 
 
 def order_hidden(g, at, parts, piece):
@@ -311,9 +330,7 @@
         refs[-1][...] = total.astype(BF)
 
     shape = jax.ShapeDtypeStruct((units, patches), BF)
-    return local_call(
-        kernel, "order_hidden", shape, [SM] + [VM] * len(parts), (at, *parts), 8, busy=(2 * units * patches * patches, 0)
-    )
+    return local_call(kernel, shape, [SM] + [VM] * len(parts), (at, *parts), 8, busy=(2 * units * patches * patches, 0))
 
 
 def weight_grad(g, at, result, features, first, pieces, hidden):
@@ -322,6 +339,7 @@
     scale = 1.0 / math.sqrt(patches)
     masks = row_masks(g)
     full, tail = divmod(features, wide)
+    parts = spans(wide, 2 * cdiv(wide, 4 * LANES) * LANES)
     fresh = result is None
 
     def kernel(pos, *refs):
@@ -332,17 +350,20 @@
             row = first + i if masks is None else masks[first + i] ^ pos[3]
             for n, ref in enumerate(piece_refs):
                 patch[i, n * piece : (n + 1) * piece] = ref[i]
-            buf[i] = (dot_nn(hidden_ref[...], patch[i]) * scale).astype(BF)
-            begun = []
-            if masks is not None or row < full:
-                ends = out_ref.at[:, pl.ds(row * wide, wide)]
-                begun.append((row < full, pltpu.make_async_copy(buf.at[i], ends, sem.at[i])))
-            if tail:
-                ends = out_ref.at[:, pl.ds(full * wide, tail)]
-                begun.append((row == full, pltpu.make_async_copy(buf.at[i, :, pl.ds(0, tail)], ends, sem.at[i])))
-            for now, copy in begun:
-                pl.when(now)(copy.start)
-            sends += begun
+            for n, (off, size) in enumerate(parts):
+                buf[i, :, off : off + size] = (dot_nn(hidden_ref[...], patch[i, :, off : off + size]) * scale).astype(BF)
+                done = sem.at[i * len(parts) + n]
+                begun = []
+                if masks is not None or row < full:
+                    ends = out_ref.at[:, pl.ds(row * wide + off, size)]
+                    begun.append((row < full, pltpu.make_async_copy(buf.at[i, :, pl.ds(off, size)], ends, done)))
+                rest = min(size, tail - off)
+                if rest > 0:
+                    ends = out_ref.at[:, pl.ds(full * wide + off, rest)]
+                    begun.append((row == full, pltpu.make_async_copy(buf.at[i, :, pl.ds(off, rest)], ends, done)))
+                for now, copy in begun:
+                    pl.when(now)(copy.start)
+                sends += begun
         for now, copy in sends:
             pl.when(now)(copy.wait)
 
@@ -354,7 +375,7 @@
         scratch_shapes=[
             pltpu.VMEM((count, patches, wide), BF),
             pltpu.VMEM((count, units, wide), BF),
-            pltpu.SemaphoreType.DMA((count,)),
+            pltpu.SemaphoreType.DMA((count * len(parts),)),
         ],
         input_output_aliases={} if fresh else {1: 0},
         compiler_params=pltpu.CompilerParams(vmem_limit_bytes=16 * MIB),
@@ -392,14 +413,14 @@
     return lax.optimization_barrier((first, *later))[1:]
 
 
-def shards(out_grad, gate_pre, up_pre, w_gate, w_up, w_down, w_proj, enc_hidden, route, img_count):
+def image_block(out_grad, gate_pre, up_pre, w_gate, w_up, w_down, w_proj, enc_hidden, route, img_count):
     g = Grid()
     at = g.place()
     slots = route.shape[0]
     own = gate_pre.shape[0]
     half = slots // CORES
     units = w_down.shape[0]
-    tall = cdiv(own, 16) * 16
+    tall = own
     share = cdiv(cdiv(units, g.cols), LANES) * LANES
     doubling = not g.rows & (g.rows - 1)
 
@@ -425,7 +446,8 @@
         saved_parts.append(g.send(mine, row=lambda r: r ^ mask))
         step *= 2
     pieces = [grads] + to_chips([grads] * (g.chips - 1))
-    pieces = pieces + [g.swap(p) for p in pieces]
+    swapped = [g.swap(grads)]
+    pieces = pieces + swapped + [g.swap(p) for p in pieces[1:]]
     if not doubling:
         saved_parts = [lax.all_gather(enc_hidden, "row", axis=0, tiled=False)]
     image_grad = input_matmul(g, at, pieces, route.reshape(1, slots), img_count, w_gate.T, w_up.T, own)
@@ -434,15 +456,17 @@
     steps = cdiv(cdiv(features, g.rows), LANES)
     piece = SHUF * half // g.chips
     image_grad, late = lax.optimization_barrier((image_grad, at))
-    w_rows = fetch_rows(g, late, w_proj, steps)
-    hidden = order_hidden(g, late, saved_parts, piece)
-    image_grad, (hidden, w_rows) = sum_rows(g, image_grad, (hidden, w_rows))
-
-    keep, give = shuffle_matmul(g, image_grad, w_rows)
+    early = steps // 2 + 1
+    w_parts = [fetch_rows(late, w_proj, steps, s, n) for s, n in ((0, early), (early, steps - early)) if n]
+    image_grad, w_parts = sum_rows(g, image_grad, w_parts)
+
+    keep, give = shuffle_matmul(g, image_grad, w_parts)
     total, *pieces = chip_sum(g, at, keep, g.swap(give))
     for part in to_chips(pieces):
         total = total + part.astype(F32)
     patch_grad = total.astype(BF)
+    late, patch_grad = lax.optimization_barrier((at, patch_grad))
+    hidden = order_hidden(g, late, saved_parts, piece)
 
     if not doubling:
         batches = [lax.all_gather(patch_grad, "row", axis=0, tiled=False)]
@@ -451,15 +475,22 @@
         while step < g.rows:
             mask = 2 * step - 1
             other = g.send(stack, row=lambda r: r ^ mask)
+            if step == 1:
+                other, hidden = lax.optimization_barrier((other, hidden))
             stack = jnp.concatenate([stack, other])
             batches.append(stack if step == 1 else other)
             step *= 2
         batches = batches or [stack]
     result, first = None, 0
+    held = []
     for batch in batches:
-        pieces = [batch] + to_chips([batch] * (g.chips - 1))
-        pieces = pieces + [g.swap(p) for p in pieces]
-        result = weight_grad(g, at, result, features, first, pieces, hidden)
+        held.append([batch] + to_chips([batch] * (g.chips - 1)))
+    for batch, pieces in zip(batches, held):
+        if result is not None:
+            result, *pieces = lax.optimization_barrier((result, *pieces))
+        others = [g.swap(batch)]
+        others += [g.swap(p) for p in pieces[1:]]
+        result = weight_grad(g, at, result, features, first, pieces + others, hidden)
         first += batch.shape[0]
     return result.T
 
@@ -477,6 +508,4 @@
         P(),
         P(),
     )
-    return jax.shard_map(
-        shards, mesh=mesh, in_specs=placed, out_specs=P(None, ("enc", "col")), check_vma=False
-    )
+    return jax.shard_map(image_block, mesh=mesh, in_specs=placed, out_specs=P(None, ("enc", "col")), check_vma=False)

time: 90.7 us -> 89.7 us (0.989)
  waiting for transfers between devices: 29.3 us -> 21.6 us
  starting transfers between devices: 30.6 us -> 37.2 us
  Pallas kernels: 29 us -> 30 us
    ppermute x35, waiting for transfers between devices: 29.3 us -> 21.6 us  [send(): return lax.ppermute(value, AXES, pairs)]
    ppermute x35, starting transfers between devices: 30.6 us -> 37.2 us  [send(): return lax.ppermute(value, AXES, pairs)]
    pallas_call x8 -> x9, Pallas kernels: 23.6 us -> 25 us  [local_call(): pl.pallas_call(kernel, out_shape=out_shape, in_specs=in_specs, out_specs=...]
  transfers between devices with their start and end apart: 35 -> 35, of which waited for: 17 -> 17; matrix products, arithmetic and copies ran while one was open for 0% -> 0% of each run, Pallas kernels for 15% -> 10%
where the time goes in v3:
time: 89.7 us; the launch traced here: 89.5 us
  starting transfers between devices  37.2 us (41%)
  Pallas kernels  30 us (33%)
  waiting for transfers between devices  21.6 us (24%)
    ppermute x35, starting transfers between devices, send(): return lax.ppermute(value, AXES, pairs)  37.2 us
    pallas_call x9, Pallas kernels, local_call(): pl.pallas_call(kernel, out_shape=out_shape, in_specs=in_specs, out_specs=...  25 us
    ppermute x35, waiting for transfers between devices, send(): return lax.ppermute(value, AXES, pairs)  21.6 us
    pallas_call x2, Pallas kernels, weight_grad(): pl.pallas_call(kernel, out_shape=jax.ShapeDtypeStruct((units, features),...  5.01 us
  transfers between devices with their start and end apart: 35, of which 17 were waited for; matrix products, arithmetic and copies ran while one was open for 0% of the time, Pallas kernels for 10%

profile of v3, /device:TPU:0, one launch (start us, length us, event | category | flops | bytes accessed | tf_op | source)
XLA Modules:
  0.0 89.5 jit_solution(4943706216670341782)
XLA Ops:
  0.1 7.9 %shard_map.100 = (bf16[2,24,3712]{2,1,0:T(8,128)(2,1)S(1)}, bf16[2,24,3712]{2,1,0:T(8,128)(2,1)S(1)}) custom-call(s32[4]{0:T(128)S(1)} %pad_add_fusion.pos, bf16[48,1024]{1,0:T(8,128)(2,1)} %grad_hbm.1, bf16[7392,1024]{1,0:T(8,128)(2,1)} %w_ref.3), custom_call_target="tpu_custom_call" | custom-call | flops 726663168 | bytes 15138816 | tf_op jit(solution)/shard_map/pallas_call | solution.py:72
  10.5 2.9 %collective-permute-start.2 = (bf16[24,1920]{1,0:T(8,128)(2,1)S(1)}, bf16[24,1920]{1,0:T(8,128)(2,1)S(1)}, u32[]{:S(2)}, u32[]{:S(2)}) collective-permute-start(bf16[24,1920]{1,0:T(8,128)(2,1)S(1)} %get-tuple-element.40), channel_id=1, source_target_pairs={{0,1},{1,0},{2,3},{3,2},{4,5},{5,4},{6,7},{7,6},{8,9},{9,8},{10,11... | collective-permute-start | bytes 276488 | tf_op jit(solution)/shard_map/ppermute | solution.py:55
  13.5 1.5 %collective-permute-start.3 = (bf16[24,1920]{1,0:T(8,128)(2,1)S(1)}, bf16[24,1920]{1,0:T(8,128)(2,1)S(1)}, u32[]{:S(2)}, u32[]{:S(2)}) collective-permute-start(bf16[24,1920]{1,0:T(8,128)(2,1)S(1)} %get-tuple-element.41), channel_id=1, source_target_pairs={{0,16},{1,17},{2,18},{3,19},{4,20},{5,21},{6,22},{7,23},{8,24},{9,... | collective-permute-start | bytes 276488 | tf_op jit(solution)/shard_map/ppermute | solution.py:55
  15.0 2.0 %collective-permute-start.1 = (bf16[1,48,800]{2,1,0:T(8,128)(2,1)S(1)}, bf16[1,48,800]{2,1,0:T(8,128)(2,1)S(1)}, u32[]{:S(2)}, u32[]{:S(2)}) collective-permute-start(bf16[1,48,800]{2,1,0:T(8,128)(2,1)S(1)} %bitcast.16), channel_id=1, source_target_pairs={{0,2},{1,3},{2,0},{3,1},{4,6},{5,7},{6,4},{7,5},{8,10},{9,11},{10,... | collective-permute-start | bytes 230408 | tf_op jit(solution)/shard_map/ppermute | solution.py:55
  17.1 2.5 %collective-permute-done.1.refs_1_ = bf16[1,48,800]{2,1,0:T(8,128)(2,1)S(1)} collective-permute-done((bf16[1,48,800]{2,1,0:T(8,128)(2,1)S(1)}, bf16[1,48,800]{2,1,0:T(8,128)(2,1)S(1)}, u32[]{:S(2)}, u32[]{:S(2)}) %collective-permute-start.1) | collective-permute-done | bytes 76832 | tf_op jit(solution)/shard_map/ppermute | solution.py:55
  21.3 2.1 %collective-permute-start.7 = (bf16[24,3712]{1,0:T(8,128)(2,1)S(1)}, bf16[24,3712]{1,0:T(8,128)(2,1)S(1)}, u32[]{:S(2)}, u32[]{:S(2)}) collective-permute-start(bf16[24,3712]{1,0:T(8,128)(2,1)S(1)} %shard_map.102.refs_0_), channel_id=1, source_target_pairs={{0,17},{1,16},{2,19},{3,18},{4,21},{5,20},{6,23},{7,22},{8,25},{9,... | collective-permute-start | bytes 534536 | tf_op jit(solution)/shard_map/ppermute | solution.py:55
  24.8 4.2 %collective-permute-done.7.refs_3_ = bf16[24,3712]{1,0:T(8,128)(2,1)S(1)} collective-permute-done((bf16[24,3712]{1,0:T(8,128)(2,1)S(1)}, bf16[24,3712]{1,0:T(8,128)(2,1)S(1)}, u32[]{:S(2)}, u32[]{:S(2)}) %collective-permute-start.7) | collective-permute-done | bytes 178208 | tf_op jit(solution)/shard_map/ppermute | solution.py:55
  29.1 2.1 %collective-permute-done.6.refs_2_ = bf16[24,3712]{1,0:T(8,128)(2,1)S(1)} collective-permute-done((bf16[24,3712]{1,0:T(8,128)(2,1)S(1)}, bf16[24,3712]{1,0:T(8,128)(2,1)S(1)}, u32[]{:S(2)}, u32[]{:S(2)}) %collective-permute-start.6) | collective-permute-done | bytes 178208 | tf_op jit(solution)/shard_map/ppermute | solution.py:55
  33.0 6.0 %shard_map.103 = bf16[48,1024]{1,0:T(8,128)(2,1)S(1)} custom-call(s32[4]{0:T(128)S(1)} %pad_add_fusion.pos, s32[4]{0:T(128)S(1)} %copy-done.1, bf16[24,3712]{1,0:T(8,128)(2,1)S(1)} %shard_map.102.refs_0_, bf16[24,3712]{1,0:T(8,128)(2,1)S(1)} %collective-permute-done.5.refs_1_, bf16[24,3712]{1,0:T(8,128)(2,1)S(1)} %collective-permute-done.6.refs_2_, ...), custom_call_target="tpu_custom_call" | custom-call | flops 2906652672 | bytes 30277632 | tf_op jit(solution)/shard_map/pallas_call | solution.py:72
  39.0 1.6 %collective-permute-start.12 = (bf16[48,1024]{1,0:T(8,128)(2,1)S(1)}, bf16[48,1024]{1,0:T(8,128)(2,1)S(1)}, u32[]{:S(2)}, u32[]{:S(2)}) collective-permute-start(bf16[48,1024]{1,0:T(8,128)(2,1)S(1)} %shard_map.103), channel_id=1, source_target_pairs={{0,2},{1,3},{2,0},{3,1},{4,6},{5,7},{6,4},{7,5},{8,10},{9,11},{10,... | collective-permute-start | bytes 294920 | tf_op jit(solution)/shard_map/ppermute | solution.py:55
  40.6 2.8 %shard_map.104.refs_0_ = bf16[4,512,1024]{2,1,0:T(8,128)(2,1)S(1)} custom-call(s32[4]{0:T(128)S(1)} %pad_add_fusion.pos, bf16[12800,1024]{1,0:T(8,128)(2,1)} %w_ref.5), custom_call_target="tpu_custom_call" | custom-call | bytes 4194304 | tf_op jit(solution)/shard_map/pallas_call | solution.py:72
  44.0 3.7 %collective-permute-start.13 = (bf16[48,1024]{1,0:T(8,128)(2,1)S(1)}, bf16[48,1024]{1,0:T(8,128)(2,1)S(1)}, u32[]{:S(2)}, u32[]{:S(2)}) collective-permute-start(bf16[48,1024]{1,0:T(8,128)(2,1)S(1)} %add_convert_fusion.1), channel_id=1, source_target_pairs={{0,6},{1,7},{2,4},{3,5},{4,2},{5,3},{6,0},{7,1},{8,14},{9,15},{10,... | collective-permute-start | bytes 294920 | tf_op jit(solution)/shard_map/ppermute | solution.py:55
  47.7 2.4 %shard_map.105.refs_1_ = bf16[3,512,1024]{2,1,0:T(8,128)(2,1)S(1)} custom-call(s32[4]{0:T(128)S(1)} %pad_add_fusion.pos, bf16[12800,1024]{1,0:T(8,128)(2,1)} %w_ref.5), custom_call_target="tpu_custom_call" | custom-call | bytes 3145728 | tf_op jit(solution)/shard_map/pallas_call | solution.py:72
  50.5 2.5 %shard_map.106 = (bf16[4,24,896]{2,1,0:T(8,128)(2,1)S(1)}, bf16[4,24,896]{2,1,0:T(8,128)(2,1)S(1)}) custom-call(bf16[48,1024]{1,0:T(8,128)(2,1)S(1)} %add_convert_fusion.grad_ref, bf16[4,512,1024]{2,1,0:T(8,128)(2,1)S(1)} %shard_map.104.refs_0_, bf16[3,512,1024]{2,1,0:T(8,128)(2,1)S(1)} %shard_map.105.refs_1_), custom_call_target="tpu_custom_call" | custom-call | flops 352321536 | bytes 7340032 | tf_op jit(solution)/shard_map/pallas_call | solution.py:72
  53.2 1.4 %collective-permute-done.14.other_ref = bf16[4,24,896]{2,1,0:T(8,128)(2,1)S(1)} collective-permute-done((bf16[4,24,896]{2,1,0:T(8,128)(2,1)S(1)}, bf16[4,24,896]{2,1,0:T(8,128)(2,1)S(1)}, u32[]{:S(2)}, u32[]{:S(2)}) %collective-permute-start.14) | collective-permute-done | bytes 172064 | tf_op jit(solution)/shard_map/ppermute | solution.py:55
  57.3 1.4 %collective-permute-start.17 = (bf16[24,896]{1,0:T(8,128)(2,1)S(1)}, bf16[24,896]{1,0:T(8,128)(2,1)S(1)}, u32[]{:S(2)}, u32[]{:S(2)}) collective-permute-start(bf16[24,896]{1,0:T(8,128)(2,1)S(1)} %get-tuple-element.57), channel_id=1, source_target_pairs={{0,17},{1,16},{2,19},{3,18},{4,21},{5,20},{6,23},{7,22},{8,25},{9,... | collective-permute-start | bytes 129032 | tf_op jit(solution)/shard_map/ppermute | solution.py:55
  58.7 3.7 %collective-permute-start.19 = (bf16[2,48,800]{2,1,0:T(8,128)(2,1)S(1)}, bf16[2,48,800]{2,1,0:T(8,128)(2,1)S(1)}, u32[]{:S(2)}, u32[]{:S(2)}) collective-permute-start(bf16[2,48,800]{2,1,0:T(8,128)(2,1)S(1)} %pad_maximum_fusion), channel_id=1, source_target_pairs={{0,6},{1,7},{2,4},{3,5},{4,2},{5,3},{6,0},{7,1},{8,14},{9,15},{10,... | collective-permute-start | bytes 460808 | tf_op jit(solution)/shard_map/ppermute | solution.py:55
  63.6 2.9 %collective-permute-done.19.refs_2_ = bf16[2,48,800]{2,1,0:T(8,128)(2,1)S(1)} collective-permute-done((bf16[2,48,800]{2,1,0:T(8,128)(2,1)S(1)}, bf16[2,48,800]{2,1,0:T(8,128)(2,1)S(1)}, u32[]{:S(2)}, u32[]{:S(2)}) %collective-permute-start.19) | collective-permute-done | bytes 153632 | tf_op jit(solution)/shard_map/ppermute | solution.py:55
  68.0 1.8 %collective-permute-start.22 = (bf16[2,24,896]{2,1,0:T(8,128)(2,1)S(1)}, bf16[2,24,896]{2,1,0:T(8,128)(2,1)S(1)}, u32[]{:S(2)}, u32[]{:S(2)}) collective-permute-start(bf16[2,24,896]{2,1,0:T(8,128)(2,1)S(1)} %pad_maximum_fusion.1.refs_0_), channel_id=1, source_target_pairs={{0,17},{1,16},{2,19},{3,18},{4,21},{5,20},{6,23},{7,22},{8,25},{9,... | collective-permute-start | bytes 258056 | tf_op jit(solution)/shard_map/ppermute | solution.py:55
  71.5 3.7 %collective-permute-start.27 = (bf16[2,24,896]{2,1,0:T(8,128)(2,1)S(1)}, bf16[2,24,896]{2,1,0:T(8,128)(2,1)S(1)}, u32[]{:S(2)}, u32[]{:S(2)}) collective-permute-start(bf16[2,24,896]{2,1,0:T(8,128)(2,1)S(1)} %pad_maximum_fusion.1.refs_0_), channel_id=1, source_target_pairs={{0,6},{1,7},{2,4},{3,5},{4,2},{5,3},{6,0},{7,1},{8,14},{9,15},{10,... | collective-permute-start | bytes 258056 | tf_op jit(solution)/shard_map/ppermute | solution.py:55
  76.3 1.5 %collective-permute-done.27.refs_1_ = bf16[2,24,896]{2,1,0:T(8,128)(2,1)S(1)} collective-permute-done((bf16[2,24,896]{2,1,0:T(8,128)(2,1)S(1)}, bf16[2,24,896]{2,1,0:T(8,128)(2,1)S(1)}, u32[]{:S(2)}, u32[]{:S(2)}) %collective-permute-start.27) | collective-permute-done | bytes 86048 | tf_op jit(solution)/shard_map/ppermute | solution.py:55
  77.8 1.7 %collective-permute-start.30 = (bf16[2,24,896]{2,1,0:T(8,128)(2,1)S(1)}, bf16[2,24,896]{2,1,0:T(8,128)(2,1)S(1)}, u32[]{:S(2)}, u32[]{:S(2)}) collective-permute-start(bf16[2,24,896]{2,1,0:T(8,128)(2,1)S(1)} %collective-permute-done.27.refs_1_), channel_id=1, source_target_pairs={{0,17},{1,16},{2,19},{3,18},{4,21},{5,20},{6,23},{7,22},{8,25},{9,... | collective-permute-start | bytes 258056 | tf_op jit(solution)/shard_map/ppermute | solution.py:55
  81.3 2.5 %weight_grad.2.refs_0_ = bf16[800,3200]{1,0:T(8,128)(2,1)} custom-call(s32[4]{0:T(128)S(1)} %pad_add_fusion.pos, bf16[2,24,896]{2,1,0:T(8,128)(2,1)S(1)} %pad_maximum_fusion.1.refs_0_, bf16[2,24,896]{2,1,0:T(8,128)(2,1)S(1)} %collective-permute-done.20.refs_1_, bf16[2,24,896]{2,1,0:T(8,128)(2,1)S(1)} %collective-permute-done.21.refs_2_, ...), custom_call_target="tpu_custom_call" | custom-call | flops 550502400 | bytes 2867200 | tf_op jit(solution)/shard_map/weight_grad/pallas_call | solution.py:370
  86.9 2.5 %weight_grad.3 = bf16[800,3200]{1,0:T(8,128)(2,1)} custom-call(s32[4]{0:T(128)S(1)} %pad_add_fusion.pos, bf16[800,3200]{1,0:T(8,128)(2,1)} %weight_grad.2.refs_0_, bf16[2,24,896]{2,1,0:T(8,128)(2,1)S(1)} %collective-permute-done.27.refs_1_, bf16[2,24,896]{2,1,0:T(8,128)(2,1)S(1)} %collective-permute-done.28.refs_2_, ...), custom_call_target="tpu_custom_call", output_to_operand_aliasing={{}: (1, {})} | custom-call | flops 550502400 | bytes 2867200 | tf_op jit(solution)/shard_map/weight_grad/pallas_call | solution.py:370
  (91 shorter events, 21.6 us)
Async XLA Ops:
  10.5 9.0 %collective-permute-start.2 = (bf16[24,1920]{1,0:T(8,128)(2,1)S(1)}, bf16[24,1920]{1,0:T(8,128)(2,1)S(1)}, u32[]{:S(2)}, u32[]{:S(2)}) collective-permute-start(bf16[24,1920]{1,0:T(8,128)(2,1)S(1)} %get-tuple-element.40), channel_id=1, source_target_pairs={{0,1},{1,0},{2,3},{3,2},{4,5},{5,4},{6,7},{7,6},{8,9},{9,8},{10,11... | collective-permute-start | bytes 276488 | tf_op jit(solution)/shard_map/ppermute | solution.py:55
  13.5 6.1 %collective-permute-start.3 = (bf16[24,1920]{1,0:T(8,128)(2,1)S(1)}, bf16[24,1920]{1,0:T(8,128)(2,1)S(1)}, u32[]{:S(2)}, u32[]{:S(2)}) collective-permute-start(bf16[24,1920]{1,0:T(8,128)(2,1)S(1)} %get-tuple-element.41), channel_id=1, source_target_pairs={{0,16},{1,17},{2,18},{3,19},{4,20},{5,21},{6,22},{7,23},{8,24},{9,... | collective-permute-start | bytes 276488 | tf_op jit(solution)/shard_map/ppermute | solution.py:55
  15.0 5.5 %collective-permute-start.4 = (bf16[24,1920]{1,0:T(8,128)(2,1)S(1)}, bf16[24,1920]{1,0:T(8,128)(2,1)S(1)}, u32[]{:S(2)}, u32[]{:S(2)}) collective-permute-start(bf16[24,1920]{1,0:T(8,128)(2,1)S(1)} %get-tuple-element.42), channel_id=1, source_target_pairs={{0,17},{1,16},{2,19},{3,18},{4,21},{5,20},{6,23},{7,22},{8,25},{9,... | collective-permute-start | bytes 276488 | tf_op jit(solution)/shard_map/ppermute | solution.py:55
  15.0 4.5 %collective-permute-start.1 = (bf16[1,48,800]{2,1,0:T(8,128)(2,1)S(1)}, bf16[1,48,800]{2,1,0:T(8,128)(2,1)S(1)}, u32[]{:S(2)}, u32[]{:S(2)}) collective-permute-start(bf16[1,48,800]{2,1,0:T(8,128)(2,1)S(1)} %bitcast.16), channel_id=1, source_target_pairs={{0,2},{1,3},{2,0},{3,1},{4,6},{5,7},{6,4},{7,5},{8,10},{9,11},{10,... | collective-permute-start | bytes 230408 | tf_op jit(solution)/shard_map/ppermute | solution.py:55
  21.3 7.8 %collective-permute-start.7 = (bf16[24,3712]{1,0:T(8,128)(2,1)S(1)}, bf16[24,3712]{1,0:T(8,128)(2,1)S(1)}, u32[]{:S(2)}, u32[]{:S(2)}) collective-permute-start(bf16[24,3712]{1,0:T(8,128)(2,1)S(1)} %shard_map.102.refs_0_), channel_id=1, source_target_pairs={{0,17},{1,16},{2,19},{3,18},{4,21},{5,20},{6,23},{7,22},{8,25},{9,... | collective-permute-start | bytes 534536 | tf_op jit(solution)/shard_map/ppermute | solution.py:55
  23.3 7.9 %collective-permute-start.6 = (bf16[24,3712]{1,0:T(8,128)(2,1)S(1)}, bf16[24,3712]{1,0:T(8,128)(2,1)S(1)}, u32[]{:S(2)}, u32[]{:S(2)}) collective-permute-start(bf16[24,3712]{1,0:T(8,128)(2,1)S(1)} %shard_map.102.refs_0_), channel_id=1, source_target_pairs={{0,16},{1,17},{2,18},{3,19},{4,20},{5,21},{6,22},{7,23},{8,24},{9,... | collective-permute-start | bytes 534536 | tf_op jit(solution)/shard_map/ppermute | solution.py:55
  23.9 7.4 %collective-permute-start.5 = (bf16[24,3712]{1,0:T(8,128)(2,1)S(1)}, bf16[24,3712]{1,0:T(8,128)(2,1)S(1)}, u32[]{:S(2)}, u32[]{:S(2)}) collective-permute-start(bf16[24,3712]{1,0:T(8,128)(2,1)S(1)} %shard_map.102.refs_0_), channel_id=1, source_target_pairs={{0,1},{1,0},{2,3},{3,2},{4,5},{5,4},{6,7},{7,6},{8,9},{9,8},{10,11... | collective-permute-start | bytes 534536 | tf_op jit(solution)/shard_map/ppermute | solution.py:55
  24.8 6.9 %collective-permute-start.8 = (bf16[24,3712]{1,0:T(8,128)(2,1)S(1)}, bf16[24,3712]{1,0:T(8,128)(2,1)S(1)}, u32[]{:S(2)}, u32[]{:S(2)}) collective-permute-start(bf16[24,3712]{1,0:T(8,128)(2,1)S(1)} %shard_map.102.refs_0_), channel_id=1, source_target_pairs={{0,8},{1,9},{2,10},{3,11},{4,12},{5,13},{6,14},{7,15},{8,0},{9,1},... | collective-permute-start | bytes 534536 | tf_op jit(solution)/shard_map/ppermute | solution.py:55
  39.0 5.0 %collective-permute-start.12 = (bf16[48,1024]{1,0:T(8,128)(2,1)S(1)}, bf16[48,1024]{1,0:T(8,128)(2,1)S(1)}, u32[]{:S(2)}, u32[]{:S(2)}) collective-permute-start(bf16[48,1024]{1,0:T(8,128)(2,1)S(1)} %shard_map.103), channel_id=1, source_target_pairs={{0,2},{1,3},{2,0},{3,1},{4,6},{5,7},{6,4},{7,5},{8,10},{9,11},{10,... | collective-permute-start | bytes 294920 | tf_op jit(solution)/shard_map/ppermute | solution.py:55
  44.0 6.5 %collective-permute-start.13 = (bf16[48,1024]{1,0:T(8,128)(2,1)S(1)}, bf16[48,1024]{1,0:T(8,128)(2,1)S(1)}, u32[]{:S(2)}, u32[]{:S(2)}) collective-permute-start(bf16[48,1024]{1,0:T(8,128)(2,1)S(1)} %add_convert_fusion.1), channel_id=1, source_target_pairs={{0,6},{1,7},{2,4},{3,5},{4,2},{5,3},{6,0},{7,1},{8,14},{9,15},{10,... | collective-permute-start | bytes 294920 | tf_op jit(solution)/shard_map/ppermute | solution.py:55
  55.2 7.3 %collective-permute-start.15 = (bf16[24,896]{1,0:T(8,128)(2,1)S(1)}, bf16[24,896]{1,0:T(8,128)(2,1)S(1)}, u32[]{:S(2)}, u32[]{:S(2)}) collective-permute-start(bf16[24,896]{1,0:T(8,128)(2,1)S(1)} %get-tuple-element.55), channel_id=1, source_target_pairs={{0,1},{1,0},{2,3},{3,2},{4,5},{5,4},{6,7},{7,6},{8,9},{9,8},{10,11... | collective-permute-start | bytes 129032 | tf_op jit(solution)/shard_map/ppermute | solution.py:55
  56.3 6.1 %collective-permute-start.16 = (bf16[24,896]{1,0:T(8,128)(2,1)S(1)}, bf16[24,896]{1,0:T(8,128)(2,1)S(1)}, u32[]{:S(2)}, u32[]{:S(2)}) collective-permute-start(bf16[24,896]{1,0:T(8,128)(2,1)S(1)} %get-tuple-element.56), channel_id=1, source_target_pairs={{0,16},{1,17},{2,18},{3,19},{4,20},{5,21},{6,22},{7,23},{8,24},{9,... | collective-permute-start | bytes 129032 | tf_op jit(solution)/shard_map/ppermute | solution.py:55
  57.3 5.2 %collective-permute-start.17 = (bf16[24,896]{1,0:T(8,128)(2,1)S(1)}, bf16[24,896]{1,0:T(8,128)(2,1)S(1)}, u32[]{:S(2)}, u32[]{:S(2)}) collective-permute-start(bf16[24,896]{1,0:T(8,128)(2,1)S(1)} %get-tuple-element.57), channel_id=1, source_target_pairs={{0,17},{1,16},{2,19},{3,18},{4,21},{5,20},{6,23},{7,22},{8,25},{9,... | collective-permute-start | bytes 129032 | tf_op jit(solution)/shard_map/ppermute | solution.py:55
  58.7 7.8 %collective-permute-start.19 = (bf16[2,48,800]{2,1,0:T(8,128)(2,1)S(1)}, bf16[2,48,800]{2,1,0:T(8,128)(2,1)S(1)}, u32[]{:S(2)}, u32[]{:S(2)}) collective-permute-start(bf16[2,48,800]{2,1,0:T(8,128)(2,1)S(1)} %pad_maximum_fusion), channel_id=1, source_target_pairs={{0,6},{1,7},{2,4},{3,5},{4,2},{5,3},{6,0},{7,1},{8,14},{9,15},{10,... | collective-permute-start | bytes 460808 | tf_op jit(solution)/shard_map/ppermute | solution.py:55
  62.5 5.5 %collective-permute-start.18 = (bf16[1,24,896]{2,1,0:T(8,128)(2,1)S(1)}, bf16[1,24,896]{2,1,0:T(8,128)(2,1)S(1)}, u32[]{:S(2)}, u32[]{:S(2)}) collective-permute-start(bf16[1,24,896]{2,1,0:T(8,128)(2,1)S(1)} %bitcast.20), channel_id=1, source_target_pairs={{0,2},{1,3},{2,0},{3,1},{4,6},{5,7},{6,4},{7,5},{8,10},{9,11},{10,... | collective-permute-start | bytes 129032 | tf_op jit(solution)/shard_map/ppermute | solution.py:55
  68.0 7.3 %collective-permute-start.22 = (bf16[2,24,896]{2,1,0:T(8,128)(2,1)S(1)}, bf16[2,24,896]{2,1,0:T(8,128)(2,1)S(1)}, u32[]{:S(2)}, u32[]{:S(2)}) collective-permute-start(bf16[2,24,896]{2,1,0:T(8,128)(2,1)S(1)} %pad_maximum_fusion.1.refs_0_), channel_id=1, source_target_pairs={{0,17},{1,16},{2,19},{3,18},{4,21},{5,20},{6,23},{7,22},{8,25},{9,... | collective-permute-start | bytes 258056 | tf_op jit(solution)/shard_map/ppermute | solution.py:55
  69.7 6.0 %collective-permute-start.21 = (bf16[2,24,896]{2,1,0:T(8,128)(2,1)S(1)}, bf16[2,24,896]{2,1,0:T(8,128)(2,1)S(1)}, u32[]{:S(2)}, u32[]{:S(2)}) collective-permute-start(bf16[2,24,896]{2,1,0:T(8,128)(2,1)S(1)} %pad_maximum_fusion.1.refs_0_), channel_id=1, source_target_pairs={{0,16},{1,17},{2,18},{3,19},{4,20},{5,21},{6,22},{7,23},{8,24},{9,... | collective-permute-start | bytes 258056 | tf_op jit(solution)/shard_map/ppermute | solution.py:55
  70.8 5.1 %collective-permute-start.20 = (bf16[2,24,896]{2,1,0:T(8,128)(2,1)S(1)}, bf16[2,24,896]{2,1,0:T(8,128)(2,1)S(1)}, u32[]{:S(2)}, u32[]{:S(2)}) collective-permute-start(bf16[2,24,896]{2,1,0:T(8,128)(2,1)S(1)} %pad_maximum_fusion.1.refs_0_), channel_id=1, source_target_pairs={{0,1},{1,0},{2,3},{3,2},{4,5},{5,4},{6,7},{7,6},{8,9},{9,8},{10,11... | collective-permute-start | bytes 258056 | tf_op jit(solution)/shard_map/ppermute | solution.py:55
  71.5 6.3 %collective-permute-start.27 = (bf16[2,24,896]{2,1,0:T(8,128)(2,1)S(1)}, bf16[2,24,896]{2,1,0:T(8,128)(2,1)S(1)}, u32[]{:S(2)}, u32[]{:S(2)}) collective-permute-start(bf16[2,24,896]{2,1,0:T(8,128)(2,1)S(1)} %pad_maximum_fusion.1.refs_0_), channel_id=1, source_target_pairs={{0,6},{1,7},{2,4},{3,5},{4,2},{5,3},{6,0},{7,1},{8,14},{9,15},{10,... | collective-permute-start | bytes 258056 | tf_op jit(solution)/shard_map/ppermute | solution.py:55
  75.2 5.3 %collective-permute-start.26 = (bf16[2,24,896]{2,1,0:T(8,128)(2,1)S(1)}, bf16[2,24,896]{2,1,0:T(8,128)(2,1)S(1)}, u32[]{:S(2)}, u32[]{:S(2)}) collective-permute-start(bf16[2,24,896]{2,1,0:T(8,128)(2,1)S(1)} %collective-permute-done.22.refs_3_), channel_id=1, source_target_pairs={{0,8},{1,9},{2,10},{3,11},{4,12},{5,13},{6,14},{7,15},{8,0},{9,1},... | collective-permute-start | bytes 258056 | tf_op jit(solution)/shard_map/ppermute | solution.py:55
  75.8 5.5 %collective-permute-start.25 = (bf16[2,24,896]{2,1,0:T(8,128)(2,1)S(1)}, bf16[2,24,896]{2,1,0:T(8,128)(2,1)S(1)}, u32[]{:S(2)}, u32[]{:S(2)}) collective-permute-start(bf16[2,24,896]{2,1,0:T(8,128)(2,1)S(1)} %collective-permute-done.21.refs_2_), channel_id=1, source_target_pairs={{0,8},{1,9},{2,10},{3,11},{4,12},{5,13},{6,14},{7,15},{8,0},{9,1},... | collective-permute-start | bytes 258056 | tf_op jit(solution)/shard_map/ppermute | solution.py:55
  75.8 5.5 %collective-permute-start.24 = (bf16[2,24,896]{2,1,0:T(8,128)(2,1)S(1)}, bf16[2,24,896]{2,1,0:T(8,128)(2,1)S(1)}, u32[]{:S(2)}, u32[]{:S(2)}) collective-permute-start(bf16[2,24,896]{2,1,0:T(8,128)(2,1)S(1)} %collective-permute-done.20.refs_1_), channel_id=1, source_target_pairs={{0,8},{1,9},{2,10},{3,11},{4,12},{5,13},{6,14},{7,15},{8,0},{9,1},... | collective-permute-start | bytes 258056 | tf_op jit(solution)/shard_map/ppermute | solution.py:55
  77.8 6.0 %collective-permute-start.30 = (bf16[2,24,896]{2,1,0:T(8,128)(2,1)S(1)}, bf16[2,24,896]{2,1,0:T(8,128)(2,1)S(1)}, u32[]{:S(2)}, u32[]{:S(2)}) collective-permute-start(bf16[2,24,896]{2,1,0:T(8,128)(2,1)S(1)} %collective-permute-done.27.refs_1_), channel_id=1, source_target_pairs={{0,17},{1,16},{2,19},{3,18},{4,21},{5,20},{6,23},{7,22},{8,25},{9,... | collective-permute-start | bytes 258056 | tf_op jit(solution)/shard_map/ppermute | solution.py:55
  79.5 4.5 %collective-permute-start.29 = (bf16[2,24,896]{2,1,0:T(8,128)(2,1)S(1)}, bf16[2,24,896]{2,1,0:T(8,128)(2,1)S(1)}, u32[]{:S(2)}, u32[]{:S(2)}) collective-permute-start(bf16[2,24,896]{2,1,0:T(8,128)(2,1)S(1)} %collective-permute-done.27.refs_1_), channel_id=1, source_target_pairs={{0,16},{1,17},{2,18},{3,19},{4,20},{5,21},{6,22},{7,23},{8,24},{9,... | collective-permute-start | bytes 258056 | tf_op jit(solution)/shard_map/ppermute | solution.py:55
  (24 other events, 230.5 us)

commit v4 on v3

--- a/solution.py
+++ b/solution.py
@@ -386,26 +386,32 @@
     )(at, *([] if fresh else [result]), *pieces, hidden)
 
 
-def row_masks(g):
+def row_steps(g):
     if g.rows & (g.rows - 1):
         return None
+    return [1 << n for n in range(g.rows.bit_length() - 1)]
+
+
+def row_masks(g):
+    steps = row_steps(g)
+    if steps is None:
+        return None
     masks = [0]
-    while len(masks) < g.rows:
-        masks = masks + [m ^ (2 * len(masks) - 1) for m in masks]
+    for step in steps:
+        masks = masks + [m ^ step for m in masks]
     return masks
 
 
 def sum_rows(g, value, beside):
-    if g.rows & (g.rows - 1):
+    steps = row_steps(g)
+    if steps is None:
         return lax.psum(value.astype(F32), "row").astype(BF), beside
-    beside, step, n = list(beside), 1, 0
-    while step < g.rows:
-        mask = 2 * step - 1
-        other = g.send(value, row=lambda r: r ^ mask)
+    beside = list(beside)
+    for n, step in enumerate(steps):
+        other = g.send(value, row=lambda r: r ^ step)
         if n < len(beside):
             other, beside[n] = lax.optimization_barrier((other, beside[n]))
         value = (value.astype(F32) + other.astype(F32)).astype(BF)
-        step, n = 2 * step, n + 1
     return value, beside
 
 
@@ -422,29 +428,30 @@
     units = w_down.shape[0]
     tall = own
     share = cdiv(cdiv(units, g.cols), LANES) * LANES
-    doubling = not g.rows & (g.rows - 1)
+    steps = row_steps(g)
+    doubling = steps is not None
 
     def to_chips(pieces):
-        return [g.send(p, dx=dx, dy=dy) for p, (dx, dy) in zip(pieces, g.shifts[1:])]
+        out = []
+        for p, (dx, dy) in zip(pieces, g.shifts[1:]):
+            out.append(g.send(p, dx=dx, dy=dy))
+        return out
 
     saved = enc_hidden[None]
     keep, give = down_matmul(g, at, out_grad, w_down, own, tall, share)
     total, *pieces = core_sum(g, at, keep, g.swap(give), tall)
     saved_parts = [saved]
-    if doubling and g.rows > 1:
+    if steps:
         (mine,) = ordered(total, saved)
-        saved_parts.append(g.send(mine, row=lambda r: r ^ 1))
+        saved_parts.append(g.send(mine, row=lambda r: r ^ steps[0]))
         total, *pieces = lax.optimization_barrier((total, *pieces))
     arrived = to_chips(pieces)
-    if doubling and g.rows > 1:
+    if steps:
         saved_parts[1], *arrived = lax.optimization_barrier((saved_parts[1], *arrived))
     grads = gate_grads(g, at, total, arrived, gate_pre, up_pre)
-    step = 2
-    while doubling and step < g.rows:
+    for step in steps[1:] if steps else ():
         (mine,) = ordered(grads, jnp.concatenate(saved_parts))
-        mask = 2 * step - 1
-        saved_parts.append(g.send(mine, row=lambda r: r ^ mask))
-        step *= 2
+        saved_parts.append(g.send(mine, row=lambda r: r ^ step))
     pieces = [grads] + to_chips([grads] * (g.chips - 1))
     swapped = [g.swap(grads)]
     pieces = pieces + swapped + [g.swap(p) for p in pieces[1:]]
@@ -453,11 +460,11 @@
     image_grad = input_matmul(g, at, pieces, route.reshape(1, slots), img_count, w_gate.T, w_up.T, own)
 
     features = w_proj.shape[0] // SHUF
-    steps = cdiv(cdiv(features, g.rows), LANES)
+    lanes = cdiv(cdiv(features, g.rows), LANES)
     piece = SHUF * half // g.chips
     image_grad, late = lax.optimization_barrier((image_grad, at))
-    early = steps // 2 + 1
-    w_parts = [fetch_rows(late, w_proj, steps, s, n) for s, n in ((0, early), (early, steps - early)) if n]
+    early = lanes // 2 + 1
+    w_parts = [fetch_rows(late, w_proj, lanes, s, n) for s, n in ((0, early), (early, lanes - early)) if n]
     image_grad, w_parts = sum_rows(g, image_grad, w_parts)
 
     keep, give = shuffle_matmul(g, image_grad, w_parts)
@@ -471,15 +478,13 @@
     if not doubling:
         batches = [lax.all_gather(patch_grad, "row", axis=0, tiled=False)]
     else:
-        stack, batches, step = patch_grad[None], [], 1
-        while step < g.rows:
-            mask = 2 * step - 1
-            other = g.send(stack, row=lambda r: r ^ mask)
-            if step == 1:
+        stack, batches = patch_grad[None], []
+        for n, step in enumerate(steps):
+            other = g.send(stack, row=lambda r: r ^ step)
+            if n == 0:
                 other, hidden = lax.optimization_barrier((other, hidden))
             stack = jnp.concatenate([stack, other])
-            batches.append(stack if step == 1 else other)
-            step *= 2
+            batches.append(stack if n == 0 else other)
         batches = batches or [stack]
     result, first = None, 0
     held = []

time: 89.7 us -> 91.6 us (1.021)
  waiting for transfers between devices: 21.6 us -> 32.3 us
  starting transfers between devices: 37.2 us -> 28.5 us
    ppermute x35, waiting for transfers between devices: 21.6 us -> 32.3 us  [send(): return lax.ppermute(value, AXES, pairs)]
    ppermute x35, starting transfers between devices: 37.2 us -> 28.5 us  [send(): return lax.ppermute(value, AXES, pairs)]
  transfers between devices with their start and end apart: 35 -> 35, of which waited for: 17 -> 21; matrix products, arithmetic and copies ran while one was open for 0% -> 0% of each run, Pallas kernels for 10% -> 10%
where the time goes in v4:
time: 91.6 us; the launch traced here: 91.4 us
  waiting for transfers between devices  32.3 us (35%)
  Pallas kernels  29.8 us (33%)
  starting transfers between devices  28.5 us (31%)
    ppermute x35, waiting for transfers between devices, send(): return lax.ppermute(value, AXES, pairs)  32.3 us
    ppermute x35, starting transfers between devices, send(): return lax.ppermute(value, AXES, pairs)  28.5 us
    pallas_call x9, Pallas kernels, local_call(): pl.pallas_call(kernel, out_shape=out_shape, in_specs=in_specs, out_specs=...  25 us
    pallas_call x2, Pallas kernels, weight_grad(): pl.pallas_call(kernel, out_shape=jax.ShapeDtypeStruct((units, features),...  4.84 us
  transfers between devices with their start and end apart: 35, of which 21 were waited for; matrix products, arithmetic and copies ran while one was open for 0% of the time, Pallas kernels for 10%

profile of v4, /device:TPU:0, one launch (start us, length us, event | category | flops | bytes accessed | tf_op | source)
XLA Modules:
  0.0 91.4 jit_solution(12770489546534757658)
XLA Ops:
  0.1 7.9 %shard_map.100 = (bf16[2,24,3712]{2,1,0:T(8,128)(2,1)S(1)}, bf16[2,24,3712]{2,1,0:T(8,128)(2,1)S(1)}) custom-call(s32[4]{0:T(128)S(1)} %pad_add_fusion.pos, bf16[48,1024]{1,0:T(8,128)(2,1)} %grad_hbm.1, bf16[7392,1024]{1,0:T(8,128)(2,1)} %w_ref.3), custom_call_target="tpu_custom_call" | custom-call | flops 726663168 | bytes 15138816 | tf_op jit(solution)/shard_map/pallas_call | solution.py:72
  10.5 2.9 %collective-permute-start.2 = (bf16[24,1920]{1,0:T(8,128)(2,1)S(1)}, bf16[24,1920]{1,0:T(8,128)(2,1)S(1)}, u32[]{:S(2)}, u32[]{:S(2)}) collective-permute-start(bf16[24,1920]{1,0:T(8,128)(2,1)S(1)} %get-tuple-element.40), channel_id=1, source_target_pairs={{0,1},{1,0},{2,3},{3,2},{4,5},{5,4},{6,7},{7,6},{8,9},{9,8},{10,11... | collective-permute-start | bytes 276488 | tf_op jit(solution)/shard_map/ppermute | solution.py:55
  13.5 1.5 %collective-permute-start.3 = (bf16[24,1920]{1,0:T(8,128)(2,1)S(1)}, bf16[24,1920]{1,0:T(8,128)(2,1)S(1)}, u32[]{:S(2)}, u32[]{:S(2)}) collective-permute-start(bf16[24,1920]{1,0:T(8,128)(2,1)S(1)} %get-tuple-element.41), channel_id=1, source_target_pairs={{0,16},{1,17},{2,18},{3,19},{4,20},{5,21},{6,22},{7,23},{8,24},{9,... | collective-permute-start | bytes 276488 | tf_op jit(solution)/shard_map/ppermute | solution.py:55
  15.0 2.0 %collective-permute-start.1 = (bf16[1,48,800]{2,1,0:T(8,128)(2,1)S(1)}, bf16[1,48,800]{2,1,0:T(8,128)(2,1)S(1)}, u32[]{:S(2)}, u32[]{:S(2)}) collective-permute-start(bf16[1,48,800]{2,1,0:T(8,128)(2,1)S(1)} %bitcast.16), channel_id=1, source_target_pairs={{0,2},{1,3},{2,0},{3,1},{4,6},{5,7},{6,4},{7,5},{8,10},{9,11},{10,... | collective-permute-start | bytes 230408 | tf_op jit(solution)/shard_map/ppermute | solution.py:55
  17.1 2.5 %collective-permute-done.1.refs_1_ = bf16[1,48,800]{2,1,0:T(8,128)(2,1)S(1)} collective-permute-done((bf16[1,48,800]{2,1,0:T(8,128)(2,1)S(1)}, bf16[1,48,800]{2,1,0:T(8,128)(2,1)S(1)}, u32[]{:S(2)}, u32[]{:S(2)}) %collective-permute-start.1) | collective-permute-done | bytes 76832 | tf_op jit(solution)/shard_map/ppermute | solution.py:55
  21.3 2.1 %collective-permute-start.7 = (bf16[24,3712]{1,0:T(8,128)(2,1)S(1)}, bf16[24,3712]{1,0:T(8,128)(2,1)S(1)}, u32[]{:S(2)}, u32[]{:S(2)}) collective-permute-start(bf16[24,3712]{1,0:T(8,128)(2,1)S(1)} %shard_map.102.refs_0_), channel_id=1, source_target_pairs={{0,17},{1,16},{2,19},{3,18},{4,21},{5,20},{6,23},{7,22},{8,25},{9,... | collective-permute-start | bytes 534536 | tf_op jit(solution)/shard_map/ppermute | solution.py:55
  24.8 4.2 %collective-permute-done.7.refs_3_ = bf16[24,3712]{1,0:T(8,128)(2,1)S(1)} collective-permute-done((bf16[24,3712]{1,0:T(8,128)(2,1)S(1)}, bf16[24,3712]{1,0:T(8,128)(2,1)S(1)}, u32[]{:S(2)}, u32[]{:S(2)}) %collective-permute-start.7) | collective-permute-done | bytes 178208 | tf_op jit(solution)/shard_map/ppermute | solution.py:55
  29.1 2.1 %collective-permute-done.6.refs_2_ = bf16[24,3712]{1,0:T(8,128)(2,1)S(1)} collective-permute-done((bf16[24,3712]{1,0:T(8,128)(2,1)S(1)}, bf16[24,3712]{1,0:T(8,128)(2,1)S(1)}, u32[]{:S(2)}, u32[]{:S(2)}) %collective-permute-start.6) | collective-permute-done | bytes 178208 | tf_op jit(solution)/shard_map/ppermute | solution.py:55
  33.0 6.0 %shard_map.103 = bf16[48,1024]{1,0:T(8,128)(2,1)S(1)} custom-call(s32[4]{0:T(128)S(1)} %pad_add_fusion.pos, s32[4]{0:T(128)S(1)} %copy-done.1, bf16[24,3712]{1,0:T(8,128)(2,1)S(1)} %shard_map.102.refs_0_, bf16[24,3712]{1,0:T(8,128)(2,1)S(1)} %collective-permute-done.5.refs_1_, bf16[24,3712]{1,0:T(8,128)(2,1)S(1)} %collective-permute-done.6.refs_2_, ...), custom_call_target="tpu_custom_call" | custom-call | flops 2906652672 | bytes 30277632 | tf_op jit(solution)/shard_map/pallas_call | solution.py:72
  39.0 1.6 %collective-permute-start.12 = (bf16[48,1024]{1,0:T(8,128)(2,1)S(1)}, bf16[48,1024]{1,0:T(8,128)(2,1)S(1)}, u32[]{:S(2)}, u32[]{:S(2)}) collective-permute-start(bf16[48,1024]{1,0:T(8,128)(2,1)S(1)} %shard_map.103), channel_id=1, source_target_pairs={{0,2},{1,3},{2,0},{3,1},{4,6},{5,7},{6,4},{7,5},{8,10},{9,11},{10,... | collective-permute-start | bytes 294920 | tf_op jit(solution)/shard_map/ppermute | solution.py:55
  40.6 2.8 %shard_map.104.refs_0_ = bf16[4,512,1024]{2,1,0:T(8,128)(2,1)S(1)} custom-call(s32[4]{0:T(128)S(1)} %pad_add_fusion.pos, bf16[12800,1024]{1,0:T(8,128)(2,1)} %w_ref.5), custom_call_target="tpu_custom_call" | custom-call | bytes 4194304 | tf_op jit(solution)/shard_map/pallas_call | solution.py:72
  44.0 2.7 %collective-permute-start.13 = (bf16[48,1024]{1,0:T(8,128)(2,1)S(1)}, bf16[48,1024]{1,0:T(8,128)(2,1)S(1)}, u32[]{:S(2)}, u32[]{:S(2)}) collective-permute-start(bf16[48,1024]{1,0:T(8,128)(2,1)S(1)} %add_convert_fusion.1), channel_id=1, source_target_pairs={{0,4},{1,5},{2,6},{3,7},{4,0},{5,1},{6,2},{7,3},{8,12},{9,13},{10,... | collective-permute-start | bytes 294920 | tf_op jit(solution)/shard_map/ppermute | solution.py:55
  46.7 2.4 %shard_map.105.refs_1_ = bf16[3,512,1024]{2,1,0:T(8,128)(2,1)S(1)} custom-call(s32[4]{0:T(128)S(1)} %pad_add_fusion.pos, bf16[12800,1024]{1,0:T(8,128)(2,1)} %w_ref.5), custom_call_target="tpu_custom_call" | custom-call | bytes 3145728 | tf_op jit(solution)/shard_map/pallas_call | solution.py:72
  49.1 2.1 %collective-permute-done.13 = bf16[48,1024]{1,0:T(8,128)(2,1)S(1)} collective-permute-done((bf16[48,1024]{1,0:T(8,128)(2,1)S(1)}, bf16[48,1024]{1,0:T(8,128)(2,1)S(1)}, u32[]{:S(2)}, u32[]{:S(2)}) %collective-permute-start.13) | collective-permute-done | bytes 98336 | tf_op jit(solution)/shard_map/ppermute | solution.py:55
  51.2 2.5 %shard_map.106 = (bf16[4,24,896]{2,1,0:T(8,128)(2,1)S(1)}, bf16[4,24,896]{2,1,0:T(8,128)(2,1)S(1)}) custom-call(bf16[48,1024]{1,0:T(8,128)(2,1)S(1)} %add_convert_fusion.grad_ref, bf16[4,512,1024]{2,1,0:T(8,128)(2,1)S(1)} %shard_map.104.refs_0_, bf16[3,512,1024]{2,1,0:T(8,128)(2,1)S(1)} %shard_map.105.refs_1_), custom_call_target="tpu_custom_call" | custom-call | flops 352321536 | bytes 7340032 | tf_op jit(solution)/shard_map/pallas_call | solution.py:72
  58.0 1.5 %collective-permute-start.17 = (bf16[24,896]{1,0:T(8,128)(2,1)S(1)}, bf16[24,896]{1,0:T(8,128)(2,1)S(1)}, u32[]{:S(2)}, u32[]{:S(2)}) collective-permute-start(bf16[24,896]{1,0:T(8,128)(2,1)S(1)} %get-tuple-element.57), channel_id=1, source_target_pairs={{0,17},{1,16},{2,19},{3,18},{4,21},{5,20},{6,23},{7,22},{8,25},{9,... | collective-permute-start | bytes 129032 | tf_op jit(solution)/shard_map/ppermute | solution.py:55
  61.4 1.5 %collective-permute-done.17 = bf16[24,896]{1,0:T(8,128)(2,1)S(1)} collective-permute-done((bf16[24,896]{1,0:T(8,128)(2,1)S(1)}, bf16[24,896]{1,0:T(8,128)(2,1)S(1)}, u32[]{:S(2)}, u32[]{:S(2)}) %collective-permute-start.17) | collective-permute-done | bytes 43040 | tf_op jit(solution)/shard_map/ppermute | solution.py:55
  63.7 6.0 %collective-permute-done.19.refs_2_ = bf16[2,48,800]{2,1,0:T(8,128)(2,1)S(1)} collective-permute-done((bf16[2,48,800]{2,1,0:T(8,128)(2,1)S(1)}, bf16[2,48,800]{2,1,0:T(8,128)(2,1)S(1)}, u32[]{:S(2)}, u32[]{:S(2)}) %collective-permute-start.19) | collective-permute-done | bytes 153632 | tf_op jit(solution)/shard_map/ppermute | solution.py:55
  71.1 1.5 %collective-permute-start.22 = (bf16[2,24,896]{2,1,0:T(8,128)(2,1)S(1)}, bf16[2,24,896]{2,1,0:T(8,128)(2,1)S(1)}, u32[]{:S(2)}, u32[]{:S(2)}) collective-permute-start(bf16[2,24,896]{2,1,0:T(8,128)(2,1)S(1)} %pad_maximum_fusion.1.refs_0_), channel_id=1, source_target_pairs={{0,17},{1,16},{2,19},{3,18},{4,21},{5,20},{6,23},{7,22},{8,25},{9,... | collective-permute-start | bytes 258056 | tf_op jit(solution)/shard_map/ppermute | solution.py:55
  74.6 2.0 %collective-permute-done.22.refs_3_ = bf16[2,24,896]{2,1,0:T(8,128)(2,1)S(1)} collective-permute-done((bf16[2,24,896]{2,1,0:T(8,128)(2,1)S(1)}, bf16[2,24,896]{2,1,0:T(8,128)(2,1)S(1)}, u32[]{:S(2)}, u32[]{:S(2)}) %collective-permute-start.22) | collective-permute-done | bytes 86048 | tf_op jit(solution)/shard_map/ppermute | solution.py:55
  78.1 2.0 %collective-permute-done.27.refs_1_ = bf16[2,24,896]{2,1,0:T(8,128)(2,1)S(1)} collective-permute-done((bf16[2,24,896]{2,1,0:T(8,128)(2,1)S(1)}, bf16[2,24,896]{2,1,0:T(8,128)(2,1)S(1)}, u32[]{:S(2)}, u32[]{:S(2)}) %collective-permute-start.27) | collective-permute-done | bytes 86048 | tf_op jit(solution)/shard_map/ppermute | solution.py:55
  80.1 1.5 %collective-permute-start.30 = (bf16[2,24,896]{2,1,0:T(8,128)(2,1)S(1)}, bf16[2,24,896]{2,1,0:T(8,128)(2,1)S(1)}, u32[]{:S(2)}, u32[]{:S(2)}) collective-permute-start(bf16[2,24,896]{2,1,0:T(8,128)(2,1)S(1)} %collective-permute-done.27.refs_1_), channel_id=1, source_target_pairs={{0,17},{1,16},{2,19},{3,18},{4,21},{5,20},{6,23},{7,22},{8,25},{9,... | collective-permute-start | bytes 258056 | tf_op jit(solution)/shard_map/ppermute | solution.py:55
  83.6 2.5 %weight_grad.2.refs_0_ = bf16[800,3200]{1,0:T(8,128)(2,1)} custom-call(s32[4]{0:T(128)S(1)} %pad_add_fusion.pos, bf16[2,24,896]{2,1,0:T(8,128)(2,1)S(1)} %pad_maximum_fusion.1.refs_0_, bf16[2,24,896]{2,1,0:T(8,128)(2,1)S(1)} %collective-permute-done.20.refs_1_, bf16[2,24,896]{2,1,0:T(8,128)(2,1)S(1)} %collective-permute-done.21.refs_2_, ...), custom_call_target="tpu_custom_call" | custom-call | flops 550502400 | bytes 2867200 | tf_op jit(solution)/shard_map/weight_grad/pallas_call | solution.py:370
  88.9 2.3 %weight_grad.3 = bf16[800,3200]{1,0:T(8,128)(2,1)} custom-call(s32[4]{0:T(128)S(1)} %pad_add_fusion.pos, bf16[800,3200]{1,0:T(8,128)(2,1)} %weight_grad.2.refs_0_, bf16[2,24,896]{2,1,0:T(8,128)(2,1)S(1)} %collective-permute-done.27.refs_1_, bf16[2,24,896]{2,1,0:T(8,128)(2,1)S(1)} %collective-permute-done.28.refs_2_, ...), custom_call_target="tpu_custom_call", output_to_operand_aliasing={{}: (1, {})} | custom-call | flops 550502400 | bytes 2867200 | tf_op jit(solution)/shard_map/weight_grad/pallas_call | solution.py:370
  (91 shorter events, 24.8 us)
Async XLA Ops:
  10.5 9.0 %collective-permute-start.2 = (bf16[24,1920]{1,0:T(8,128)(2,1)S(1)}, bf16[24,1920]{1,0:T(8,128)(2,1)S(1)}, u32[]{:S(2)}, u32[]{:S(2)}) collective-permute-start(bf16[24,1920]{1,0:T(8,128)(2,1)S(1)} %get-tuple-element.40), channel_id=1, source_target_pairs={{0,1},{1,0},{2,3},{3,2},{4,5},{5,4},{6,7},{7,6},{8,9},{9,8},{10,11... | collective-permute-start | bytes 276488 | tf_op jit(solution)/shard_map/ppermute | solution.py:55
  13.5 6.1 %collective-permute-start.3 = (bf16[24,1920]{1,0:T(8,128)(2,1)S(1)}, bf16[24,1920]{1,0:T(8,128)(2,1)S(1)}, u32[]{:S(2)}, u32[]{:S(2)}) collective-permute-start(bf16[24,1920]{1,0:T(8,128)(2,1)S(1)} %get-tuple-element.41), channel_id=1, source_target_pairs={{0,16},{1,17},{2,18},{3,19},{4,20},{5,21},{6,22},{7,23},{8,24},{9,... | collective-permute-start | bytes 276488 | tf_op jit(solution)/shard_map/ppermute | solution.py:55
  15.0 5.5 %collective-permute-start.4 = (bf16[24,1920]{1,0:T(8,128)(2,1)S(1)}, bf16[24,1920]{1,0:T(8,128)(2,1)S(1)}, u32[]{:S(2)}, u32[]{:S(2)}) collective-permute-start(bf16[24,1920]{1,0:T(8,128)(2,1)S(1)} %get-tuple-element.42), channel_id=1, source_target_pairs={{0,17},{1,16},{2,19},{3,18},{4,21},{5,20},{6,23},{7,22},{8,25},{9,... | collective-permute-start | bytes 276488 | tf_op jit(solution)/shard_map/ppermute | solution.py:55
  15.0 4.5 %collective-permute-start.1 = (bf16[1,48,800]{2,1,0:T(8,128)(2,1)S(1)}, bf16[1,48,800]{2,1,0:T(8,128)(2,1)S(1)}, u32[]{:S(2)}, u32[]{:S(2)}) collective-permute-start(bf16[1,48,800]{2,1,0:T(8,128)(2,1)S(1)} %bitcast.16), channel_id=1, source_target_pairs={{0,2},{1,3},{2,0},{3,1},{4,6},{5,7},{6,4},{7,5},{8,10},{9,11},{10,... | collective-permute-start | bytes 230408 | tf_op jit(solution)/shard_map/ppermute | solution.py:55
  21.3 7.8 %collective-permute-start.7 = (bf16[24,3712]{1,0:T(8,128)(2,1)S(1)}, bf16[24,3712]{1,0:T(8,128)(2,1)S(1)}, u32[]{:S(2)}, u32[]{:S(2)}) collective-permute-start(bf16[24,3712]{1,0:T(8,128)(2,1)S(1)} %shard_map.102.refs_0_), channel_id=1, source_target_pairs={{0,17},{1,16},{2,19},{3,18},{4,21},{5,20},{6,23},{7,22},{8,25},{9,... | collective-permute-start | bytes 534536 | tf_op jit(solution)/shard_map/ppermute | solution.py:55
  23.3 7.9 %collective-permute-start.6 = (bf16[24,3712]{1,0:T(8,128)(2,1)S(1)}, bf16[24,3712]{1,0:T(8,128)(2,1)S(1)}, u32[]{:S(2)}, u32[]{:S(2)}) collective-permute-start(bf16[24,3712]{1,0:T(8,128)(2,1)S(1)} %shard_map.102.refs_0_), channel_id=1, source_target_pairs={{0,16},{1,17},{2,18},{3,19},{4,20},{5,21},{6,22},{7,23},{8,24},{9,... | collective-permute-start | bytes 534536 | tf_op jit(solution)/shard_map/ppermute | solution.py:55
  23.9 7.4 %collective-permute-start.5 = (bf16[24,3712]{1,0:T(8,128)(2,1)S(1)}, bf16[24,3712]{1,0:T(8,128)(2,1)S(1)}, u32[]{:S(2)}, u32[]{:S(2)}) collective-permute-start(bf16[24,3712]{1,0:T(8,128)(2,1)S(1)} %shard_map.102.refs_0_), channel_id=1, source_target_pairs={{0,1},{1,0},{2,3},{3,2},{4,5},{5,4},{6,7},{7,6},{8,9},{9,8},{10,11... | collective-permute-start | bytes 534536 | tf_op jit(solution)/shard_map/ppermute | solution.py:55
  24.8 6.9 %collective-permute-start.8 = (bf16[24,3712]{1,0:T(8,128)(2,1)S(1)}, bf16[24,3712]{1,0:T(8,128)(2,1)S(1)}, u32[]{:S(2)}, u32[]{:S(2)}) collective-permute-start(bf16[24,3712]{1,0:T(8,128)(2,1)S(1)} %shard_map.102.refs_0_), channel_id=1, source_target_pairs={{0,8},{1,9},{2,10},{3,11},{4,12},{5,13},{6,14},{7,15},{8,0},{9,1},... | collective-permute-start | bytes 534536 | tf_op jit(solution)/shard_map/ppermute | solution.py:55
  39.0 5.0 %collective-permute-start.12 = (bf16[48,1024]{1,0:T(8,128)(2,1)S(1)}, bf16[48,1024]{1,0:T(8,128)(2,1)S(1)}, u32[]{:S(2)}, u32[]{:S(2)}) collective-permute-start(bf16[48,1024]{1,0:T(8,128)(2,1)S(1)} %shard_map.103), channel_id=1, source_target_pairs={{0,2},{1,3},{2,0},{3,1},{4,6},{5,7},{6,4},{7,5},{8,10},{9,11},{10,... | collective-permute-start | bytes 294920 | tf_op jit(solution)/shard_map/ppermute | solution.py:55
  44.0 7.2 %collective-permute-start.13 = (bf16[48,1024]{1,0:T(8,128)(2,1)S(1)}, bf16[48,1024]{1,0:T(8,128)(2,1)S(1)}, u32[]{:S(2)}, u32[]{:S(2)}) collective-permute-start(bf16[48,1024]{1,0:T(8,128)(2,1)S(1)} %add_convert_fusion.1), channel_id=1, source_target_pairs={{0,4},{1,5},{2,6},{3,7},{4,0},{5,1},{6,2},{7,3},{8,12},{9,13},{10,... | collective-permute-start | bytes 294920 | tf_op jit(solution)/shard_map/ppermute | solution.py:55
  55.9 4.7 %collective-permute-start.15 = (bf16[24,896]{1,0:T(8,128)(2,1)S(1)}, bf16[24,896]{1,0:T(8,128)(2,1)S(1)}, u32[]{:S(2)}, u32[]{:S(2)}) collective-permute-start(bf16[24,896]{1,0:T(8,128)(2,1)S(1)} %get-tuple-element.55), channel_id=1, source_target_pairs={{0,1},{1,0},{2,3},{3,2},{4,5},{5,4},{6,7},{7,6},{8,9},{9,8},{10,11... | collective-permute-start | bytes 129032 | tf_op jit(solution)/shard_map/ppermute | solution.py:55
  58.0 4.9 %collective-permute-start.17 = (bf16[24,896]{1,0:T(8,128)(2,1)S(1)}, bf16[24,896]{1,0:T(8,128)(2,1)S(1)}, u32[]{:S(2)}, u32[]{:S(2)}) collective-permute-start(bf16[24,896]{1,0:T(8,128)(2,1)S(1)} %get-tuple-element.57), channel_id=1, source_target_pairs={{0,17},{1,16},{2,19},{3,18},{4,21},{5,20},{6,23},{7,22},{8,25},{9,... | collective-permute-start | bytes 129032 | tf_op jit(solution)/shard_map/ppermute | solution.py:55
  59.4 10.2 %collective-permute-start.19 = (bf16[2,48,800]{2,1,0:T(8,128)(2,1)S(1)}, bf16[2,48,800]{2,1,0:T(8,128)(2,1)S(1)}, u32[]{:S(2)}, u32[]{:S(2)}) collective-permute-start(bf16[2,48,800]{2,1,0:T(8,128)(2,1)S(1)} %pad_maximum_fusion), channel_id=1, source_target_pairs={{0,4},{1,5},{2,6},{3,7},{4,0},{5,1},{6,2},{7,3},{8,12},{9,13},{10,... | collective-permute-start | bytes 460808 | tf_op jit(solution)/shard_map/ppermute | solution.py:55
  62.9 8.1 %collective-permute-start.18 = (bf16[1,24,896]{2,1,0:T(8,128)(2,1)S(1)}, bf16[1,24,896]{2,1,0:T(8,128)(2,1)S(1)}, u32[]{:S(2)}, u32[]{:S(2)}) collective-permute-start(bf16[1,24,896]{2,1,0:T(8,128)(2,1)S(1)} %bitcast.20), channel_id=1, source_target_pairs={{0,2},{1,3},{2,0},{3,1},{4,6},{5,7},{6,4},{7,5},{8,10},{9,11},{10,... | collective-permute-start | bytes 129032 | tf_op jit(solution)/shard_map/ppermute | solution.py:55
  71.1 5.6 %collective-permute-start.22 = (bf16[2,24,896]{2,1,0:T(8,128)(2,1)S(1)}, bf16[2,24,896]{2,1,0:T(8,128)(2,1)S(1)}, u32[]{:S(2)}, u32[]{:S(2)}) collective-permute-start(bf16[2,24,896]{2,1,0:T(8,128)(2,1)S(1)} %pad_maximum_fusion.1.refs_0_), channel_id=1, source_target_pairs={{0,17},{1,16},{2,19},{3,18},{4,21},{5,20},{6,23},{7,22},{8,25},{9,... | collective-permute-start | bytes 258056 | tf_op jit(solution)/shard_map/ppermute | solution.py:55
  72.6 4.5 %collective-permute-start.21 = (bf16[2,24,896]{2,1,0:T(8,128)(2,1)S(1)}, bf16[2,24,896]{2,1,0:T(8,128)(2,1)S(1)}, u32[]{:S(2)}, u32[]{:S(2)}) collective-permute-start(bf16[2,24,896]{2,1,0:T(8,128)(2,1)S(1)} %pad_maximum_fusion.1.refs_0_), channel_id=1, source_target_pairs={{0,16},{1,17},{2,18},{3,19},{4,20},{5,21},{6,22},{7,23},{8,24},{9,... | collective-permute-start | bytes 258056 | tf_op jit(solution)/shard_map/ppermute | solution.py:55
  74.6 5.5 %collective-permute-start.27 = (bf16[2,24,896]{2,1,0:T(8,128)(2,1)S(1)}, bf16[2,24,896]{2,1,0:T(8,128)(2,1)S(1)}, u32[]{:S(2)}, u32[]{:S(2)}) collective-permute-start(bf16[2,24,896]{2,1,0:T(8,128)(2,1)S(1)} %pad_maximum_fusion.1.refs_0_), channel_id=1, source_target_pairs={{0,4},{1,5},{2,6},{3,7},{4,0},{5,1},{6,2},{7,3},{8,12},{9,13},{10,... | collective-permute-start | bytes 258056 | tf_op jit(solution)/shard_map/ppermute | solution.py:55
  74.6 7.0 %collective-permute-start.23 = (bf16[2,24,896]{2,1,0:T(8,128)(2,1)S(1)}, bf16[2,24,896]{2,1,0:T(8,128)(2,1)S(1)}, u32[]{:S(2)}, u32[]{:S(2)}) collective-permute-start(bf16[2,24,896]{2,1,0:T(8,128)(2,1)S(1)} %pad_maximum_fusion.1.refs_0_), channel_id=1, source_target_pairs={{0,8},{1,9},{2,10},{3,11},{4,12},{5,13},{6,14},{7,15},{8,0},{9,1},... | collective-permute-start | bytes 258056 | tf_op jit(solution)/shard_map/ppermute | solution.py:55
  76.6 6.0 %collective-permute-start.26 = (bf16[2,24,896]{2,1,0:T(8,128)(2,1)S(1)}, bf16[2,24,896]{2,1,0:T(8,128)(2,1)S(1)}, u32[]{:S(2)}, u32[]{:S(2)}) collective-permute-start(bf16[2,24,896]{2,1,0:T(8,128)(2,1)S(1)} %collective-permute-done.22.refs_3_), channel_id=1, source_target_pairs={{0,8},{1,9},{2,10},{3,11},{4,12},{5,13},{6,14},{7,15},{8,0},{9,1},... | collective-permute-start | bytes 258056 | tf_op jit(solution)/shard_map/ppermute | solution.py:55
  77.1 6.5 %collective-permute-start.25 = (bf16[2,24,896]{2,1,0:T(8,128)(2,1)S(1)}, bf16[2,24,896]{2,1,0:T(8,128)(2,1)S(1)}, u32[]{:S(2)}, u32[]{:S(2)}) collective-permute-start(bf16[2,24,896]{2,1,0:T(8,128)(2,1)S(1)} %collective-permute-done.21.refs_2_), channel_id=1, source_target_pairs={{0,8},{1,9},{2,10},{3,11},{4,12},{5,13},{6,14},{7,15},{8,0},{9,1},... | collective-permute-start | bytes 258056 | tf_op jit(solution)/shard_map/ppermute | solution.py:55
  78.1 5.5 %collective-permute-start.24 = (bf16[2,24,896]{2,1,0:T(8,128)(2,1)S(1)}, bf16[2,24,896]{2,1,0:T(8,128)(2,1)S(1)}, u32[]{:S(2)}, u32[]{:S(2)}) collective-permute-start(bf16[2,24,896]{2,1,0:T(8,128)(2,1)S(1)} %collective-permute-done.20.refs_1_), channel_id=1, source_target_pairs={{0,8},{1,9},{2,10},{3,11},{4,12},{5,13},{6,14},{7,15},{8,0},{9,1},... | collective-permute-start | bytes 258056 | tf_op jit(solution)/shard_map/ppermute | solution.py:55
  80.1 6.0 %collective-permute-start.30 = (bf16[2,24,896]{2,1,0:T(8,128)(2,1)S(1)}, bf16[2,24,896]{2,1,0:T(8,128)(2,1)S(1)}, u32[]{:S(2)}, u32[]{:S(2)}) collective-permute-start(bf16[2,24,896]{2,1,0:T(8,128)(2,1)S(1)} %collective-permute-done.27.refs_1_), channel_id=1, source_target_pairs={{0,17},{1,16},{2,19},{3,18},{4,21},{5,20},{6,23},{7,22},{8,25},{9,... | collective-permute-start | bytes 258056 | tf_op jit(solution)/shard_map/ppermute | solution.py:55
  81.6 4.6 %collective-permute-start.29 = (bf16[2,24,896]{2,1,0:T(8,128)(2,1)S(1)}, bf16[2,24,896]{2,1,0:T(8,128)(2,1)S(1)}, u32[]{:S(2)}, u32[]{:S(2)}) collective-permute-start(bf16[2,24,896]{2,1,0:T(8,128)(2,1)S(1)} %collective-permute-done.27.refs_1_), channel_id=1, source_target_pairs={{0,16},{1,17},{2,18},{3,19},{4,20},{5,21},{6,22},{7,23},{8,24},{9,... | collective-permute-start | bytes 258056 | tf_op jit(solution)/shard_map/ppermute | solution.py:55
  82.6 4.5 %collective-permute-start.28 = (bf16[2,24,896]{2,1,0:T(8,128)(2,1)S(1)}, bf16[2,24,896]{2,1,0:T(8,128)(2,1)S(1)}, u32[]{:S(2)}, u32[]{:S(2)}) collective-permute-start(bf16[2,24,896]{2,1,0:T(8,128)(2,1)S(1)} %collective-permute-done.27.refs_1_), channel_id=1, source_target_pairs={{0,1},{1,0},{2,3},{3,2},{4,5},{5,4},{6,7},{7,6},{8,9},{9,8},{10,11... | collective-permute-start | bytes 258056 | tf_op jit(solution)/shard_map/ppermute | solution.py:55
  (24 other events, 230.4 us)

commit v5 on v4

--- a/solution.py
+++ b/solution.py
@@ -442,13 +442,12 @@
     total, *pieces = core_sum(g, at, keep, g.swap(give), tall)
     saved_parts = [saved]
     if steps:
-        (mine,) = ordered(total, saved)
+        (mine,) = ordered(give, saved)
         saved_parts.append(g.send(mine, row=lambda r: r ^ steps[0]))
-        total, *pieces = lax.optimization_barrier((total, *pieces))
     arrived = to_chips(pieces)
+    grads = gate_grads(g, at, total, arrived, gate_pre, up_pre)
     if steps:
-        saved_parts[1], *arrived = lax.optimization_barrier((saved_parts[1], *arrived))
-    grads = gate_grads(g, at, total, arrived, gate_pre, up_pre)
+        saved_parts[1], grads = lax.optimization_barrier((saved_parts[1], grads))
     for step in steps[1:] if steps else ():
         (mine,) = ordered(grads, jnp.concatenate(saved_parts))
         saved_parts.append(g.send(mine, row=lambda r: r ^ step))
@@ -491,8 +490,6 @@
     for batch in batches:
         held.append([batch] + to_chips([batch] * (g.chips - 1)))
     for batch, pieces in zip(batches, held):
-        if result is not None:
-            result, *pieces = lax.optimization_barrier((result, *pieces))
         others = [g.swap(batch)]
         others += [g.swap(p) for p in pieces[1:]]
         result = weight_grad(g, at, result, features, first, pieces + others, hidden)

time: 91.6 us -> 90.5 us (0.988)
  waiting for transfers between devices: 32.3 us -> 30.6 us
    ppermute x35, waiting for transfers between devices: 32.3 us -> 30.6 us  [send(): return lax.ppermute(value, AXES, pairs)]
  transfers between devices with their start and end apart: 35 -> 35, of which waited for: 21 -> 17; matrix products, arithmetic and copies ran while one was open for 0% -> 0% of each run, Pallas kernels for 10% -> 11%
where the time goes in v5:
time: 90.5 us; the launch traced here: 90.4 us
  waiting for transfers between devices  30.6 us (34%)
  Pallas kernels  29.8 us (33%)
  starting transfers between devices  29.2 us (32%)
    ppermute x35, waiting for transfers between devices, send(): return lax.ppermute(value, AXES, pairs)  30.6 us
    ppermute x35, starting transfers between devices, send(): return lax.ppermute(value, AXES, pairs)  29.2 us
    pallas_call x9, Pallas kernels, local_call(): pl.pallas_call(kernel, out_shape=out_shape, in_specs=in_specs, out_specs=...  25 us
    pallas_call x2, Pallas kernels, weight_grad(): pl.pallas_call(kernel, out_shape=jax.ShapeDtypeStruct((units, features),...  4.85 us
  transfers between devices with their start and end apart: 35, of which 17 were waited for; matrix products, arithmetic and copies ran while one was open for 0% of the time, Pallas kernels for 11%

profile of v5, /device:TPU:0, one launch (start us, length us, event | category | flops | bytes accessed | tf_op | source)
XLA Modules:
  0.0 90.4 jit_solution(10235206770722438881)
XLA Ops:
  0.1 7.9 %shard_map.100 = (bf16[2,24,3712]{2,1,0:T(8,128)(2,1)S(1)}, bf16[2,24,3712]{2,1,0:T(8,128)(2,1)S(1)}) custom-call(s32[4]{0:T(128)S(1)} %pad_add_fusion.pos, bf16[48,1024]{1,0:T(8,128)(2,1)} %grad_hbm.1, bf16[7392,1024]{1,0:T(8,128)(2,1)} %w_ref.3), custom_call_target="tpu_custom_call" | custom-call | flops 726663168 | bytes 15138816 | tf_op jit(solution)/shard_map/pallas_call | solution.py:72
  10.5 2.9 %collective-permute-start.2 = (bf16[24,1920]{1,0:T(8,128)(2,1)S(1)}, bf16[24,1920]{1,0:T(8,128)(2,1)S(1)}, u32[]{:S(2)}, u32[]{:S(2)}) collective-permute-start(bf16[24,1920]{1,0:T(8,128)(2,1)S(1)} %get-tuple-element.35), channel_id=1, source_target_pairs={{0,1},{1,0},{2,3},{3,2},{4,5},{5,4},{6,7},{7,6},{8,9},{9,8},{10,11... | collective-permute-start | bytes 276488 | tf_op jit(solution)/shard_map/ppermute | solution.py:55
  13.5 1.5 %collective-permute-start.3 = (bf16[24,1920]{1,0:T(8,128)(2,1)S(1)}, bf16[24,1920]{1,0:T(8,128)(2,1)S(1)}, u32[]{:S(2)}, u32[]{:S(2)}) collective-permute-start(bf16[24,1920]{1,0:T(8,128)(2,1)S(1)} %get-tuple-element.36), channel_id=1, source_target_pairs={{0,16},{1,17},{2,18},{3,19},{4,20},{5,21},{6,22},{7,23},{8,24},{9,... | collective-permute-start | bytes 276488 | tf_op jit(solution)/shard_map/ppermute | solution.py:55
  15.0 2.0 %collective-permute-start = (bf16[1,48,800]{2,1,0:T(8,128)(2,1)S(1)}, bf16[1,48,800]{2,1,0:T(8,128)(2,1)S(1)}, u32[]{:S(2)}, u32[]{:S(2)}) collective-permute-start(bf16[1,48,800]{2,1,0:T(8,128)(2,1)S(1)} %bitcast.16), channel_id=1, source_target_pairs={{0,2},{1,3},{2,0},{3,1},{4,6},{5,7},{6,4},{7,5},{8,10},{9,11},{10,... | collective-permute-start | bytes 230408 | tf_op jit(solution)/shard_map/ppermute | solution.py:55
  17.1 1.9 %collective-permute-done.3.refs_1_ = bf16[24,1920]{1,0:T(8,128)(2,1)S(1)} collective-permute-done((bf16[24,1920]{1,0:T(8,128)(2,1)S(1)}, bf16[24,1920]{1,0:T(8,128)(2,1)S(1)}, u32[]{:S(2)}, u32[]{:S(2)}) %collective-permute-start.3) | collective-permute-done | bytes 92192 | tf_op jit(solution)/shard_map/ppermute | solution.py:55
  21.3 1.9 %collective-permute-start.7 = (bf16[24,3712]{1,0:T(8,128)(2,1)S(1)}, bf16[24,3712]{1,0:T(8,128)(2,1)S(1)}, u32[]{:S(2)}, u32[]{:S(2)}) collective-permute-start(bf16[24,3712]{1,0:T(8,128)(2,1)S(1)} %shard_map.102.refs_0_), channel_id=1, source_target_pairs={{0,17},{1,16},{2,19},{3,18},{4,21},{5,20},{6,23},{7,22},{8,25},{9,... | collective-permute-start | bytes 534536 | tf_op jit(solution)/shard_map/ppermute | solution.py:55
  24.8 4.2 %collective-permute-done.7.refs_3_ = bf16[24,3712]{1,0:T(8,128)(2,1)S(1)} collective-permute-done((bf16[24,3712]{1,0:T(8,128)(2,1)S(1)}, bf16[24,3712]{1,0:T(8,128)(2,1)S(1)}, u32[]{:S(2)}, u32[]{:S(2)}) %collective-permute-start.7) | collective-permute-done | bytes 178208 | tf_op jit(solution)/shard_map/ppermute | solution.py:55
  29.1 2.1 %collective-permute-done.6.refs_2_ = bf16[24,3712]{1,0:T(8,128)(2,1)S(1)} collective-permute-done((bf16[24,3712]{1,0:T(8,128)(2,1)S(1)}, bf16[24,3712]{1,0:T(8,128)(2,1)S(1)}, u32[]{:S(2)}, u32[]{:S(2)}) %collective-permute-start.6) | collective-permute-done | bytes 178208 | tf_op jit(solution)/shard_map/ppermute | solution.py:55
  33.0 6.0 %shard_map.103 = bf16[48,1024]{1,0:T(8,128)(2,1)S(1)} custom-call(s32[4]{0:T(128)S(1)} %pad_add_fusion.pos, s32[4]{0:T(128)S(1)} %copy-done.1, bf16[24,3712]{1,0:T(8,128)(2,1)S(1)} %shard_map.102.refs_0_, bf16[24,3712]{1,0:T(8,128)(2,1)S(1)} %collective-permute-done.5.refs_1_, bf16[24,3712]{1,0:T(8,128)(2,1)S(1)} %collective-permute-done.6.refs_2_, ...), custom_call_target="tpu_custom_call" | custom-call | flops 2906652672 | bytes 30277632 | tf_op jit(solution)/shard_map/pallas_call | solution.py:72
  39.0 1.6 %collective-permute-start.12 = (bf16[48,1024]{1,0:T(8,128)(2,1)S(1)}, bf16[48,1024]{1,0:T(8,128)(2,1)S(1)}, u32[]{:S(2)}, u32[]{:S(2)}) collective-permute-start(bf16[48,1024]{1,0:T(8,128)(2,1)S(1)} %shard_map.103), channel_id=1, source_target_pairs={{0,2},{1,3},{2,0},{3,1},{4,6},{5,7},{6,4},{7,5},{8,10},{9,11},{10,... | collective-permute-start | bytes 294920 | tf_op jit(solution)/shard_map/ppermute | solution.py:55
  40.6 2.8 %shard_map.104.refs_0_ = bf16[4,512,1024]{2,1,0:T(8,128)(2,1)S(1)} custom-call(s32[4]{0:T(128)S(1)} %pad_add_fusion.pos, bf16[12800,1024]{1,0:T(8,128)(2,1)} %w_ref.5), custom_call_target="tpu_custom_call" | custom-call | bytes 4194304 | tf_op jit(solution)/shard_map/pallas_call | solution.py:72
  44.0 2.7 %collective-permute-start.13 = (bf16[48,1024]{1,0:T(8,128)(2,1)S(1)}, bf16[48,1024]{1,0:T(8,128)(2,1)S(1)}, u32[]{:S(2)}, u32[]{:S(2)}) collective-permute-start(bf16[48,1024]{1,0:T(8,128)(2,1)S(1)} %add_convert_fusion.1), channel_id=1, source_target_pairs={{0,4},{1,5},{2,6},{3,7},{4,0},{5,1},{6,2},{7,3},{8,12},{9,13},{10,... | collective-permute-start | bytes 294920 | tf_op jit(solution)/shard_map/ppermute | solution.py:55
  46.7 2.4 %shard_map.105.refs_1_ = bf16[3,512,1024]{2,1,0:T(8,128)(2,1)S(1)} custom-call(s32[4]{0:T(128)S(1)} %pad_add_fusion.pos, bf16[12800,1024]{1,0:T(8,128)(2,1)} %w_ref.5), custom_call_target="tpu_custom_call" | custom-call | bytes 3145728 | tf_op jit(solution)/shard_map/pallas_call | solution.py:72
  49.1 2.1 %collective-permute-done.13 = bf16[48,1024]{1,0:T(8,128)(2,1)S(1)} collective-permute-done((bf16[48,1024]{1,0:T(8,128)(2,1)S(1)}, bf16[48,1024]{1,0:T(8,128)(2,1)S(1)}, u32[]{:S(2)}, u32[]{:S(2)}) %collective-permute-start.13) | collective-permute-done | bytes 98336 | tf_op jit(solution)/shard_map/ppermute | solution.py:55
  51.3 2.5 %shard_map.106 = (bf16[4,24,896]{2,1,0:T(8,128)(2,1)S(1)}, bf16[4,24,896]{2,1,0:T(8,128)(2,1)S(1)}) custom-call(bf16[48,1024]{1,0:T(8,128)(2,1)S(1)} %add_convert_fusion.grad_ref, bf16[4,512,1024]{2,1,0:T(8,128)(2,1)S(1)} %shard_map.104.refs_0_, bf16[3,512,1024]{2,1,0:T(8,128)(2,1)S(1)} %shard_map.105.refs_1_), custom_call_target="tpu_custom_call" | custom-call | flops 352321536 | bytes 7340032 | tf_op jit(solution)/shard_map/pallas_call | solution.py:72
  58.0 1.5 %collective-permute-start.17 = (bf16[24,896]{1,0:T(8,128)(2,1)S(1)}, bf16[24,896]{1,0:T(8,128)(2,1)S(1)}, u32[]{:S(2)}, u32[]{:S(2)}) collective-permute-start(bf16[24,896]{1,0:T(8,128)(2,1)S(1)} %get-tuple-element.50), channel_id=1, source_target_pairs={{0,17},{1,16},{2,19},{3,18},{4,21},{5,20},{6,23},{7,22},{8,25},{9,... | collective-permute-start | bytes 129032 | tf_op jit(solution)/shard_map/ppermute | solution.py:55
  61.3 1.5 %collective-permute-done.17 = bf16[24,896]{1,0:T(8,128)(2,1)S(1)} collective-permute-done((bf16[24,896]{1,0:T(8,128)(2,1)S(1)}, bf16[24,896]{1,0:T(8,128)(2,1)S(1)}, u32[]{:S(2)}, u32[]{:S(2)}) %collective-permute-start.17) | collective-permute-done | bytes 43040 | tf_op jit(solution)/shard_map/ppermute | solution.py:55
  63.7 6.0 %collective-permute-done.19.refs_2_ = bf16[2,48,800]{2,1,0:T(8,128)(2,1)S(1)} collective-permute-done((bf16[2,48,800]{2,1,0:T(8,128)(2,1)S(1)}, bf16[2,48,800]{2,1,0:T(8,128)(2,1)S(1)}, u32[]{:S(2)}, u32[]{:S(2)}) %collective-permute-start.19) | collective-permute-done | bytes 153632 | tf_op jit(solution)/shard_map/ppermute | solution.py:55
  71.2 1.5 %collective-permute-start.22 = (bf16[2,24,896]{2,1,0:T(8,128)(2,1)S(1)}, bf16[2,24,896]{2,1,0:T(8,128)(2,1)S(1)}, u32[]{:S(2)}, u32[]{:S(2)}) collective-permute-start(bf16[2,24,896]{2,1,0:T(8,128)(2,1)S(1)} %pad_maximum_fusion.1.refs_0_), channel_id=1, source_target_pairs={{0,17},{1,16},{2,19},{3,18},{4,21},{5,20},{6,23},{7,22},{8,25},{9,... | collective-permute-start | bytes 258056 | tf_op jit(solution)/shard_map/ppermute | solution.py:55
  74.8 2.7 %collective-permute-done.27.refs_1_ = bf16[2,24,896]{2,1,0:T(8,128)(2,1)S(1)} collective-permute-done((bf16[2,24,896]{2,1,0:T(8,128)(2,1)S(1)}, bf16[2,24,896]{2,1,0:T(8,128)(2,1)S(1)}, u32[]{:S(2)}, u32[]{:S(2)}) %collective-permute-start.27) | collective-permute-done | bytes 86048 | tf_op jit(solution)/shard_map/ppermute | solution.py:55
  77.5 1.5 %collective-permute-start.30 = (bf16[2,24,896]{2,1,0:T(8,128)(2,1)S(1)}, bf16[2,24,896]{2,1,0:T(8,128)(2,1)S(1)}, u32[]{:S(2)}, u32[]{:S(2)}) collective-permute-start(bf16[2,24,896]{2,1,0:T(8,128)(2,1)S(1)} %collective-permute-done.27.refs_1_), channel_id=1, source_target_pairs={{0,17},{1,16},{2,19},{3,18},{4,21},{5,20},{6,23},{7,22},{8,25},{9,... | collective-permute-start | bytes 258056 | tf_op jit(solution)/shard_map/ppermute | solution.py:55
  81.5 2.3 %collective-permute-done.30.refs_4_ = bf16[2,24,896]{2,1,0:T(8,128)(2,1)S(1)} collective-permute-done((bf16[2,24,896]{2,1,0:T(8,128)(2,1)S(1)}, bf16[2,24,896]{2,1,0:T(8,128)(2,1)S(1)}, u32[]{:S(2)}, u32[]{:S(2)}) %collective-permute-start.30) | collective-permute-done | bytes 86048 | tf_op jit(solution)/shard_map/ppermute | solution.py:55
  85.3 2.5 %weight_grad.2.refs_0_ = bf16[800,3200]{1,0:T(8,128)(2,1)} custom-call(s32[4]{0:T(128)S(1)} %pad_add_fusion.pos, bf16[2,24,896]{2,1,0:T(8,128)(2,1)S(1)} %pad_maximum_fusion.1.refs_0_, bf16[2,24,896]{2,1,0:T(8,128)(2,1)S(1)} %collective-permute-done.20.refs_1_, bf16[2,24,896]{2,1,0:T(8,128)(2,1)S(1)} %collective-permute-done.21.refs_2_, ...), custom_call_target="tpu_custom_call" | custom-call | flops 550502400 | bytes 2867200 | tf_op jit(solution)/shard_map/weight_grad/pallas_call | solution.py:370
  87.9 2.3 %weight_grad.3 = bf16[800,3200]{1,0:T(8,128)(2,1)} custom-call(s32[4]{0:T(128)S(1)} %pad_add_fusion.pos, bf16[800,3200]{1,0:T(8,128)(2,1)} %weight_grad.2.refs_0_, bf16[2,24,896]{2,1,0:T(8,128)(2,1)S(1)} %collective-permute-done.27.refs_1_, bf16[2,24,896]{2,1,0:T(8,128)(2,1)S(1)} %collective-permute-done.28.refs_2_, ...), custom_call_target="tpu_custom_call", output_to_operand_aliasing={{}: (1, {})} | custom-call | flops 550502400 | bytes 2867200 | tf_op jit(solution)/shard_map/weight_grad/pallas_call | solution.py:370
  (91 shorter events, 23.4 us)
Async XLA Ops:
  10.5 6.5 %collective-permute-start.2 = (bf16[24,1920]{1,0:T(8,128)(2,1)S(1)}, bf16[24,1920]{1,0:T(8,128)(2,1)S(1)}, u32[]{:S(2)}, u32[]{:S(2)}) collective-permute-start(bf16[24,1920]{1,0:T(8,128)(2,1)S(1)} %get-tuple-element.35), channel_id=1, source_target_pairs={{0,1},{1,0},{2,3},{3,2},{4,5},{5,4},{6,7},{7,6},{8,9},{9,8},{10,11... | collective-permute-start | bytes 276488 | tf_op jit(solution)/shard_map/ppermute | solution.py:55
  13.5 5.5 %collective-permute-start.3 = (bf16[24,1920]{1,0:T(8,128)(2,1)S(1)}, bf16[24,1920]{1,0:T(8,128)(2,1)S(1)}, u32[]{:S(2)}, u32[]{:S(2)}) collective-permute-start(bf16[24,1920]{1,0:T(8,128)(2,1)S(1)} %get-tuple-element.36), channel_id=1, source_target_pairs={{0,16},{1,17},{2,18},{3,19},{4,20},{5,21},{6,22},{7,23},{8,24},{9,... | collective-permute-start | bytes 276488 | tf_op jit(solution)/shard_map/ppermute | solution.py:55
  15.0 5.5 %collective-permute-start.4 = (bf16[24,1920]{1,0:T(8,128)(2,1)S(1)}, bf16[24,1920]{1,0:T(8,128)(2,1)S(1)}, u32[]{:S(2)}, u32[]{:S(2)}) collective-permute-start(bf16[24,1920]{1,0:T(8,128)(2,1)S(1)} %get-tuple-element.37), channel_id=1, source_target_pairs={{0,17},{1,16},{2,19},{3,18},{4,21},{5,20},{6,23},{7,22},{8,25},{9,... | collective-permute-start | bytes 276488 | tf_op jit(solution)/shard_map/ppermute | solution.py:55
  15.0 6.2 %collective-permute-start = (bf16[1,48,800]{2,1,0:T(8,128)(2,1)S(1)}, bf16[1,48,800]{2,1,0:T(8,128)(2,1)S(1)}, u32[]{:S(2)}, u32[]{:S(2)}) collective-permute-start(bf16[1,48,800]{2,1,0:T(8,128)(2,1)S(1)} %bitcast.16), channel_id=1, source_target_pairs={{0,2},{1,3},{2,0},{3,1},{4,6},{5,7},{6,4},{7,5},{8,10},{9,11},{10,... | collective-permute-start | bytes 230408 | tf_op jit(solution)/shard_map/ppermute | solution.py:55
  21.3 7.8 %collective-permute-start.7 = (bf16[24,3712]{1,0:T(8,128)(2,1)S(1)}, bf16[24,3712]{1,0:T(8,128)(2,1)S(1)}, u32[]{:S(2)}, u32[]{:S(2)}) collective-permute-start(bf16[24,3712]{1,0:T(8,128)(2,1)S(1)} %shard_map.102.refs_0_), channel_id=1, source_target_pairs={{0,17},{1,16},{2,19},{3,18},{4,21},{5,20},{6,23},{7,22},{8,25},{9,... | collective-permute-start | bytes 534536 | tf_op jit(solution)/shard_map/ppermute | solution.py:55
  23.2 8.0 %collective-permute-start.6 = (bf16[24,3712]{1,0:T(8,128)(2,1)S(1)}, bf16[24,3712]{1,0:T(8,128)(2,1)S(1)}, u32[]{:S(2)}, u32[]{:S(2)}) collective-permute-start(bf16[24,3712]{1,0:T(8,128)(2,1)S(1)} %shard_map.102.refs_0_), channel_id=1, source_target_pairs={{0,16},{1,17},{2,18},{3,19},{4,20},{5,21},{6,22},{7,23},{8,24},{9,... | collective-permute-start | bytes 534536 | tf_op jit(solution)/shard_map/ppermute | solution.py:55
  23.8 7.4 %collective-permute-start.5 = (bf16[24,3712]{1,0:T(8,128)(2,1)S(1)}, bf16[24,3712]{1,0:T(8,128)(2,1)S(1)}, u32[]{:S(2)}, u32[]{:S(2)}) collective-permute-start(bf16[24,3712]{1,0:T(8,128)(2,1)S(1)} %shard_map.102.refs_0_), channel_id=1, source_target_pairs={{0,1},{1,0},{2,3},{3,2},{4,5},{5,4},{6,7},{7,6},{8,9},{9,8},{10,11... | collective-permute-start | bytes 534536 | tf_op jit(solution)/shard_map/ppermute | solution.py:55
  24.8 6.9 %collective-permute-start.8 = (bf16[24,3712]{1,0:T(8,128)(2,1)S(1)}, bf16[24,3712]{1,0:T(8,128)(2,1)S(1)}, u32[]{:S(2)}, u32[]{:S(2)}) collective-permute-start(bf16[24,3712]{1,0:T(8,128)(2,1)S(1)} %shard_map.102.refs_0_), channel_id=1, source_target_pairs={{0,8},{1,9},{2,10},{3,11},{4,12},{5,13},{6,14},{7,15},{8,0},{9,1},... | collective-permute-start | bytes 534536 | tf_op jit(solution)/shard_map/ppermute | solution.py:55
  39.0 5.0 %collective-permute-start.12 = (bf16[48,1024]{1,0:T(8,128)(2,1)S(1)}, bf16[48,1024]{1,0:T(8,128)(2,1)S(1)}, u32[]{:S(2)}, u32[]{:S(2)}) collective-permute-start(bf16[48,1024]{1,0:T(8,128)(2,1)S(1)} %shard_map.103), channel_id=1, source_target_pairs={{0,2},{1,3},{2,0},{3,1},{4,6},{5,7},{6,4},{7,5},{8,10},{9,11},{10,... | collective-permute-start | bytes 294920 | tf_op jit(solution)/shard_map/ppermute | solution.py:55
  44.0 7.2 %collective-permute-start.13 = (bf16[48,1024]{1,0:T(8,128)(2,1)S(1)}, bf16[48,1024]{1,0:T(8,128)(2,1)S(1)}, u32[]{:S(2)}, u32[]{:S(2)}) collective-permute-start(bf16[48,1024]{1,0:T(8,128)(2,1)S(1)} %add_convert_fusion.1), channel_id=1, source_target_pairs={{0,4},{1,5},{2,6},{3,7},{4,0},{5,1},{6,2},{7,3},{8,12},{9,13},{10,... | collective-permute-start | bytes 294920 | tf_op jit(solution)/shard_map/ppermute | solution.py:55
  55.9 4.7 %collective-permute-start.15 = (bf16[24,896]{1,0:T(8,128)(2,1)S(1)}, bf16[24,896]{1,0:T(8,128)(2,1)S(1)}, u32[]{:S(2)}, u32[]{:S(2)}) collective-permute-start(bf16[24,896]{1,0:T(8,128)(2,1)S(1)} %get-tuple-element.48), channel_id=1, source_target_pairs={{0,1},{1,0},{2,3},{3,2},{4,5},{5,4},{6,7},{7,6},{8,9},{9,8},{10,11... | collective-permute-start | bytes 129032 | tf_op jit(solution)/shard_map/ppermute | solution.py:55
  57.0 4.4 %collective-permute-start.16 = (bf16[24,896]{1,0:T(8,128)(2,1)S(1)}, bf16[24,896]{1,0:T(8,128)(2,1)S(1)}, u32[]{:S(2)}, u32[]{:S(2)}) collective-permute-start(bf16[24,896]{1,0:T(8,128)(2,1)S(1)} %get-tuple-element.49), channel_id=1, source_target_pairs={{0,16},{1,17},{2,18},{3,19},{4,20},{5,21},{6,22},{7,23},{8,24},{9,... | collective-permute-start | bytes 129032 | tf_op jit(solution)/shard_map/ppermute | solution.py:55
  58.0 4.9 %collective-permute-start.17 = (bf16[24,896]{1,0:T(8,128)(2,1)S(1)}, bf16[24,896]{1,0:T(8,128)(2,1)S(1)}, u32[]{:S(2)}, u32[]{:S(2)}) collective-permute-start(bf16[24,896]{1,0:T(8,128)(2,1)S(1)} %get-tuple-element.50), channel_id=1, source_target_pairs={{0,17},{1,16},{2,19},{3,18},{4,21},{5,20},{6,23},{7,22},{8,25},{9,... | collective-permute-start | bytes 129032 | tf_op jit(solution)/shard_map/ppermute | solution.py:55
  59.5 10.2 %collective-permute-start.19 = (bf16[2,48,800]{2,1,0:T(8,128)(2,1)S(1)}, bf16[2,48,800]{2,1,0:T(8,128)(2,1)S(1)}, u32[]{:S(2)}, u32[]{:S(2)}) collective-permute-start(bf16[2,48,800]{2,1,0:T(8,128)(2,1)S(1)} %pad_maximum_fusion), channel_id=1, source_target_pairs={{0,4},{1,5},{2,6},{3,7},{4,0},{5,1},{6,2},{7,3},{8,12},{9,13},{10,... | collective-permute-start | bytes 460808 | tf_op jit(solution)/shard_map/ppermute | solution.py:55
  62.9 8.1 %collective-permute-start.18 = (bf16[1,24,896]{2,1,0:T(8,128)(2,1)S(1)}, bf16[1,24,896]{2,1,0:T(8,128)(2,1)S(1)}, u32[]{:S(2)}, u32[]{:S(2)}) collective-permute-start(bf16[1,24,896]{2,1,0:T(8,128)(2,1)S(1)} %bitcast.20), channel_id=1, source_target_pairs={{0,2},{1,3},{2,0},{3,1},{4,6},{5,7},{6,4},{7,5},{8,10},{9,11},{10,... | collective-permute-start | bytes 129032 | tf_op jit(solution)/shard_map/ppermute | solution.py:55
  71.1 6.4 %collective-permute-start.27 = (bf16[2,24,896]{2,1,0:T(8,128)(2,1)S(1)}, bf16[2,24,896]{2,1,0:T(8,128)(2,1)S(1)}, u32[]{:S(2)}, u32[]{:S(2)}) collective-permute-start(bf16[2,24,896]{2,1,0:T(8,128)(2,1)S(1)} %pad_maximum_fusion.1.refs_0_), channel_id=1, source_target_pairs={{0,4},{1,5},{2,6},{3,7},{4,0},{5,1},{6,2},{7,3},{8,12},{9,13},{10,... | collective-permute-start | bytes 258056 | tf_op jit(solution)/shard_map/ppermute | solution.py:55
  71.2 7.8 %collective-permute-start.23 = (bf16[2,24,896]{2,1,0:T(8,128)(2,1)S(1)}, bf16[2,24,896]{2,1,0:T(8,128)(2,1)S(1)}, u32[]{:S(2)}, u32[]{:S(2)}) collective-permute-start(bf16[2,24,896]{2,1,0:T(8,128)(2,1)S(1)} %pad_maximum_fusion.1.refs_0_), channel_id=1, source_target_pairs={{0,8},{1,9},{2,10},{3,11},{4,12},{5,13},{6,14},{7,15},{8,0},{9,1},... | collective-permute-start | bytes 258056 | tf_op jit(solution)/shard_map/ppermute | solution.py:55
  71.2 8.8 %collective-permute-start.22 = (bf16[2,24,896]{2,1,0:T(8,128)(2,1)S(1)}, bf16[2,24,896]{2,1,0:T(8,128)(2,1)S(1)}, u32[]{:S(2)}, u32[]{:S(2)}) collective-permute-start(bf16[2,24,896]{2,1,0:T(8,128)(2,1)S(1)} %pad_maximum_fusion.1.refs_0_), channel_id=1, source_target_pairs={{0,17},{1,16},{2,19},{3,18},{4,21},{5,20},{6,23},{7,22},{8,25},{9,... | collective-permute-start | bytes 258056 | tf_op jit(solution)/shard_map/ppermute | solution.py:55
  72.8 8.2 %collective-permute-start.21 = (bf16[2,24,896]{2,1,0:T(8,128)(2,1)S(1)}, bf16[2,24,896]{2,1,0:T(8,128)(2,1)S(1)}, u32[]{:S(2)}, u32[]{:S(2)}) collective-permute-start(bf16[2,24,896]{2,1,0:T(8,128)(2,1)S(1)} %pad_maximum_fusion.1.refs_0_), channel_id=1, source_target_pairs={{0,16},{1,17},{2,18},{3,19},{4,20},{5,21},{6,22},{7,23},{8,24},{9,... | collective-permute-start | bytes 258056 | tf_op jit(solution)/shard_map/ppermute | solution.py:55
  73.8 7.2 %collective-permute-start.20 = (bf16[2,24,896]{2,1,0:T(8,128)(2,1)S(1)}, bf16[2,24,896]{2,1,0:T(8,128)(2,1)S(1)}, u32[]{:S(2)}, u32[]{:S(2)}) collective-permute-start(bf16[2,24,896]{2,1,0:T(8,128)(2,1)S(1)} %pad_maximum_fusion.1.refs_0_), channel_id=1, source_target_pairs={{0,1},{1,0},{2,3},{3,2},{4,5},{5,4},{6,7},{7,6},{8,9},{9,8},{10,11... | collective-permute-start | bytes 258056 | tf_op jit(solution)/shard_map/ppermute | solution.py:55
  77.5 6.3 %collective-permute-start.30 = (bf16[2,24,896]{2,1,0:T(8,128)(2,1)S(1)}, bf16[2,24,896]{2,1,0:T(8,128)(2,1)S(1)}, u32[]{:S(2)}, u32[]{:S(2)}) collective-permute-start(bf16[2,24,896]{2,1,0:T(8,128)(2,1)S(1)} %collective-permute-done.27.refs_1_), channel_id=1, source_target_pairs={{0,17},{1,16},{2,19},{3,18},{4,21},{5,20},{6,23},{7,22},{8,25},{9,... | collective-permute-start | bytes 258056 | tf_op jit(solution)/shard_map/ppermute | solution.py:55
  78.9 5.3 %collective-permute-start.29 = (bf16[2,24,896]{2,1,0:T(8,128)(2,1)S(1)}, bf16[2,24,896]{2,1,0:T(8,128)(2,1)S(1)}, u32[]{:S(2)}, u32[]{:S(2)}) collective-permute-start(bf16[2,24,896]{2,1,0:T(8,128)(2,1)S(1)} %collective-permute-done.27.refs_1_), channel_id=1, source_target_pairs={{0,16},{1,17},{2,18},{3,19},{4,20},{5,21},{6,22},{7,23},{8,24},{9,... | collective-permute-start | bytes 258056 | tf_op jit(solution)/shard_map/ppermute | solution.py:55
  80.0 4.7 %collective-permute-start.28 = (bf16[2,24,896]{2,1,0:T(8,128)(2,1)S(1)}, bf16[2,24,896]{2,1,0:T(8,128)(2,1)S(1)}, u32[]{:S(2)}, u32[]{:S(2)}) collective-permute-start(bf16[2,24,896]{2,1,0:T(8,128)(2,1)S(1)} %collective-permute-done.27.refs_1_), channel_id=1, source_target_pairs={{0,1},{1,0},{2,3},{3,2},{4,5},{5,4},{6,7},{7,6},{8,9},{9,8},{10,11... | collective-permute-start | bytes 258056 | tf_op jit(solution)/shard_map/ppermute | solution.py:55
  81.0 4.3 %collective-permute-start.25 = (bf16[2,24,896]{2,1,0:T(8,128)(2,1)S(1)}, bf16[2,24,896]{2,1,0:T(8,128)(2,1)S(1)}, u32[]{:S(2)}, u32[]{:S(2)}) collective-permute-start(bf16[2,24,896]{2,1,0:T(8,128)(2,1)S(1)} %collective-permute-done.21.refs_2_), channel_id=1, source_target_pairs={{0,8},{1,9},{2,10},{3,11},{4,12},{5,13},{6,14},{7,15},{8,0},{9,1},... | collective-permute-start | bytes 258056 | tf_op jit(solution)/shard_map/ppermute | solution.py:55
  (24 other events, 231.5 us)
